TPU v7x, 256 devices: a whole 4x4x8 slice. The times are simulated.
256 devices in a mesh: src: 8 (over z_lo, core), tgt: 32 (over y, x, z_hi).
Axes of the slice: x: 4, y: 4, z: 8 (z_hi: 2, z_lo: 4; z = z_hi * 4 + z_lo), core: 2. Of those that a mesh axis runs over, the one named last changes fastest.
Arguments:
- src_feat: bfloat16 [16, 128, 1024], P('src', None, 'tgt'), may hold values from -6 to 6
- tgt_feat: bfloat16 [128, 96, 1024], P('tgt'), may hold values from -6 to 6
- w_src: bfloat16 [8, 3, 3], replicated, may hold values from -2 to 2
- b_src: float32 [8], replicated, may hold values from -3 to 3
- w_tgt: bfloat16 [8, 8, 3, 3], replicated, may hold values from -0.75 to 0.75
- b_tgt: float32 [8], replicated, may hold values from -3 to 3
- w_out: float32 [8], replicated, may hold values from -2 to 2
- cotangent: bfloat16 [128, 96, 16, 128], P('tgt', None, 'src'), may hold values from -6 to 6
Outputs:
- score: bfloat16 [128, 96, 16, 128], P('tgt', None, 'src')
- grad_src: float32 [1024, 16, 128], P('tgt', 'src')
- grad_tgt: float32 [128, 96, 1024], P('tgt', None, 'src')
All inputs are finite; a program needn't handle non-finite values.
Results may differ from a plain program's by a relative error of at most 0.0064.
Values may be sent and summed in bfloat16 or wider, within the bound.
No kernel may reach another device: no remote copies, remote signals or barrier semaphores. Data moves between devices by JAX's collectives and lax.ppermute only.
A program may use at most 128 MiB of HBM per device.

v0:
```python
import jax
import jax.numpy as jnp
from jax import lax
from jax.sharding import PartitionSpec as P


def extended(cells, sides, width):
    for axis, dim in sides:
        count = lax.axis_size(axis)
        ends = count - 1
        head = lax.slice_in_dim(cells, 0, width, axis=dim)
        tail = lax.slice_in_dim(cells, cells.shape[dim] - width, cells.shape[dim], axis=dim)
        cells = jnp.concatenate(
            [
                lax.ppermute(tail, axis, [(i, (i + 1) % count) for i in range(ends)]),
                cells,
                lax.ppermute(head, axis, [((i + 1) % count, i) for i in range(ends)]),
            ],
            axis=dim,
        )
    return cells


def source_filter(corr_ext, w_src, b_src):
    padded = jnp.pad(corr_ext, ((0, 0), (0, 0), (0, 0), (1, 1)))
    rows_i = corr_ext.shape[2] - 2
    cols_j = corr_ext.shape[3]
    total = (
        jnp.zeros(
            (w_src.shape[0], corr_ext.shape[0], corr_ext.shape[1], rows_i, cols_j), jnp.float32
        )
        + b_src[:, None, None, None, None]
    )
    for a in range(3):
        for b in range(3):
            weight = w_src[:, a, b].astype(jnp.float32)[:, None, None, None, None]
            total = total + weight * padded[None, :, :, a : a + rows_i, b : b + cols_j].astype(
                jnp.float32
            )
    return total


def target_filter(hidden_ext, w_tgt, b_tgt):
    padded = jnp.pad(hidden_ext, ((0, 0), (0, 0), (1, 1), (0, 0), (0, 0)))
    rows_k = hidden_ext.shape[1] - 2
    cols_l = hidden_ext.shape[2]
    total = (
        jnp.zeros((w_tgt.shape[0], rows_k) + hidden_ext.shape[2:], jnp.float32)
        + b_tgt[:, None, None, None, None]
    )
    for a in range(3):
        for b in range(3):
            total = total + jnp.einsum(
                "op,pklij->oklij",
                w_tgt[:, :, a, b],
                padded[:, a : a + rows_k, b : b + cols_l],
                preferred_element_type=jnp.float32,
            )
    return total


def target_adjoint(grads_ext, w_tgt):
    padded = jnp.pad(grads_ext, ((0, 0), (0, 0), (1, 1), (0, 0), (0, 0)))
    rows_k = grads_ext.shape[1] - 2
    cols_l = grads_ext.shape[2]
    total = jnp.zeros((w_tgt.shape[1], rows_k) + grads_ext.shape[2:], jnp.float32)
    for a in range(3):
        for b in range(3):
            total = total + jnp.einsum(
                "op,oklij->pklij",
                w_tgt[:, :, a, b],
                padded[:, 2 - a : 2 - a + rows_k, 2 - b : 2 - b + cols_l],
                preferred_element_type=jnp.float32,
            )
    return total


def source_adjoint(grads_ext, w_src):
    padded = jnp.pad(grads_ext, ((0, 0), (0, 0), (0, 0), (0, 0), (1, 1)))
    rows_i = grads_ext.shape[3] - 2
    cols_j = grads_ext.shape[4]
    total = jnp.zeros(grads_ext.shape[1:3] + (rows_i, cols_j), jnp.float32)
    for a in range(3):
        for b in range(3):
            weight = w_src[:, a, b].astype(jnp.float32)[:, None, None, None, None]
            total = total + jnp.sum(
                weight
                * padded[:, :, :, 2 - a : 2 - a + rows_i, 2 - b : 2 - b + cols_j].astype(
                    jnp.float32
                ),
                axis=0,
            )
    return total


def pre_grads(cot_f32, gains, pre):
    sig = jax.nn.sigmoid(pre)
    return (cot_f32[None] * gains * (sig * (1.0 + pre * (1.0 - sig)))).astype(jnp.bfloat16)


def body(src_feat, tgt_feat, w_src, b_src, w_tgt, b_tgt, w_out, cotangent):
    tgt_rows, tgt_cols, src_rows, src_cols = cotangent.shape
    chans = tgt_feat.shape[2]
    scale = chans ** (-0.5)
    tgt_flat = tgt_feat.reshape(tgt_rows * tgt_cols, chans)
    dims = (((1,), (1,)), ((), ()))
    src_full = lax.all_gather(src_feat, "tgt", axis=2, tiled=True)
    src_flat = src_full.reshape(src_rows * src_cols, chans)
    raw = lax.dot_general(tgt_flat, src_flat, dims, preferred_element_type=jnp.float32)
    corr = (raw * scale).astype(jnp.bfloat16).reshape(tgt_rows, tgt_cols, src_rows, src_cols)
    gains = w_out[:, None, None, None, None]
    corr_ext = extended(corr, (("src", 2),), 1)
    hidden = source_filter(corr_ext, w_src, b_src).astype(jnp.bfloat16)
    hidden_ext = extended(hidden, (("tgt", 1),), 1)
    pre = target_filter(hidden_ext, w_tgt, b_tgt)
    g_pre = pre_grads(cotangent.astype(jnp.float32), gains, pre)
    g_pre_ext = extended(g_pre, (("tgt", 1),), 1)
    score = jnp.sum(gains * jax.nn.silu(pre), axis=0).astype(jnp.bfloat16)
    g_hidden = target_adjoint(g_pre_ext, w_tgt).astype(jnp.bfloat16)
    g_hidden_ext = extended(g_hidden, (("src", 3),), 1)
    g_corr = source_adjoint(g_hidden_ext, w_src)
    g_flat = g_corr.astype(jnp.bfloat16).reshape(tgt_rows * tgt_cols, src_rows * src_cols)
    grad_src = lax.psum_scatter(
        lax.dot_general(
            tgt_flat, g_flat, (((0,), (0,)), ((), ())), preferred_element_type=jnp.float32
        )
        * scale,
        "tgt",
        scatter_dimension=0,
        tiled=True,
    )
    grad_src = grad_src.reshape(grad_src.shape[0], src_rows, src_cols)
    term = (jnp.dot(g_flat, src_flat, preferred_element_type=jnp.float32) * scale).reshape(
        tgt_rows, tgt_cols, chans
    )
    grad_tgt = lax.psum_scatter(term, "src", scatter_dimension=2, tiled=True)
    return (score, grad_src, grad_tgt)


def solution(mesh):
    placed = (
        P("src", None, "tgt"),
        P("tgt", None, None),
        P(),
        P(),
        P(),
        P(),
        P(),
        P("tgt", None, "src", None),
    )
    return jax.shard_map(
        body,
        mesh=mesh,
        in_specs=placed,
        out_specs=(P("tgt", None, "src", None), P("tgt", "src", None), P("tgt", None, "src")),
        check_vma=False,
    )
```

profile of v0, /device:TPU:32, one launch (start us, length us, event | category | flops | bytes accessed | tf_op | source)
XLA Modules:
  0.0 546.6 jit_solution(14578360614142474657)
XLA Ops:
  8.0 124.5 %all_gather.3 = bf16[2,128,1024]{1,0,2:T(2,128)(2,1)S(1)} all-gather(bf16[2,128,32]{1,0,2:T(2,128)(2,1)S(1)} %copy.32), channel_id=1, replica_groups=mesh['src'=8,'tgt'=32] {'tgt'}, dimensions={2}, use_global_device_ids=true | all-gather | bytes 540672 | tf_op jit(solution)/shard_map/all_gather | solution.py:107
  135.7 3.6 collective-permute-start.1
  146.7 2.3 add_convert_fusion.1
  152.1 2.3 fusion.61
  154.4 9.0 %collective-permute-done.2 = bf16[8,1,96,2,128]{4,0,3,2,1:T(8,128)(2,1)S(1)} collective-permute-done((bf16[8,1,96,2,128]{4,0,3,2,1:T(8,128)(2,1)S(1)}, bf16[8,1,96,2,128]{4,0,3,2,1:T(8,128)(2,1)S(1)}, u32[]{:S(2)}, u32[]{:S(2)}) %collective-permute-start.2) | collective-permute-done | bytes 393248 | tf_op jit(solution)/shard_map/ppermute | solution.py:15
  163.3 20.1 %collective-permute-done.3 = bf16[8,1,96,2,128]{4,0,3,2,1:T(8,128)(2,1)S(1)} collective-permute-done((bf16[8,1,96,2,128]{4,0,3,2,1:T(8,128)(2,1)S(1)}, bf16[8,1,96,2,128]{4,0,3,2,1:T(8,128)(2,1)S(1)}, u32[]{:S(2)}, u32[]{:S(2)}) %collective-permute-start.3) | collective-permute-done | bytes 393248 | tf_op jit(solution)/shard_map/ppermute | solution.py:17
  185.6 2.3 fusion.53
  187.9 2.2 fusion.19
  190.1 2.2 fusion.15
  192.3 7.5 %fusion.14 = (bf16[8,4,96,2,128]{4,0,3,2,1:T(8,128)(2,1)S(1)}, bf16[4,96,2,128]{3,2,1,0:T(2,128)(2,1)}) fusion(f32[4,96,2,128]{3,2,1,0:T(2,128)S(1)} %convert_element_type.234, f32[8]{0:T(128)S(1)} %copy-done.5, bf16[8,8,3,3]{1,0,3,2:T(8,128)(2,1)S(1)} %copy-done.2, bf16[8,1,96,2,128]{4,0,3,2,1:T(8,128)(2,1)S(1)} %collective-permute-done.3, ...), kind=kOutput, calls=%fused_computation.19 | convolution fusion | flops 36732928 | bytes 29690880 | tf_op jit(solution)/shard_map/op,pklij->oklij/dot_general | solution.py:53
  201.3 8.7 %collective-permute-start.4 = (bf16[8,1,96,2,128]{4,0,3,2,1:T(8,128)(2,1)S(1)}, bf16[8,1,96,2,128]{4,0,3,2,1:T(8,128)(2,1)S(1)}, u32[]{:S(2)}, u32[]{:S(2)}) collective-permute-start(bf16[8,1,96,2,128]{4,0,3,2,1:T(8,128)(2,1)S(1)} %get-tuple-element.26), channel_id=1, source_target_pairs={{0,1},{1,2},{2,3},{3,4},{4,5},{5,6},{6,7},{7,8},{8,9},{9,10},{10,1... | collective-permute-start | bytes 1179656 | tf_op jit(solution)/shard_map/ppermute | solution.py:15
  210.0 2.3 fusion.59
  212.3 9.4 %collective-permute-done.5 = bf16[8,1,96,2,128]{4,0,3,2,1:T(8,128)(2,1)S(1)} collective-permute-done((bf16[8,1,96,2,128]{4,0,3,2,1:T(8,128)(2,1)S(1)}, bf16[8,1,96,2,128]{4,0,3,2,1:T(8,128)(2,1)S(1)}, u32[]{:S(2)}, u32[]{:S(2)}) %collective-permute-start.5) | collective-permute-done | bytes 393248 | tf_op jit(solution)/shard_map/ppermute | solution.py:17
  224.2 2.3 fusion.51
  226.6 2.3 fusion.27
  228.8 2.2 fusion.23
  231.1 6.3 %fusion.31 = bf16[8,4,96,2,128]{4,0,3,2,1:T(8,128)(2,1)S(1)} fusion(f32[4,96,2,128,8]{3,4,2,1,0:T(8,128)} %fusion.27, f32[4,96,2,128,8]{3,4,2,1,0:T(8,128)} %fusion.51, f32[4,96,2,128,8]{3,4,2,1,0:T(8,128)S(1)} %fusion.55, f32[4,96,2,128,8]{3,4,2,1,0:T(8,128)} %fusion.59, f32[4,96,2,128,8]{3,4,2,1,0:T(8,128)S(1)} %fusion.63, ...), kind=kOutput, calls=%fused_computation.52 | convolution fusion | flops 26607616 | bytes 29100032 | tf_op jit(solution)/shard_map/op,oklij->pklij/dot_general | solution.py:69
  239.6 3.9 collective-permute-start.7
  243.5 7.5 %collective-permute-done.6 = bf16[8,4,96,1,128]{4,0,3,2,1:T(8,128)(2,1)S(1)} collective-permute-done((bf16[8,4,96,1,128]{4,0,3,2,1:T(8,128)(2,1)S(1)}, bf16[8,4,96,1,128]{4,0,3,2,1:T(8,128)(2,1)S(1)}, u32[]{:S(2)}, u32[]{:S(2)}) %collective-permute-start.6) | collective-permute-done | bytes 786464 | tf_op jit(solution)/shard_map/ppermute | solution.py:15
  252.7 4.0 fusion.5
  256.8 8.9 %multiply_reduce_fusion.8 = (f32[4,96,2,128]{3,2,1,0:T(2,128)S(1)}, f32[4,96,2,128]{3,2,1,0:T(2,128)S(1)}, f32[4,96,2,128]{3,2,1,0:T(2,128)S(1)}, f32[4,96,2,128...) fusion(bf16[8,4,96,4,130]{4,0,3,2,1:T(8,128)(2,1)S(1)} %fusion.5, ...), kind=kLoop, calls=%fused_computation.30 | loop fusion | flops 13565952 | bytes 11796672 | tf_op jit(solution)/shard_map/reduce_sum | solution.py:86
  265.7 4.2 multiply_reduce_fusion.7
  274.1 234.6 %reduce-scatter.7.cloned.1.call-done = f32[32,256]{1,0:T(8,128)} async-done(((f32[1024,256]{1,0:T(8,128)}), f32[32,256]{1,0:T(8,128)}) %reduce-scatter.7.cloned.1.call-update) | async-done | bytes 32784
  510.2 29.6 %reduce-scatter.5.cloned.1.call-done = f32[4,96,128]{2,1,0:T(8,128)} async-done(((f32[4,96,1024]{2,1,0:T(8,128)}), f32[4,96,128]{2,1,0:T(8,128)}) %reduce-scatter.5.cloned.1.call-update) | async-done | bytes 196624 | tf_op jit(solution)/shard_map/reduce_scatter | solution.py:136
  (53 shorter events, 30.1 us)
Async XLA Ops:
  7.2 125.8 %copy-start = (bf16[4,96,1024]{2,1,0:T(8,128)(2,1)S(1)}, bf16[4,96,1024]{2,1,0:T(8,128)(2,1)}, u32[]{:S(2)}) copy-start(bf16[4,96,1024]{2,1,0:T(8,128)(2,1)} %param.9) | copy-start | bytes 2359300
  7.2 132.1 %copy-start.3 = (bf16[8,3,3]{0,2,1:T(4,128)(2,1)S(1)}, bf16[8,3,3]{0,2,1:T(4,128)(2,1)}, u32[]{:S(2)}) copy-start(bf16[8,3,3]{0,2,1:T(4,128)(2,1)} %param.10) | copy-start | bytes 436
  7.2 501.5 %reduce-scatter.7.cloned.1.call-start = ((), (), s32[]{:S(2)}) async-start(), calls=%async_computation.3 | async-start | bytes 1081344
  133.7 7.0 %collective-permute-start = (bf16[4,96,1,128]{3,2,1,0:T(2,128)(2,1)S(1)}, bf16[4,96,1,128]{3,2,1,0:T(2,128)(2,1)S(1)}, u32[]{:S(2)}, u32[]{:S(2)}) collective-permute-start(bf16[4,96,1,128]{3,2,1,0:T(2,128)(2,1)S(1)} %get-tuple-element.38), channel_id=1, source_target_pairs={{0,32},{32,64},{64,96},{96,128},{128,160},{160,192},{192,224},{1,3... | collective-permute-start | bytes 294920 | tf_op jit(solution)/shard_map/ppermute | solution.py:15
  135.7 6.8 %collective-permute-start.1 = (bf16[4,96,1,128]{3,2,1,0:T(2,128)(2,1)S(1)}, bf16[4,96,1,128]{3,2,1,0:T(2,128)(2,1)S(1)}, u32[]{:S(2)}, u32[]{:S(2)}) collective-permute-start(bf16[4,96,1,128]{3,2,1,0:T(2,128)(2,1)S(1)} %get-tuple-element.39), channel_id=1, source_target_pairs={{32,0},{64,32},{96,64},{128,96},{160,128},{192,160},{224,192},{33,... | collective-permute-start | bytes 294920 | tf_op jit(solution)/shard_map/ppermute | solution.py:17
  139.3 7.4 %copy-start.4 = (f32[8]{0:T(128)S(1)}, f32[8]{0:T(128)}, u32[]{:S(2)}) copy-start(f32[8]{0:T(128)} %param.11) | copy-start | bytes 100
  146.7 5.2 copy-start.1
  146.7 5.4 copy-start.2
  149.1 14.2 %collective-permute-start.2 = (bf16[8,1,96,2,128]{4,0,3,2,1:T(8,128)(2,1)S(1)}, bf16[8,1,96,2,128]{4,0,3,2,1:T(8,128)(2,1)S(1)}, u32[]{:S(2)}, u32[]{:S(2)}) collective-permute-start(bf16[8,1,96,2,128]{4,0,3,2,1:T(8,128)(2,1)S(1)} %get-tuple-element.27), channel_id=1, source_target_pairs={{0,1},{1,2},{2,3},{3,4},{4,5},{5,6},{6,7},{7,8},{8,9},{9,10},{10,1... | collective-permute-start | bytes 1179656 | tf_op jit(solution)/shard_map/ppermute | solution.py:15
  150.5 33.0 %collective-permute-start.3 = (bf16[8,1,96,2,128]{4,0,3,2,1:T(8,128)(2,1)S(1)}, bf16[8,1,96,2,128]{4,0,3,2,1:T(8,128)(2,1)S(1)}, u32[]{:S(2)}, u32[]{:S(2)}) collective-permute-start(bf16[8,1,96,2,128]{4,0,3,2,1:T(8,128)(2,1)S(1)} %get-tuple-element.28), channel_id=1, source_target_pairs={{1,0},{2,1},{3,2},{4,3},{5,4},{6,5},{7,6},{8,7},{9,8},{10,9},{11,1... | collective-permute-start | bytes 1179656 | tf_op jit(solution)/shard_map/ppermute | solution.py:17
  190.1 2.2 copy-start.5
  190.1 2.2 copy-start.6
  200.0 21.8 %collective-permute-start.5 = (bf16[8,1,96,2,128]{4,0,3,2,1:T(8,128)(2,1)S(1)}, bf16[8,1,96,2,128]{4,0,3,2,1:T(8,128)(2,1)S(1)}, u32[]{:S(2)}, u32[]{:S(2)}) collective-permute-start(bf16[8,1,96,2,128]{4,0,3,2,1:T(8,128)(2,1)S(1)} %get-tuple-element.25), channel_id=1, source_target_pairs={{1,0},{2,1},{3,2},{4,3},{5,4},{6,5},{7,6},{8,7},{9,8},{10,9},{11,1... | collective-permute-start | bytes 1179656 | tf_op jit(solution)/shard_map/ppermute | solution.py:17
  201.3 20.5 %collective-permute-start.4 = (bf16[8,1,96,2,128]{4,0,3,2,1:T(8,128)(2,1)S(1)}, bf16[8,1,96,2,128]{4,0,3,2,1:T(8,128)(2,1)S(1)}, u32[]{:S(2)}, u32[]{:S(2)}) collective-permute-start(bf16[8,1,96,2,128]{4,0,3,2,1:T(8,128)(2,1)S(1)} %get-tuple-element.26), channel_id=1, source_target_pairs={{0,1},{1,2},{2,3},{3,4},{4,5},{5,6},{6,7},{7,8},{8,9},{9,10},{10,1... | collective-permute-start | bytes 1179656 | tf_op jit(solution)/shard_map/ppermute | solution.py:15
  237.7 13.3 %collective-permute-start.6 = (bf16[8,4,96,1,128]{4,0,3,2,1:T(8,128)(2,1)S(1)}, bf16[8,4,96,1,128]{4,0,3,2,1:T(8,128)(2,1)S(1)}, u32[]{:S(2)}, u32[]{:S(2)}) collective-permute-start(bf16[8,4,96,1,128]{4,0,3,2,1:T(8,128)(2,1)S(1)} %get-tuple-element.23), channel_id=1, source_target_pairs={{0,32},{32,64},{64,96},{96,128},{128,160},{160,192},{192,224},{1,3... | collective-permute-start | bytes 2359304 | tf_op jit(solution)/shard_map/ppermute | solution.py:15
  239.6 13.1 %collective-permute-start.7 = (bf16[8,4,96,1,128]{4,0,3,2,1:T(8,128)(2,1)S(1)}, bf16[8,4,96,1,128]{4,0,3,2,1:T(8,128)(2,1)S(1)}, u32[]{:S(2)}, u32[]{:S(2)}) collective-permute-start(bf16[8,4,96,1,128]{4,0,3,2,1:T(8,128)(2,1)S(1)} %get-tuple-element.24), channel_id=1, source_target_pairs={{32,0},{64,32},{96,64},{128,96},{160,128},{192,160},{224,192},{33,... | collective-permute-start | bytes 2359304 | tf_op jit(solution)/shard_map/ppermute | solution.py:17
  272.5 267.3 %reduce-scatter.5.cloned.1.call-start = ((), (), s32[]{:S(2)}) async-start(), calls=%async_computation.2 | async-start | bytes 1769472 | tf_op jit(solution)/shard_map/reduce_scatter | solution.py:136
Sparse Core Ops, SparseCore 0:
  272.6 236.0 reduce-scatter.6
  512.0 27.7 reduce-scatter.4
where the time goes:
time: 551 us; the launch traced here: 547 us
  waiting for transfers between devices  315 us (57%)
  blocking collectives  125 us (23%)
  matrix products  38.9 us (7%)
  other arithmetic  24.5 us (4%)
  starting transfers between devices  24.2 us (4%)
  between operations  14.4 us (3%)
    unnamed x3, waiting for transfers between devices  235 us
    all_gather x1, blocking collectives, body(): src_full = lax.all_gather(src_feat, 'tgt', axis=2, tiled=True)  125 us
    ppermute x4, waiting for transfers between devices, extended(): lax.ppermute(head, axis, [((i + 1) % count, i) for i in range(ends)])  33 us
    reduce_scatter x1, waiting for transfers between devices, body(): grad_tgt = lax.psum_scatter(term, 'src', scatter_dimension=2, tiled=True)  29.6 us
    dot_general x9, matrix products, target_filter(): jnp.einsum('op,pklij->oklij', w_tgt[:, :, a, b], padded[:, a:a + rows_k,...  18.6 us
    dot_general x9, matrix products, target_adjoint(): jnp.einsum('op,oklij->pklij', w_tgt[:, :, a, b], padded[:, 2 - a:2 - a +...  17.9 us
    ppermute x4, waiting for transfers between devices, extended(): lax.ppermute(tail, axis, [(i, (i + 1) % count) for i in range(ends)])  17.8 us
    ppermute x4, starting transfers between devices, extended(): lax.ppermute(tail, axis, [(i, (i + 1) % count) for i in range(ends)])  13.9 us
  transfers between devices with their start and end apart: 10, of which 9 were waited for; matrix products, arithmetic and copies ran while one was open for 1% of the time, Pallas kernels for 0%

commit v1 on v0

v1 whole, which is shorter than its diff:
```python
import functools

import jax
import jax.numpy as jnp
import numpy as np
from jax import lax
from jax.experimental import pallas as pl
from jax.experimental.pallas import tpu as pltpu
from jax.sharding import PartitionSpec as P

BF = jnp.bfloat16
F32 = jnp.float32
TAPS = 10


def shift_lanes(v, by):
    n = v.shape[1]
    lane = lax.broadcasted_iota(jnp.int32, v.shape, 1)
    edge = 0 if by == 1 else n - 1
    return jnp.where(lane == edge, 0.0, pltpu.roll(v, by % n, 1))


def conv_kernel(
    cols,
    wf_ref, wb_ref, bias_ref, wout_ref,
    own_ref, up_ref, dn_ref, lo_ref, hi_ref, cot_ref, cup_ref, cdn_ref,
    score_ref, g_ref, glo_ref, ghi_ref,
    cs, rows, cotf, cots, gp, sc, gs,
):
    for k in range(8):
        ref, at = (up_ref, k) if k < 2 else (own_ref, k - 2) if k < 6 else (dn_ref, k - 6)
        plane = ref[at].astype(F32)
        cs[0, pl.ds(k, cols, stride=8), :] = lo_ref[k].astype(F32)
        cs[1, pl.ds(k, cols, stride=8), :] = plane[:, :128]
        cs[2, pl.ds(k, cols, stride=8), :] = plane[:, 128:]
        cs[3, pl.ds(k, cols, stride=8), :] = hi_ref[k].astype(F32)
    zeros = jnp.zeros((cols, 128), F32)
    cotf[pl.ds(0, 2 * cols), :] = cup_ref[...].astype(F32)
    cotf[pl.ds(2 * cols, 8 * cols), :] = cot_ref[...].astype(F32)
    cotf[pl.ds(10 * cols, 2 * cols), :] = cdn_ref[...].astype(F32)
    for i in range(2):
        cots[i, pl.ds(0, cols, stride=8), :] = zeros
        cots[i, pl.ds(7, cols, stride=8), :] = zeros
        for k in range(6):
            cots[i, pl.ds(k + 1, cols, stride=8), :] = cotf[pl.ds(2 * cols * k + i, cols, stride=2), :]

    group = TAPS * 8
    for end in (0, cols + 1):
        rows[pl.ds(end * group, group), :] = jnp.zeros((group, 256), BF)
        gp[pl.ds(end * 64, 64), :] = jnp.zeros((64, 256), BF)

    def spread(l, _):
        at = pl.multiple_of(l * 8, 8)
        taps = []
        for i in range(4):
            v = cs[i, pl.ds(at, 8), :]
            taps.append((shift_lanes(v, 1), v, shift_lanes(v, -1)))
        for i in range(2):
            block = [taps[i + a][b] for a in range(3) for b in range(3)]
            block.append(jnp.zeros((8, 128), F32))
            rows[pl.ds(pl.multiple_of((l + 1) * group, 16), group), pl.ds(i * 128, 128)] = jnp.concatenate(block, 0).astype(BF)
        return 0

    lax.fori_loop(0, cols, spread, 0, unroll=4)

    wf = wf_ref[...]
    wb = wb_ref[...]

    def forward(l, _):
        kind = jnp.where(l == 0, 0, jnp.where(l == cols - 1, 2, 1))
        window = rows[pl.ds(pl.multiple_of(l * group, 16), 3 * group), :]
        u = jnp.dot(wf, window, preferred_element_type=F32)
        u = u + bias_ref[pl.ds(pl.multiple_of(kind * 64, 64), 64), :]
        th = jnp.tanh(u)
        q = u * th
        g = (1.0 + u) + th * (1.0 - q)
        s = u + q
        at = pl.multiple_of(l * 8, 8)
        cot = jnp.concatenate([cots[0, pl.ds(at, 8), :], cots[1, pl.ds(at, 8), :]], 1)
        total = jnp.zeros((8, 256), F32)
        out = []
        for o in range(8):
            w = wout_ref[o]
            total = total + w * s[o * 8:o * 8 + 8]
            out.append(g[o * 8:o * 8 + 8] * (cot * (0.5 * w)))
        gp[pl.ds(pl.multiple_of((l + 1) * 64, 64), 64), :] = jnp.concatenate(out, 0).astype(BF)
        sc[0, pl.ds(at, 8), :] = total[:, :128]
        sc[1, pl.ds(at, 8), :] = total[:, 128:]
        return 0

    lax.fori_loop(0, cols, forward, 0, unroll=4)

    def backward(m, _):
        window = gp[pl.ds(pl.multiple_of(m * 128, 128), 256), :]
        t = jnp.dot(wb, window, preferred_element_type=F32)
        at = pl.multiple_of(m * 8, 8)
        for io in range(4):
            part = []
            for b in range(3):
                pieces = []
                for a in range(3):
                    i = io - a
                    if 0 <= i < 2:
                        pieces.append(t[(b * 3 + a) * 8:(b * 3 + a) * 8 + 8, i * 128:(i + 1) * 128])
                part.append(functools.reduce(jnp.add, pieces))
            gs[io, pl.ds(at, 8), :] = shift_lanes(part[0], -1) + part[1] + shift_lanes(part[2], 1)
        return 0

    lax.fori_loop(0, cols // 2, backward, 0, unroll=4)

    for k in range(4):
        for i in range(2):
            cotf[pl.ds(2 * cols * k + i, cols, stride=2), :] = sc[i, pl.ds(k + 2, cols, stride=8), :]
    score_ref[...] = cotf[pl.ds(0, 8 * cols), :].astype(BF)
    for k in range(4):
        here = pl.ds(k * cols, cols)
        glo_ref[here, :] = gs[0, pl.ds(k, cols, stride=4), :].astype(BF)
        g_ref[here, pl.ds(0, 128)] = gs[1, pl.ds(k, cols, stride=4), :]
        g_ref[here, pl.ds(128, 128)] = gs[2, pl.ds(k, cols, stride=4), :]
        ghi_ref[here, :] = gs[3, pl.ds(k, cols, stride=4), :].astype(BF)


def conv(cols, weights, own, up, dn, lo, hi, cot, cup, cdn):
    wf, wb, bias, w_out = weights
    vmem = pl.BlockSpec(memory_space=pltpu.VMEM)
    smem = pl.BlockSpec(memory_space=pltpu.SMEM)
    n = 4 * cols
    return pl.pallas_call(
        functools.partial(conv_kernel, cols),
        out_shape=(
            jax.ShapeDtypeStruct((8 * cols, 128), BF),
            jax.ShapeDtypeStruct((n, 256), F32),
            jax.ShapeDtypeStruct((n, 128), BF),
            jax.ShapeDtypeStruct((n, 128), BF),
        ),
        in_specs=[vmem, vmem, vmem, smem] + [vmem] * 8,
        out_specs=(vmem,) * 4,
        scratch_shapes=[
            pltpu.VMEM((4, 8 * cols, 128), F32),
            pltpu.VMEM(((cols + 2) * TAPS * 8, 256), BF),
            pltpu.VMEM((12 * cols, 128), F32),
            pltpu.VMEM((2, 8 * cols, 128), F32),
            pltpu.VMEM(((cols + 2) * 64, 256), BF),
            pltpu.VMEM((2, 8 * cols, 128), F32),
            pltpu.VMEM((4, 4 * cols, 128), F32),
        ],
        compiler_params=pltpu.CompilerParams(vmem_limit_bytes=40 * 2**20),
        cost_estimate=pl.CostEstimate(flops=4 * 10**9, transcendentals=10**7, bytes_accessed=4 * 10**6),
    )(wf, wb, bias, w_out, own, up, dn, lo, hi, cot, cup, cdn)


def filters(w_src, b_src, w_tgt, b_tgt, first_row, total_rows):
    both = jnp.einsum(
        "opde,pab->odeab", w_tgt.astype(F32), w_src.astype(F32), precision=lax.Precision.HIGHEST
    )
    up = np.zeros((3, 8, 8), np.float32)
    for d in range(3):
        for m in range(1, 7):
            up[d, m, m + d - 1] = 1
    flat = jnp.pad(both.reshape(8, 3, 3, 9), ((0, 0), (0, 0), (0, 0), (0, TAPS - 9)))
    wf = (0.5 * jnp.einsum("odex,dmk->omexk", flat, up)).reshape(64, 3 * TAPS * 8).astype(BF)
    back = np.zeros((3, 4, 8), np.float32)
    side = np.zeros((3, 2, 4), np.float32)
    for d in range(3):
        for k in range(4):
            back[d, k, k + 3 - d] = 1
        for s in range(2):
            side[d, s, s + 2 - d] = 1
    spots = np.einsum("dkm,esl->desklm", back, side)
    wb = jnp.einsum("odeab,desklm->baskyom".replace("y", "l"), both, spots).reshape(72, 256).astype(BF)
    lift = jnp.einsum(
        "opde,p->ode", w_tgt.astype(F32), b_src, precision=lax.Precision.HIGHEST
    )
    row = first_row - 2 + jnp.arange(8)
    inside = ((row >= 0) & (row < total_rows)).astype(F32)
    edge = np.ones((3, 3), np.float32)
    edge[0, 0] = 0
    edge[2, 2] = 0
    along = jnp.einsum("ode,te->tod", lift, edge, precision=lax.Precision.HIGHEST)
    reach = jnp.einsum("dmk,k->md", up, inside, precision=lax.Precision.HIGHEST)
    bias = b_tgt[None, :, None] + jnp.einsum("tod,md->tom", along, reach, precision=lax.Precision.HIGHEST)
    bias = jnp.broadcast_to((0.5 * bias).reshape(192, 1), (192, 256))
    return wf, wb, bias


def permuted(x, pairs):
    return lax.ppermute(x, ("src", "tgt"), pairs)


def body(src_feat, tgt_feat, w_src, b_src, w_tgt, b_tgt, w_out, cotangent):
    rows_k, cols, rows_i, cols_j = cotangent.shape
    chans = tgt_feat.shape[2]
    scale = chans ** (-0.5)
    n_src, n_tgt = lax.axis_size("src"), lax.axis_size("tgt")
    s, t = lax.axis_index("src"), lax.axis_index("tgt")
    block = chans // n_tgt

    def joint(move):
        out = []
        for a in range(n_src):
            for b in range(n_tgt):
                c, d = move(a, b)
                if 0 <= c < n_src and 0 <= d < n_tgt:
                    out.append((a * n_tgt + b, c * n_tgt + d))
        return out

    tgt_up = joint(lambda a, b: (a, b + 1))
    tgt_dn = joint(lambda a, b: (a, b - 1))
    src_up = joint(lambda a, b: (a + 1, b))
    src_dn = joint(lambda a, b: (a - 1, b))

    weights = filters(w_src, b_src, w_tgt, b_tgt, t * rows_k, rows_k * n_tgt)
    tgt_flat = tgt_feat.reshape(rows_k * cols, chans)

    piece = src_feat.reshape(rows_i * cols_j, block).T
    src_t = lax.all_to_all(
        jnp.broadcast_to(piece[None], (n_tgt, block, rows_i * cols_j)), "tgt", 0, 0, tiled=True
    ).reshape(chans, rows_i * cols_j)

    raw = jnp.dot(tgt_flat, src_t, preferred_element_type=F32)
    own = (raw * scale).astype(BF).reshape(rows_k, cols, rows_i * cols_j)
    cot = cotangent.reshape(rows_k, cols * rows_i, cols_j)
    up = permuted(own[rows_k - 2:], tgt_up)
    dn = permuted(own[:2], tgt_dn)
    cup = permuted(cot[rows_k - 1], tgt_up)
    cdn = permuted(cot[0], tgt_dn)
    tall = jnp.concatenate([up, own, dn], 0)
    lo = permuted(tall[:, :, cols_j:], src_up)
    hi = permuted(tall[:, :, :cols_j], src_dn)

    score, g_own, g_lo, g_hi = conv(
        cols, (*weights, w_out), own, up, dn, lo, hi,
        cot.reshape(rows_k * cols * rows_i, cols_j), cup, cdn,
    )
    from_hi = permuted(g_lo, src_dn)
    from_lo = permuted(g_hi, src_up)
    g = (g_own + jnp.concatenate([from_lo, from_hi], 1).astype(F32)).astype(BF)

    part = lax.dot_general(tgt_flat, g, (((0,), (0,)), ((), ())), preferred_element_type=F32) * scale
    parts = lax.all_to_all(
        part.astype(BF).reshape(n_tgt, block, rows_i * cols_j), "tgt", 0, 0, tiled=True
    )
    grad_src = jnp.sum(parts.astype(F32), 0).reshape(block, rows_i, cols_j)

    z, core = s // 2, s % 2
    cut = src_t.reshape(n_src, chans // n_src, rows_i * cols_j)
    hops = n_src // 2

    def blocks(side):
        return jnp.concatenate([lax.dynamic_index_in_dim(cut, (z ^ m) * 2 + side, 0, False) for m in range(hops)], 0)

    over = (((1,), (1,)), ((), ()))
    mine = lax.dot_general(g, blocks(core), over, preferred_element_type=F32) * scale
    other = lax.dot_general(g, blocks(1 - core), over, preferred_element_type=F32) * scale
    got = permuted(other.astype(BF), joint(lambda a, b: (a ^ 1, b)))
    both = mine + got.astype(F32)
    width = chans // n_src
    total = both[:, :width]
    for m in range(1, hops):
        total = total + permuted(
            both[:, m * width:(m + 1) * width].astype(BF), joint(lambda a, b, m=m: (a ^ (2 * m), b))
        ).astype(F32)
    grad_tgt = total.reshape(rows_k, cols, width)
    return (score.reshape(cotangent.shape), grad_src, grad_tgt)


def solution(mesh):
    placed = (
        P("src", None, "tgt"),
        P("tgt", None, None),
        P(),
        P(),
        P(),
        P(),
        P(),
        P("tgt", None, "src", None),
    )
    return jax.shard_map(
        body,
        mesh=mesh,
        in_specs=placed,
        out_specs=(P("tgt", None, "src", None), P("tgt", "src", None), P("tgt", None, "src")),
        check_vma=False,
    )
```

time: 551 us -> 129 us (0.23)
  waiting for transfers between devices: 315 us -> 43 us
  blocking collectives: 125 us -> 0 us
  matrix products: 38.9 us -> 3.89 us
  starting transfers between devices: 24.2 us -> 53.5 us
  other arithmetic: 24.5 us -> 0.9 us
  Pallas kernels: 0 us -> 14.3 us
  between operations: 14.4 us -> 1.09 us
  local copies, waits for them, and re-layouts: 4.98 us -> 11.3 us
    unnamed x3 -> x0, waiting for transfers between devices: 235 us -> none
    all_gather x1 -> x0, blocking collectives: 125 us -> none  [body(): src_full = lax.all_gather(src_feat, 'tgt', axis=2, tiled=True)]
    dot_general x21 -> x11, matrix products: 38.9 us -> 3.89 us  [the longest x1 1.21 us: filters(): jnp.einsum('odeab,desklm->baskyom'.replace('y', 'l'), both, spots)]
    reduce_scatter x1 -> x0, waiting for transfers between devices: 29.6 us -> none  [body(): grad_tgt = lax.psum_scatter(term, 'src', scatter_dimension=2, tiled=True)]
    all_to_all x0 -> x2, starting transfers between devices: none -> 27 us  [the longest x1 13.8 us: body(): lax.all_to_all(part.astype(BF).reshape(n_tgt, block, rows_i * cols_j), 't...]
    ppermute x8 -> x12, waiting for transfers between devices: 50.8 us -> 27.9 us  [permuted(): return lax.ppermute(x, ('src', 'tgt'), pairs)]
    all_to_all x0 -> x2, waiting for transfers between devices: none -> 15 us  [the longest x1 11.2 us: body(): lax.all_to_all(jnp.broadcast_to(piece[None], (n_tgt, block, rows_i * cols...]
    pallas_call x0 -> x1, Pallas kernels: none -> 14.3 us  [conv(): pl.pallas_call(functools.partial(conv_kernel, cols), out_shape=(jax.Shape...]
  transfers between devices with their start and end apart: 10 -> 14, of which waited for: 9 -> 8; matrix products, arithmetic and copies ran while one was open for 1% -> 8% of each run, Pallas kernels for 0% -> 0%
where the time goes in v1:
time: 129 us; the launch traced here: 128 us
  starting transfers between devices  53.5 us (41%)
  waiting for transfers between devices  43 us (33%)
  Pallas kernels  14.3 us (11%)
  local copies, waits for them, and re-layouts  11.3 us (9%)
  matrix products  3.89 us (3%)
    ppermute x12, waiting for transfers between devices, permuted(): return lax.ppermute(x, ('src', 'tgt'), pairs)  27.9 us
    ppermute x12, starting transfers between devices, permuted(): return lax.ppermute(x, ('src', 'tgt'), pairs)  26.5 us
    pallas_call x1, Pallas kernels, conv(): pl.pallas_call(functools.partial(conv_kernel, cols), out_shape=(jax.Shape...  14.3 us
    all_to_all x1, starting transfers between devices, body(): lax.all_to_all(part.astype(BF).reshape(n_tgt, block, rows_i * cols_j), 't...  13.8 us
    all_to_all x1, starting transfers between devices, body(): lax.all_to_all(jnp.broadcast_to(piece[None], (n_tgt, block, rows_i * cols...  13.2 us
    all_to_all x1, waiting for transfers between devices, body(): lax.all_to_all(jnp.broadcast_to(piece[None], (n_tgt, block, rows_i * cols...  11.2 us
    all_to_all x1, waiting for transfers between devices, body(): lax.all_to_all(part.astype(BF).reshape(n_tgt, block, rows_i * cols_j), 't...  3.8 us
    unnamed x22, local copies, waits for them, and re-layouts  2.86 us
  transfers between devices with their start and end apart: 14, of which 8 were waited for; matrix products, arithmetic and copies ran while one was open for 8% of the time, Pallas kernels for 0%

profile of v1, /device:TPU:32, one launch (start us, length us, event | category | flops | bytes accessed | tf_op | source)
XLA Modules:
  0.0 127.9 jit_solution(6786492860087705538)
XLA Ops:
  2.3 13.2 %all-to-all-start = ((bf16[32,32,256]{2,1,0:T(8,128)(2,1)}), bf16[32,32,256]{2,1,0:T(8,128)(2,1)S(1)}, u32[]{:S(2)}, u32[]{:S(2)}) async-start(bf16[32,32,256]{2,1,0:T(8,128)(2,1)} %broadcast_in_dim.16), calls=%async_computation | async-start | bytes 1048576 | tf_op jit(solution)/shard_map/all_to_all | solution.py:216
  15.6 7.6 %collective-permute-start.4 = (bf16[192,128]{1,0:T(8,128)(2,1)S(1)}, bf16[192,128]{1,0:T(8,128)(2,1)S(1)}, u32[]{:S(2)}, u32[]{:S(2)}) collective-permute-start(bf16[192,128]{1,0:T(8,128)(2,1)S(1)} %bitcast.118), channel_id=1, source_target_pairs={{0,1},{1,2},{2,3},{3,4},{4,5},{5,6},{6,7},{7,8},{8,9},{9,10},{10,1... | collective-permute-start | bytes 147464 | tf_op jit(solution)/shard_map/ppermute | solution.py:187
  23.2 1.3 %collective-permute-start.5 = (bf16[192,128]{1,0:T(8,128)(2,1)S(1)}, bf16[192,128]{1,0:T(8,128)(2,1)S(1)}, u32[]{:S(2)}, u32[]{:S(2)}) collective-permute-start(bf16[192,128]{1,0:T(8,128)(2,1)S(1)} %bitcast.117), channel_id=1, source_target_pairs={{1,0},{2,1},{3,2},{4,3},{5,4},{6,5},{7,6},{8,7},{9,8},{10,9},{11,1... | collective-permute-start | bytes 147464 | tf_op jit(solution)/shard_map/ppermute | solution.py:187
  27.8 1.2 fusion.4
  29.0 11.2 %all-to-all-done = bf16[32,32,256]{2,1,0:T(8,128)(2,1)S(1)} async-done(((bf16[32,32,256]{2,1,0:T(8,128)(2,1)}), bf16[32,32,256]{2,1,0:T(8,128)(2,1)S(1)}, u32[]{:S(2)}, u32[]{:S(2)}) %all-to-all-start) | async-done | bytes 524320 | tf_op jit(solution)/shard_map/all_to_all | solution.py:216
  40.7 2.1 %collective-permute-start = (bf16[2,96,256]{2,1,0:T(8,128)(2,1)S(1)}, bf16[2,96,256]{2,1,0:T(8,128)(2,1)S(1)}, u32[]{:S(2)}, u32[]{:S(2)}) collective-permute-start(bf16[2,96,256]{2,1,0:T(8,128)(2,1)S(1)} %bitcast.116), channel_id=1, source_target_pairs={{0,1},{1,2},{2,3},{3,4},{4,5},{5,6},{6,7},{7,8},{8,9},{9,10},{10,1... | collective-permute-start | bytes 294920 | tf_op jit(solution)/shard_map/ppermute | solution.py:187
  42.8 1.3 %collective-permute-start.1 = (bf16[2,96,256]{2,1,0:T(8,128)(2,1)S(1)}, bf16[2,96,256]{2,1,0:T(8,128)(2,1)S(1)}, u32[]{:S(2)}, u32[]{:S(2)}) collective-permute-start(bf16[2,96,256]{2,1,0:T(8,128)(2,1)S(1)} %bitcast.115), channel_id=1, source_target_pairs={{1,0},{2,1},{3,2},{4,3},{5,4},{6,5},{7,6},{8,7},{9,8},{10,9},{11,1... | collective-permute-start | bytes 294920 | tf_op jit(solution)/shard_map/ppermute | solution.py:187
  45.0 8.2 %collective-permute-done.1.dn_ref = bf16[2,96,256]{2,1,0:T(8,128)(2,1)S(1)} collective-permute-done((bf16[2,96,256]{2,1,0:T(8,128)(2,1)S(1)}, bf16[2,96,256]{2,1,0:T(8,128)(2,1)S(1)}, u32[]{:S(2)}, u32[]{:S(2)}) %collective-permute-start.1) | collective-permute-done | bytes 98336 | tf_op jit(solution)/shard_map/ppermute | solution.py:187
  54.1 2.0 %collective-permute-start.2 = (bf16[8,96,128]{2,1,0:T(8,128)(2,1)}, bf16[8,96,128]{2,1,0:T(8,128)(2,1)S(1)}, u32[]{:S(2)}, u32[]{:S(2)}) collective-permute-start(bf16[8,96,128]{2,1,0:T(8,128)(2,1)} %get-tuple-element.23), channel_id=1, source_target_pairs={{0,32},{1,33},{2,34},{3,35},{4,36},{5,37},{6,38},{7,39},{8,40},{9,... | collective-permute-start | bytes 589832 | tf_op jit(solution)/shard_map/ppermute | solution.py:187
  56.1 3.6 %collective-permute-start.3 = (bf16[8,96,128]{2,1,0:T(8,128)(2,1)}, bf16[8,96,128]{2,1,0:T(8,128)(2,1)S(1)}, u32[]{:S(2)}, u32[]{:S(2)}) collective-permute-start(bf16[8,96,128]{2,1,0:T(8,128)(2,1)} %get-tuple-element.22), channel_id=1, source_target_pairs={{32,0},{33,1},{34,2},{35,3},{36,4},{37,5},{38,6},{39,7},{40,8},{41... | collective-permute-start | bytes 589832 | tf_op jit(solution)/shard_map/ppermute | solution.py:187
  60.0 1.5 %copy.22 = bf16[8,8,3,10,8]{1,0,4,3,2:T(8,128)(2,1)S(1)} copy(bf16[8,8,3,10,8]{3,4,1,2,0:T(8,128)(2,1)S(1)} %fusion.7) | data formatting | bytes 61440 | tf_op jit(solution)/shard_map/convert_element_type | solution.py:161
  62.0 1.1 copy.24
  64.7 14.3 %shard_map.139 = (bf16[768,128]{1,0:T(8,128)(2,1)}, f32[384,256]{1,0:T(8,128)S(1)}, bf16[384,128]{1,0:T(8,128)(2,1)S(1)}, bf16[384,128]{1,0:T(8,128)(2,1)S(1)}) custom-call(bf16[64,240]{1,0:T(8,128)(2,1)S(1)} %copy.26.wf_ref, bf16[72,256]{1,0:T(8,128)(2,1)S(1)} %convert_element_type.61.wb_ref, f32[192,256]{1,0:T(8,128)S(1)} %broadcast_in_dim.7.bias_ref, ...), custom_call_target="tpu_custom_call" | custom-call | flops 4000000000 | bytes 4000000 | tf_op jit(solution)/shard_map/pallas_call | solution.py:128
  79.1 2.9 %collective-permute-start.7 = (bf16[384,128]{1,0:T(8,128)(2,1)S(1)}, bf16[384,128]{1,0:T(8,128)(2,1)S(1)}, u32[]{:S(2)}, u32[]{:S(2)}) collective-permute-start(bf16[384,128]{1,0:T(8,128)(2,1)S(1)} %get-tuple-element.10), channel_id=1, source_target_pairs={{32,0},{33,1},{34,2},{35,3},{36,4},{37,5},{38,6},{39,7},{40,8},{41... | collective-permute-start | bytes 294920 | tf_op jit(solution)/shard_map/ppermute | solution.py:187
  82.0 1.9 %collective-permute-start.6 = (bf16[384,128]{1,0:T(8,128)(2,1)S(1)}, bf16[384,128]{1,0:T(8,128)(2,1)S(1)}, u32[]{:S(2)}, u32[]{:S(2)}) collective-permute-start(bf16[384,128]{1,0:T(8,128)(2,1)S(1)} %get-tuple-element.9), channel_id=1, source_target_pairs={{0,32},{1,33},{2,34},{3,35},{4,36},{5,37},{6,38},{7,39},{8,40},{9,... | collective-permute-start | bytes 294920 | tf_op jit(solution)/shard_map/ppermute | solution.py:187
  84.2 3.7 %collective-permute-done.6 = bf16[384,128]{1,0:T(8,128)(2,1)S(1)} collective-permute-done((bf16[384,128]{1,0:T(8,128)(2,1)S(1)}, bf16[384,128]{1,0:T(8,128)(2,1)S(1)}, u32[]{:S(2)}, u32[]{:S(2)}) %collective-permute-start.6) | collective-permute-done | bytes 98336 | tf_op jit(solution)/shard_map/ppermute | solution.py:187
  88.9 1.0 copy.27
  89.9 13.8 %all-to-all-start.1 = ((bf16[32,32,256]{2,1,0:T(8,128)(2,1)}), bf16[32,32,256]{2,1,0:T(8,128)(2,1)S(1)}, u32[]{:S(2)}, u32[]{:S(2)}) async-start(bf16[32,32,256]{2,1,0:T(8,128)(2,1)} %bitcast.35), calls=%async_computation.1 | async-start | bytes 1048576 | tf_op jit(solution)/shard_map/all_to_all | solution.py:240
  104.1 1.1 collective-permute-start.11
  105.2 1.1 collective-permute-start.10
  106.3 1.4 %collective-permute-start.9 = (bf16[384,128]{1,0:T(8,128)(2,1)S(1)}, bf16[384,128]{1,0:T(8,128)(2,1)S(1)}, u32[]{:S(2)}, u32[]{:S(2)}) collective-permute-start(bf16[384,128]{1,0:T(8,128)(2,1)S(1)} %get-tuple-element.19), channel_id=1, source_target_pairs={{0,64},{1,65},{2,66},{3,67},{4,68},{5,69},{6,70},{7,71},{8,72},{9,... | collective-permute-start | bytes 294920 | tf_op jit(solution)/shard_map/ppermute | solution.py:187
  107.7 9.2 %collective-permute-done.11 = bf16[384,128]{1,0:T(8,128)(2,1)S(1)} collective-permute-done((bf16[384,128]{1,0:T(8,128)(2,1)S(1)}, bf16[384,128]{1,0:T(8,128)(2,1)S(1)}, u32[]{:S(2)}, u32[]{:S(2)}) %collective-permute-start.11) | collective-permute-done | bytes 98336 | tf_op jit(solution)/shard_map/ppermute | solution.py:187
  116.9 5.8 %collective-permute-done.10 = bf16[384,128]{1,0:T(8,128)(2,1)S(1)} collective-permute-done((bf16[384,128]{1,0:T(8,128)(2,1)S(1)}, bf16[384,128]{1,0:T(8,128)(2,1)S(1)}, u32[]{:S(2)}, u32[]{:S(2)}) %collective-permute-start.10) | collective-permute-done | bytes 98336 | tf_op jit(solution)/shard_map/ppermute | solution.py:187
  123.4 3.8 %all-to-all-done.1 = bf16[32,32,256]{2,1,0:T(8,128)(2,1)S(1)} async-done(((bf16[32,32,256]{2,1,0:T(8,128)(2,1)}), bf16[32,32,256]{2,1,0:T(8,128)(2,1)S(1)}, u32[]{:S(2)}, u32[]{:S(2)}) %all-to-all-start.1) | async-done | bytes 524320 | tf_op jit(solution)/shard_map/all_to_all | solution.py:240
  (60 shorter events, 12.3 us)
Async XLA Ops:
  0.6 39.7 %copy-start = (bf16[4,96,1024]{2,1,0:T(8,128)(2,1)S(1)}, bf16[4,96,1024]{2,1,0:T(8,128)(2,1)}, u32[]{:S(2)}) copy-start(bf16[4,96,1024]{2,1,0:T(8,128)(2,1)} %param.13) | copy-start | bytes 2359300
  2.3 13.2 %copy-start.1 = (bf16[4,96,2,128]{3,2,1,0:T(2,128)(2,1)S(1)}, bf16[4,96,2,128]{3,2,1,0:T(2,128)(2,1)}, u32[]{:S(2)}) copy-start(bf16[4,96,2,128]{3,2,1,0:T(2,128)(2,1)} %param.19) | copy-start | bytes 589828
  2.3 38.0 %all-to-all-start = ((bf16[32,32,256]{2,1,0:T(8,128)(2,1)}), bf16[32,32,256]{2,1,0:T(8,128)(2,1)S(1)}, u32[]{:S(2)}, u32[]{:S(2)}) async-start(bf16[32,32,256]{2,1,0:T(8,128)(2,1)} %broadcast_in_dim.16), calls=%async_computation | async-start | bytes 1048576 | tf_op jit(solution)/shard_map/all_to_all | solution.py:216
  15.5 9.0 %copy-start.3 = (bf16[8,8,3,3]{1,0,3,2:T(8,128)(2,1)S(1)}, bf16[8,8,3,3]{1,0,3,2:T(8,128)(2,1)}, u32[]{:S(2)}) copy-start(bf16[8,8,3,3]{1,0,3,2:T(8,128)(2,1)} %param.16) | copy-start | bytes 3460
  15.6 8.9 %copy-start.6 = (bf16[8,3,3]{0,2,1:T(4,128)(2,1)S(1)}, bf16[8,3,3]{0,2,1:T(4,128)(2,1)}, u32[]{:S(2)}) copy-start(bf16[8,3,3]{0,2,1:T(4,128)(2,1)} %param.14) | copy-start | bytes 436
  15.6 48.3 %collective-permute-start.4 = (bf16[192,128]{1,0:T(8,128)(2,1)S(1)}, bf16[192,128]{1,0:T(8,128)(2,1)S(1)}, u32[]{:S(2)}, u32[]{:S(2)}) collective-permute-start(bf16[192,128]{1,0:T(8,128)(2,1)S(1)} %bitcast.118), channel_id=1, source_target_pairs={{0,1},{1,2},{2,3},{3,4},{4,5},{5,6},{6,7},{7,8},{8,9},{9,10},{10,1... | collective-permute-start | bytes 147464 | tf_op jit(solution)/shard_map/ppermute | solution.py:187
  23.2 40.7 %collective-permute-start.5 = (bf16[192,128]{1,0:T(8,128)(2,1)S(1)}, bf16[192,128]{1,0:T(8,128)(2,1)S(1)}, u32[]{:S(2)}, u32[]{:S(2)}) collective-permute-start(bf16[192,128]{1,0:T(8,128)(2,1)S(1)} %bitcast.117), channel_id=1, source_target_pairs={{1,0},{2,1},{3,2},{4,3},{5,4},{6,5},{7,6},{8,7},{9,8},{10,9},{11,1... | collective-permute-start | bytes 147464 | tf_op jit(solution)/shard_map/ppermute | solution.py:187
  25.6 0.7 copy-start.7
  26.2 0.7 copy-start.5
  26.9 0.9 copy-start.10
  40.7 3.4 %copy-start.4 = (f32[3,8,8]{1,2,0:T(8,128)S(1)}, f32[3,8,8]{1,2,0:T(8,128)}, u32[]{:S(2)}) copy-start(f32[3,8,8]{1,2,0:T(8,128)} %constant.90) | copy-start | bytes 2308
  40.7 4.3 %collective-permute-start = (bf16[2,96,256]{2,1,0:T(8,128)(2,1)S(1)}, bf16[2,96,256]{2,1,0:T(8,128)(2,1)S(1)}, u32[]{:S(2)}, u32[]{:S(2)}) collective-permute-start(bf16[2,96,256]{2,1,0:T(8,128)(2,1)S(1)} %bitcast.116), channel_id=1, source_target_pairs={{0,1},{1,2},{2,3},{3,4},{4,5},{5,6},{6,7},{7,8},{8,9},{9,10},{10,1... | collective-permute-start | bytes 294920 | tf_op jit(solution)/shard_map/ppermute | solution.py:187
  42.8 10.4 %collective-permute-start.1 = (bf16[2,96,256]{2,1,0:T(8,128)(2,1)S(1)}, bf16[2,96,256]{2,1,0:T(8,128)(2,1)S(1)}, u32[]{:S(2)}, u32[]{:S(2)}) collective-permute-start(bf16[2,96,256]{2,1,0:T(8,128)(2,1)S(1)} %bitcast.115), channel_id=1, source_target_pairs={{1,0},{2,1},{3,2},{4,3},{5,4},{6,5},{7,6},{8,7},{9,8},{10,9},{11,1... | collective-permute-start | bytes 294920 | tf_op jit(solution)/shard_map/ppermute | solution.py:187
  54.0 5.7 %copy-start.9 = (f32[8]{0:T(128)S(1)}, f32[8]{0:T(128)}, u32[]{:S(2)}) copy-start(f32[8]{0:T(128)} %param.17) | copy-start | bytes 100
  54.1 9.9 %collective-permute-start.2 = (bf16[8,96,128]{2,1,0:T(8,128)(2,1)}, bf16[8,96,128]{2,1,0:T(8,128)(2,1)S(1)}, u32[]{:S(2)}, u32[]{:S(2)}) collective-permute-start(bf16[8,96,128]{2,1,0:T(8,128)(2,1)} %get-tuple-element.23), channel_id=1, source_target_pairs={{0,32},{1,33},{2,34},{3,35},{4,36},{5,37},{6,38},{7,39},{8,40},{9,... | collective-permute-start | bytes 589832 | tf_op jit(solution)/shard_map/ppermute | solution.py:187
  56.1 7.9 %collective-permute-start.3 = (bf16[8,96,128]{2,1,0:T(8,128)(2,1)}, bf16[8,96,128]{2,1,0:T(8,128)(2,1)S(1)}, u32[]{:S(2)}, u32[]{:S(2)}) collective-permute-start(bf16[8,96,128]{2,1,0:T(8,128)(2,1)} %get-tuple-element.22), channel_id=1, source_target_pairs={{32,0},{33,1},{34,2},{35,3},{36,4},{37,5},{38,6},{39,7},{40,8},{41... | collective-permute-start | bytes 589832 | tf_op jit(solution)/shard_map/ppermute | solution.py:187
  64.1 0.7 copy-start.2
  79.1 5.1 %collective-permute-start.7 = (bf16[384,128]{1,0:T(8,128)(2,1)S(1)}, bf16[384,128]{1,0:T(8,128)(2,1)S(1)}, u32[]{:S(2)}, u32[]{:S(2)}) collective-permute-start(bf16[384,128]{1,0:T(8,128)(2,1)S(1)} %get-tuple-element.10), channel_id=1, source_target_pairs={{32,0},{33,1},{34,2},{35,3},{36,4},{37,5},{38,6},{39,7},{40,8},{41... | collective-permute-start | bytes 294920 | tf_op jit(solution)/shard_map/ppermute | solution.py:187
  82.0 5.9 %collective-permute-start.6 = (bf16[384,128]{1,0:T(8,128)(2,1)S(1)}, bf16[384,128]{1,0:T(8,128)(2,1)S(1)}, u32[]{:S(2)}, u32[]{:S(2)}) collective-permute-start(bf16[384,128]{1,0:T(8,128)(2,1)S(1)} %get-tuple-element.9), channel_id=1, source_target_pairs={{0,32},{1,33},{2,34},{3,35},{4,36},{5,37},{6,38},{7,39},{8,40},{9,... | collective-permute-start | bytes 294920 | tf_op jit(solution)/shard_map/ppermute | solution.py:187
  88.3 15.4 %collective-permute-start.8 = (bf16[384,512]{1,0:T(8,128)(2,1)S(1)}, bf16[384,512]{1,0:T(8,128)(2,1)S(1)}, u32[]{:S(2)}, u32[]{:S(2)}) collective-permute-start(bf16[384,512]{1,0:T(8,128)(2,1)S(1)} %fusion.3), channel_id=1, source_target_pairs={{0,32},{1,33},{2,34},{3,35},{4,36},{5,37},{6,38},{7,39},{8,40},{9,... | collective-permute-start | bytes 1179656 | tf_op jit(solution)/shard_map/ppermute | solution.py:187
  89.9 37.3 %all-to-all-start.1 = ((bf16[32,32,256]{2,1,0:T(8,128)(2,1)}), bf16[32,32,256]{2,1,0:T(8,128)(2,1)S(1)}, u32[]{:S(2)}, u32[]{:S(2)}) async-start(bf16[32,32,256]{2,1,0:T(8,128)(2,1)} %bitcast.35), calls=%async_computation.1 | async-start | bytes 1048576 | tf_op jit(solution)/shard_map/all_to_all | solution.py:240
  104.1 12.8 %collective-permute-start.11 = (bf16[384,128]{1,0:T(8,128)(2,1)S(1)}, bf16[384,128]{1,0:T(8,128)(2,1)S(1)}, u32[]{:S(2)}, u32[]{:S(2)}) collective-permute-start(bf16[384,128]{1,0:T(8,128)(2,1)S(1)} %get-tuple-element.20), channel_id=1, source_target_pairs={{0,192},{1,193},{2,194},{3,195},{4,196},{5,197},{6,198},{7,199},{8... | collective-permute-start | bytes 294920 | tf_op jit(solution)/shard_map/ppermute | solution.py:187
  105.2 17.5 %collective-permute-start.10 = (bf16[384,128]{1,0:T(8,128)(2,1)S(1)}, bf16[384,128]{1,0:T(8,128)(2,1)S(1)}, u32[]{:S(2)}, u32[]{:S(2)}) collective-permute-start(bf16[384,128]{1,0:T(8,128)(2,1)S(1)} %get-tuple-element.21), channel_id=1, source_target_pairs={{0,128},{1,129},{2,130},{3,131},{4,132},{5,133},{6,134},{7,135},{8... | collective-permute-start | bytes 294920 | tf_op jit(solution)/shard_map/ppermute | solution.py:187
  106.3 16.4 %collective-permute-start.9 = (bf16[384,128]{1,0:T(8,128)(2,1)S(1)}, bf16[384,128]{1,0:T(8,128)(2,1)S(1)}, u32[]{:S(2)}, u32[]{:S(2)}) collective-permute-start(bf16[384,128]{1,0:T(8,128)(2,1)S(1)} %get-tuple-element.19), channel_id=1, source_target_pairs={{0,64},{1,65},{2,66},{3,67},{4,68},{5,69},{6,70},{7,71},{8,72},{9,... | collective-permute-start | bytes 294920 | tf_op jit(solution)/shard_map/ppermute | solution.py:187
  (1 other events, 0.7 us)

commit v2 on v1

--- a/solution.py
+++ b/solution.py
@@ -22,22 +22,32 @@
 
 def conv_kernel(
     cols,
-    wf_ref, wb_ref, bias_ref, wout_ref,
-    own_ref, up_ref, dn_ref, lo_ref, hi_ref, cot_ref, cup_ref, cdn_ref,
-    score_ref, g_ref, glo_ref, ghi_ref,
+    core_ref, wout_ref, wf_ref, wb_ref, bias_ref,
+    own_ref, up_ref, dn_ref, far_ref, near_ref, cot_ref,
+    score_ref, g_ref, far_out, near_out,
     cs, rows, cotf, cots, gp, sc, gs,
 ):
+    first = core_ref[0] == 0
+
     for k in range(8):
-        ref, at = (up_ref, k) if k < 2 else (own_ref, k - 2) if k < 6 else (dn_ref, k - 6)
-        plane = ref[at].astype(F32)
-        cs[0, pl.ds(k, cols, stride=8), :] = lo_ref[k].astype(F32)
-        cs[1, pl.ds(k, cols, stride=8), :] = plane[:, :128]
-        cs[2, pl.ds(k, cols, stride=8), :] = plane[:, 128:]
-        cs[3, pl.ds(k, cols, stride=8), :] = hi_ref[k].astype(F32)
+        if 2 <= k < 6:
+            left = own_ref[pl.ds((k - 2) * cols, cols), pl.ds(0, 128)]
+            right = own_ref[pl.ds((k - 2) * cols, cols), pl.ds(128, 128)]
+        else:
+            ref, at = (up_ref, k) if k < 2 else (dn_ref, k - 6)
+            left = ref[pl.ds(at * cols, cols), :]
+            right = ref[pl.ds((at + 2) * cols, cols), :]
+        here = pl.ds(k * cols, cols)
+        far, near = far_ref[here, :].astype(F32), near_ref[here, :].astype(F32)
+        where = pl.ds(k, cols, stride=8)
+        cs[0, where, :] = jnp.where(first, far, near)
+        cs[1, where, :] = left.astype(F32)
+        cs[2, where, :] = right.astype(F32)
+        cs[3, where, :] = jnp.where(first, near, far)
     zeros = jnp.zeros((cols, 128), F32)
-    cotf[pl.ds(0, 2 * cols), :] = cup_ref[...].astype(F32)
+    cotf[pl.ds(0, 2 * cols), :] = up_ref[pl.ds(4 * cols, 2 * cols), :].astype(F32)
     cotf[pl.ds(2 * cols, 8 * cols), :] = cot_ref[...].astype(F32)
-    cotf[pl.ds(10 * cols, 2 * cols), :] = cdn_ref[...].astype(F32)
+    cotf[pl.ds(10 * cols, 2 * cols), :] = dn_ref[pl.ds(4 * cols, 2 * cols), :].astype(F32)
     for i in range(2):
         cots[i, pl.ds(0, cols, stride=8), :] = zeros
         cots[i, pl.ds(7, cols, stride=8), :] = zeros
@@ -61,7 +71,7 @@
             rows[pl.ds(pl.multiple_of((l + 1) * group, 16), group), pl.ds(i * 128, 128)] = jnp.concatenate(block, 0).astype(BF)
         return 0
 
-    lax.fori_loop(0, cols, spread, 0, unroll=4)
+    lax.fori_loop(0, cols, spread, 0, unroll=16)
 
     wf = wf_ref[...]
     wb = wb_ref[...]
@@ -88,7 +98,7 @@
         sc[1, pl.ds(at, 8), :] = total[:, 128:]
         return 0
 
-    lax.fori_loop(0, cols, forward, 0, unroll=4)
+    lax.fori_loop(0, cols, forward, 0, unroll=32)
 
     def backward(m, _):
         window = gp[pl.ds(pl.multiple_of(m * 128, 128), 256), :]
@@ -106,7 +116,7 @@
             gs[io, pl.ds(at, 8), :] = shift_lanes(part[0], -1) + part[1] + shift_lanes(part[2], 1)
         return 0
 
-    lax.fori_loop(0, cols // 2, backward, 0, unroll=4)
+    lax.fori_loop(0, cols // 2, backward, 0, unroll=16)
 
     for k in range(4):
         for i in range(2):
@@ -114,14 +124,14 @@
     score_ref[...] = cotf[pl.ds(0, 8 * cols), :].astype(BF)
     for k in range(4):
         here = pl.ds(k * cols, cols)
-        glo_ref[here, :] = gs[0, pl.ds(k, cols, stride=4), :].astype(BF)
-        g_ref[here, pl.ds(0, 128)] = gs[1, pl.ds(k, cols, stride=4), :]
-        g_ref[here, pl.ds(128, 128)] = gs[2, pl.ds(k, cols, stride=4), :]
-        ghi_ref[here, :] = gs[3, pl.ds(k, cols, stride=4), :].astype(BF)
-
-
-def conv(cols, weights, own, up, dn, lo, hi, cot, cup, cdn):
-    wf, wb, bias, w_out = weights
+        lo, mid_lo, mid_hi, hi = (gs[i, pl.ds(k, cols, stride=4), :] for i in range(4))
+        g_ref[here, pl.ds(0, 128)] = mid_lo
+        g_ref[here, pl.ds(128, 128)] = mid_hi
+        far_out[here, :] = jnp.where(first, lo, hi).astype(BF)
+        near_out[here, :] = jnp.where(first, hi, lo).astype(BF)
+
+
+def conv(cols, core, w_out, weights, own, up, dn, far, near, cot):
     vmem = pl.BlockSpec(memory_space=pltpu.VMEM)
     smem = pl.BlockSpec(memory_space=pltpu.SMEM)
     n = 4 * cols
@@ -133,7 +143,7 @@
             jax.ShapeDtypeStruct((n, 128), BF),
             jax.ShapeDtypeStruct((n, 128), BF),
         ),
-        in_specs=[vmem, vmem, vmem, smem] + [vmem] * 8,
+        in_specs=[smem, smem] + [vmem] * 9,
         out_specs=(vmem,) * 4,
         scratch_shapes=[
             pltpu.VMEM((4, 8 * cols, 128), F32),
@@ -146,7 +156,7 @@
         ],
         compiler_params=pltpu.CompilerParams(vmem_limit_bytes=40 * 2**20),
         cost_estimate=pl.CostEstimate(flops=4 * 10**9, transcendentals=10**7, bytes_accessed=4 * 10**6),
-    )(wf, wb, bias, w_out, own, up, dn, lo, hi, cot, cup, cdn)
+    )(core, w_out, *weights, own, up, dn, far, near, cot)
 
 
 def filters(w_src, b_src, w_tgt, b_tgt, first_row, total_rows):
@@ -183,102 +193,127 @@
     return wf, wb, bias
 
 
-def permuted(x, pairs):
-    return lax.ppermute(x, ("src", "tgt"), pairs)
+SRC = ("z", "core")
+TGT = ("y", "x", "zh")
+SIZES = {"z": 4, "core": 2, "y": 4, "x": 4, "zh": 2}
+
+
+def moved(x, move):
+    n_src, n_tgt = lax.axis_size(SRC), lax.axis_size(TGT)
+    pairs = []
+    for a in range(n_src):
+        for b in range(n_tgt):
+            c, d = move(a, b)
+            if 0 <= c < n_src and 0 <= d < n_tgt:
+                pairs.append((a * n_tgt + b, c * n_tgt + d))
+    return lax.ppermute(x, SRC + TGT, pairs)
+
+
+def far_row(a, b):
+    return (a + 1 if a % 2 else a - 1, b)
+
+
+def near_row(a, b):
+    return (a ^ 1, b)
 
 
 def body(src_feat, tgt_feat, w_src, b_src, w_tgt, b_tgt, w_out, cotangent):
     rows_k, cols, rows_i, cols_j = cotangent.shape
     chans = tgt_feat.shape[2]
     scale = chans ** (-0.5)
-    n_src, n_tgt = lax.axis_size("src"), lax.axis_size("tgt")
-    s, t = lax.axis_index("src"), lax.axis_index("tgt")
+    n_src, n_tgt = lax.axis_size(SRC), lax.axis_size(TGT)
+    t, z, core, zh = (lax.axis_index(a) for a in (TGT, "z", "core", "zh"))
+    first = core == 0
     block = chans // n_tgt
-
-    def joint(move):
-        out = []
-        for a in range(n_src):
-            for b in range(n_tgt):
-                c, d = move(a, b)
-                if 0 <= c < n_src and 0 <= d < n_tgt:
-                    out.append((a * n_tgt + b, c * n_tgt + d))
-        return out
-
-    tgt_up = joint(lambda a, b: (a, b + 1))
-    tgt_dn = joint(lambda a, b: (a, b - 1))
-    src_up = joint(lambda a, b: (a + 1, b))
-    src_dn = joint(lambda a, b: (a - 1, b))
+    pixels = rows_i * cols_j
 
     weights = filters(w_src, b_src, w_tgt, b_tgt, t * rows_k, rows_k * n_tgt)
     tgt_flat = tgt_feat.reshape(rows_k * cols, chans)
 
-    piece = src_feat.reshape(rows_i * cols_j, block).T
+    piece = src_feat.reshape(pixels, block).T
     src_t = lax.all_to_all(
-        jnp.broadcast_to(piece[None], (n_tgt, block, rows_i * cols_j)), "tgt", 0, 0, tiled=True
-    ).reshape(chans, rows_i * cols_j)
+        jnp.broadcast_to(piece[None], (n_tgt, block, pixels)), TGT, 0, 0, tiled=True
+    ).reshape(chans, pixels)
 
     raw = jnp.dot(tgt_flat, src_t, preferred_element_type=F32)
-    own = (raw * scale).astype(BF).reshape(rows_k, cols, rows_i * cols_j)
-    cot = cotangent.reshape(rows_k, cols * rows_i, cols_j)
-    up = permuted(own[rows_k - 2:], tgt_up)
-    dn = permuted(own[:2], tgt_dn)
-    cup = permuted(cot[rows_k - 1], tgt_up)
-    cdn = permuted(cot[0], tgt_dn)
-    tall = jnp.concatenate([up, own, dn], 0)
-    lo = permuted(tall[:, :, cols_j:], src_up)
-    hi = permuted(tall[:, :, :cols_j], src_dn)
-
-    score, g_own, g_lo, g_hi = conv(
-        cols, (*weights, w_out), own, up, dn, lo, hi,
-        cot.reshape(rows_k * cols * rows_i, cols_j), cup, cdn,
-    )
-    from_hi = permuted(g_lo, src_dn)
-    from_lo = permuted(g_hi, src_up)
-    g = (g_own + jnp.concatenate([from_lo, from_hi], 1).astype(F32)).astype(BF)
-
-    part = lax.dot_general(tgt_flat, g, (((0,), (0,)), ((), ())), preferred_element_type=F32) * scale
-    parts = lax.all_to_all(
-        part.astype(BF).reshape(n_tgt, block, rows_i * cols_j), "tgt", 0, 0, tiled=True
-    )
-    grad_src = jnp.sum(parts.astype(F32), 0).reshape(block, rows_i, cols_j)
-
-    z, core = s // 2, s % 2
-    cut = src_t.reshape(n_src, chans // n_src, rows_i * cols_j)
+    own = (raw * scale).astype(BF)
+    cot = cotangent.reshape(rows_k * cols * rows_i, cols_j)
+
+    def edge(k, cot_k):
+        part = own[k * cols:(k + 2) * cols]
+        line = cot[cot_k * cols * rows_i:(cot_k + 1) * cols * rows_i]
+        return jnp.concatenate([part[:, :cols_j], part[:, cols_j:], line], 0)
+
+    up = moved(edge(rows_k - 2, rows_k - 1), lambda a, b: (a, b + 1))
+    dn = moved(edge(0, 0), lambda a, b: (a, b - 1))
+    two = 2 * cols
+    low = jnp.concatenate([up[:two], own[:, :cols_j], dn[:two]], 0)
+    high = jnp.concatenate([up[two:2 * two], own[:, cols_j:], dn[two:2 * two]], 0)
+    near = moved(jnp.where(first, high, low), near_row)
+    far = moved(jnp.where(first, low, high), far_row)
+
+    score, g_own, to_far, to_near = conv(
+        cols, core.astype(jnp.int32)[None], w_out, weights, own, up, dn, far, near, cot
+    )
+    from_near = moved(to_near, near_row)
+    from_far = moved(to_far, far_row)
+    g = jnp.concatenate(
+        [
+            g_own[:, :cols_j] + jnp.where(first, from_far, from_near).astype(F32),
+            g_own[:, cols_j:] + jnp.where(first, from_near, from_far).astype(F32),
+        ],
+        1,
+    ).astype(BF)
+
+    cut = src_t.reshape(n_src, chans // n_src, pixels)
     hops = n_src // 2
 
     def blocks(side):
-        return jnp.concatenate([lax.dynamic_index_in_dim(cut, (z ^ m) * 2 + side, 0, False) for m in range(hops)], 0)
+        return jnp.concatenate(
+            [lax.dynamic_index_in_dim(cut, (z ^ m) * 2 + side, 0, False) for m in range(hops)], 0
+        )
 
     over = (((1,), (1,)), ((), ()))
+    other = lax.dot_general(g, blocks(1 - core), over, preferred_element_type=F32) * scale
+    got = moved(other.astype(BF), near_row)
     mine = lax.dot_general(g, blocks(core), over, preferred_element_type=F32) * scale
-    other = lax.dot_general(g, blocks(1 - core), over, preferred_element_type=F32) * scale
-    got = permuted(other.astype(BF), joint(lambda a, b: (a ^ 1, b)))
     both = mine + got.astype(F32)
     width = chans // n_src
     total = both[:, :width]
     for m in range(1, hops):
-        total = total + permuted(
-            both[:, m * width:(m + 1) * width].astype(BF), joint(lambda a, b, m=m: (a ^ (2 * m), b))
+        total = total + moved(
+            both[:, m * width:(m + 1) * width].astype(BF), lambda a, b, m=m: (a ^ (2 * m), b)
         ).astype(F32)
     grad_tgt = total.reshape(rows_k, cols, width)
-    return (score.reshape(cotangent.shape), grad_src, grad_tgt)
+
+    part = lax.dot_general(tgt_flat, g, (((0,), (0,)), ((), ())), preferred_element_type=F32) * scale
+    plane = n_tgt // 2
+    parts = lax.all_to_all(
+        part.astype(BF).reshape(plane, 2 * block, pixels), ("y", "x"), 0, 0, tiled=True
+    )
+    halves = jnp.sum(parts.astype(F32), 0).reshape(2, block, pixels)
+    keep = lax.dynamic_index_in_dim(halves, zh, 0, False)
+    send = lax.dynamic_index_in_dim(halves, 1 - zh, 0, False)
+    grad_src = keep + moved(send.astype(BF), lambda a, b: (a, b ^ 1)).astype(F32)
+    return (score.reshape(cotangent.shape), grad_src.reshape(block, rows_i, cols_j), grad_tgt)
 
 
 def solution(mesh):
+    fine = jax.sharding.Mesh(mesh.devices.reshape(tuple(SIZES.values())), tuple(SIZES))
     placed = (
-        P("src", None, "tgt"),
-        P("tgt", None, None),
-        P(),
-        P(),
-        P(),
-        P(),
-        P(),
-        P("tgt", None, "src", None),
+        P(SRC, None, TGT),
+        P(TGT, None, None),
+        P(),
+        P(),
+        P(),
+        P(),
+        P(),
+        P(TGT, None, SRC, None),
     )
     return jax.shard_map(
         body,
-        mesh=mesh,
+        mesh=fine,
         in_specs=placed,
-        out_specs=(P("tgt", None, "src", None), P("tgt", "src", None), P("tgt", None, "src")),
+        out_specs=(P(TGT, None, SRC, None), P(TGT, SRC, None), P(TGT, None, SRC)),
         check_vma=False,
     )

time: 129 us -> 107 us (0.83)
  starting transfers between devices: 53.5 us -> 37.7 us
  Pallas kernels: 14.3 us -> 8.58 us
  waiting for transfers between devices: 43 us -> 45.1 us
  local copies, waits for them, and re-layouts: 11.3 us -> 9.68 us
    ppermute x12 -> x11, starting transfers between devices: 26.5 us -> 17.6 us  [moved(): return lax.ppermute(x, SRC + TGT, pairs)]
    all_to_all x2, waiting for transfers between devices: 15 us -> 23.1 us  [the longest x1 14.8 us: body(): lax.all_to_all(jnp.broadcast_to(piece[None], (n_tgt, block, pixels)), TGT...]
    all_to_all x2, starting transfers between devices: 27 us -> 20.1 us  [the longest x1 13.2 us: body(): lax.all_to_all(jnp.broadcast_to(piece[None], (n_tgt, block, pixels)), TGT...]
    ppermute x12 -> x11, waiting for transfers between devices: 27.9 us -> 22 us  [moved(): return lax.ppermute(x, SRC + TGT, pairs)]
    pallas_call x1, Pallas kernels: 14.3 us -> 8.58 us  [conv(): pl.pallas_call(functools.partial(conv_kernel, cols), out_shape=(jax.Shape...]
  transfers between devices with their start and end apart: 14 -> 13, of which waited for: 8 -> 6; matrix products, arithmetic and copies ran while one was open for 8% -> 7% of each run, Pallas kernels for 0% -> 0%
where the time goes in v2:
time: 107 us; the launch traced here: 106 us
  waiting for transfers between devices  45.1 us (42%)
  starting transfers between devices  37.7 us (35%)
  local copies, waits for them, and re-layouts  9.68 us (9%)
  Pallas kernels  8.58 us (8%)
  matrix products  3.1 us (3%)
  between operations  1.07 us (1%)
    ppermute x11, waiting for transfers between devices, moved(): return lax.ppermute(x, SRC + TGT, pairs)  22 us
    ppermute x11, starting transfers between devices, moved(): return lax.ppermute(x, SRC + TGT, pairs)  17.6 us
    all_to_all x1, waiting for transfers between devices, body(): lax.all_to_all(jnp.broadcast_to(piece[None], (n_tgt, block, pixels)), TGT...  14.8 us
    all_to_all x1, starting transfers between devices, body(): lax.all_to_all(jnp.broadcast_to(piece[None], (n_tgt, block, pixels)), TGT...  13.2 us
    pallas_call x1, Pallas kernels, conv(): pl.pallas_call(functools.partial(conv_kernel, cols), out_shape=(jax.Shape...  8.58 us
    all_to_all x1, waiting for transfers between devices, body(): lax.all_to_all(part.astype(BF).reshape(plane, 2 * block, pixels), ('y', '...  8.24 us
    all_to_all x1, starting transfers between devices, body(): lax.all_to_all(part.astype(BF).reshape(plane, 2 * block, pixels), ('y', '...  6.94 us
    unnamed x22, local copies, waits for them, and re-layouts  3.08 us
  transfers between devices with their start and end apart: 13, of which 6 were waited for; matrix products, arithmetic and copies ran while one was open for 7% of the time, Pallas kernels for 0%

profile of v2, /device:TPU:32, one launch (start us, length us, event | category | flops | bytes accessed | tf_op | source)
XLA Modules:
  0.0 106.1 jit_solution(17739361549387471400)
XLA Ops:
  0.6 0.8 bitcast_bitcast_fusion
  1.4 0.9 broadcast_in_dim.20
  2.3 13.2 %all-to-all-start = ((bf16[32,32,256]{2,1,0:T(8,128)(2,1)}), bf16[32,32,256]{2,1,0:T(8,128)(2,1)S(1)}, u32[]{:S(2)}, u32[]{:S(2)}) async-start(bf16[32,32,256]{2,1,0:T(8,128)(2,1)} %broadcast_in_dim.20), calls=%async_computation | async-start | bytes 1048576 | tf_op jit(solution)/shard_map/all_to_all | solution.py:234
  17.4 1.5 %copy.22 = bf16[8,8,3,10,8]{1,0,4,3,2:T(8,128)(2,1)S(1)} copy(bf16[8,8,3,10,8]{3,4,1,2,0:T(8,128)(2,1)S(1)} %fusion.6) | data formatting | bytes 61440 | tf_op jit(solution)/shard_map/convert_element_type | solution.py:171
  19.5 0.8 convert_element_type.71.wb_ref
  22.5 14.8 %all-to-all-done = bf16[32,32,256]{2,1,0:T(8,128)(2,1)S(1)} async-done(((bf16[32,32,256]{2,1,0:T(8,128)(2,1)}), bf16[32,32,256]{2,1,0:T(8,128)(2,1)S(1)}, u32[]{:S(2)}, u32[]{:S(2)}) %all-to-all-start) | async-done | bytes 524320 | tf_op jit(solution)/shard_map/all_to_all | solution.py:234
  37.8 2.4 %collective-permute-start = (bf16[576,128]{1,0:T(8,128)(2,1)S(1)}, bf16[576,128]{1,0:T(8,128)(2,1)S(1)}, u32[]{:S(2)}, u32[]{:S(2)}) collective-permute-start(bf16[576,128]{1,0:T(8,128)(2,1)S(1)} %pad_maximum_fusion.3), channel_id=1, source_target_pairs={{0,1},{1,2},{2,3},{3,4},{4,5},{5,6},{6,7},{7,8},{8,9},{9,10},{10,1... | collective-permute-start | bytes 442376 | tf_op jit(solution)/shard_map/ppermute | solution.py:209
  40.2 1.3 %collective-permute-start.1 = (bf16[576,128]{1,0:T(8,128)(2,1)S(1)}, bf16[576,128]{1,0:T(8,128)(2,1)S(1)}, u32[]{:S(2)}, u32[]{:S(2)}) collective-permute-start(bf16[576,128]{1,0:T(8,128)(2,1)S(1)} %pad_maximum_fusion.4), channel_id=1, source_target_pairs={{1,0},{2,1},{3,2},{4,3},{5,4},{6,5},{7,6},{8,7},{9,8},{10,9},{11,1... | collective-permute-start | bytes 442376 | tf_op jit(solution)/shard_map/ppermute | solution.py:209
  41.5 12.6 %collective-permute-done.1.dn_ref = bf16[576,128]{1,0:T(8,128)(2,1)S(1)} collective-permute-done((bf16[576,128]{1,0:T(8,128)(2,1)S(1)}, bf16[576,128]{1,0:T(8,128)(2,1)S(1)}, u32[]{:S(2)}, u32[]{:S(2)}) %collective-permute-start.1) | collective-permute-done | bytes 147488 | tf_op jit(solution)/shard_map/ppermute | solution.py:209
  54.3 1.9 %collective-permute-start.2 = (bf16[768,128]{1,0:T(8,128)(2,1)S(1)}, bf16[768,128]{1,0:T(8,128)(2,1)S(1)}, u32[]{:S(2)}, u32[]{:S(2)}) collective-permute-start(bf16[768,128]{1,0:T(8,128)(2,1)S(1)} %get-tuple-element.25), channel_id=1, source_target_pairs={{32,64},{33,65},{34,66},{35,67},{36,68},{37,69},{38,70},{39,71},{4... | collective-permute-start | bytes 589832 | tf_op jit(solution)/shard_map/ppermute | solution.py:209
  56.2 1.2 %collective-permute-start.3 = (bf16[768,128]{1,0:T(8,128)(2,1)S(1)}, bf16[768,128]{1,0:T(8,128)(2,1)S(1)}, u32[]{:S(2)}, u32[]{:S(2)}) collective-permute-start(bf16[768,128]{1,0:T(8,128)(2,1)S(1)} %get-tuple-element.24), channel_id=1, source_target_pairs={{0,32},{1,33},{2,34},{3,35},{4,36},{5,37},{6,38},{7,39},{8,40},{9,... | collective-permute-start | bytes 589832 | tf_op jit(solution)/shard_map/ppermute | solution.py:209
  57.8 3.6 %collective-permute-done.2.far_ref = bf16[768,128]{1,0:T(8,128)(2,1)S(1)} collective-permute-done((bf16[768,128]{1,0:T(8,128)(2,1)S(1)}, bf16[768,128]{1,0:T(8,128)(2,1)S(1)}, u32[]{:S(2)}, u32[]{:S(2)}) %collective-permute-start.2) | collective-permute-done | bytes 196640 | tf_op jit(solution)/shard_map/ppermute | solution.py:209
  62.1 8.6 %shard_map.139 = (bf16[768,128]{1,0:T(8,128)(2,1)}, f32[384,256]{1,0:T(8,128)S(1)}, bf16[384,128]{1,0:T(8,128)(2,1)S(1)}, bf16[384,128]{1,0:T(8,128)(2,1)S(1)}) custom-call(s32[1]{0:T(128)} %bitcast.core_ref, f32[8]{0:T(128)S(1)} %copy-done.2, bf16[64,240]{1,0:T(8,128)(2,1)S(1)} %copy.26.wf_ref, bf16[72,256]{1,0:T(8,128)(2,1)S(1)} %convert_element_type.71.wb_ref, ...), custom_call_target="tpu_custom_call" | custom-call | flops 4000000000 | bytes 4000000 | tf_op jit(solution)/shard_map/pallas_call | solution.py:138
  70.6 1.9 %collective-permute-start.4 = (bf16[384,128]{1,0:T(8,128)(2,1)S(1)}, bf16[384,128]{1,0:T(8,128)(2,1)S(1)}, u32[]{:S(2)}, u32[]{:S(2)}) collective-permute-start(bf16[384,128]{1,0:T(8,128)(2,1)S(1)} %get-tuple-element.9), channel_id=1, source_target_pairs={{32,64},{33,65},{34,66},{35,67},{36,68},{37,69},{38,70},{39,71},{4... | collective-permute-start | bytes 294920 | tf_op jit(solution)/shard_map/ppermute | solution.py:209
  72.6 1.2 %collective-permute-start.5 = (bf16[384,128]{1,0:T(8,128)(2,1)S(1)}, bf16[384,128]{1,0:T(8,128)(2,1)S(1)}, u32[]{:S(2)}, u32[]{:S(2)}) collective-permute-start(bf16[384,128]{1,0:T(8,128)(2,1)S(1)} %get-tuple-element.10), channel_id=1, source_target_pairs={{0,32},{1,33},{2,34},{3,35},{4,36},{5,37},{6,38},{7,39},{8,40},{9,... | collective-permute-start | bytes 294920 | tf_op jit(solution)/shard_map/ppermute | solution.py:209
  73.8 2.8 %collective-permute-done.4 = bf16[384,128]{1,0:T(8,128)(2,1)S(1)} collective-permute-done((bf16[384,128]{1,0:T(8,128)(2,1)S(1)}, bf16[384,128]{1,0:T(8,128)(2,1)S(1)}, u32[]{:S(2)}, u32[]{:S(2)}) %collective-permute-start.4) | collective-permute-done | bytes 98336 | tf_op jit(solution)/shard_map/ppermute | solution.py:209
  77.5 1.0 copy.27
  78.5 6.9 %all-to-all-start.1 = ((bf16[16,64,256]{2,1,0:T(8,128)(2,1)}), bf16[16,64,256]{2,1,0:T(8,128)(2,1)S(1)}, u32[]{:S(2)}, u32[]{:S(2)}) async-start(bf16[16,64,256]{2,1,0:T(8,128)(2,1)} %bitcast.33), calls=%async_computation.1 | async-start | bytes 1048576 | tf_op jit(solution)/shard_map/all_to_all | solution.py:291
  85.8 1.1 collective-permute-start.10
  86.9 1.8 %collective-permute-start.9 = (bf16[384,128]{1,0:T(8,128)(2,1)S(1)}, bf16[384,128]{1,0:T(8,128)(2,1)S(1)}, u32[]{:S(2)}, u32[]{:S(2)}) collective-permute-start(bf16[384,128]{1,0:T(8,128)(2,1)S(1)} %get-tuple-element.23), channel_id=1, source_target_pairs={{0,128},{1,129},{2,130},{3,131},{4,132},{5,133},{6,134},{7,135},{8... | collective-permute-start | bytes 294920 | tf_op jit(solution)/shard_map/ppermute | solution.py:209
  88.7 0.7 collective-permute-start.8
  89.4 8.2 %all-to-all-done.1 = bf16[16,64,256]{2,1,0:T(8,128)(2,1)S(1)} async-done(((bf16[16,64,256]{2,1,0:T(8,128)(2,1)}), bf16[16,64,256]{2,1,0:T(8,128)(2,1)S(1)}, u32[]{:S(2)}, u32[]{:S(2)}) %all-to-all-start.1) | async-done | bytes 524320 | tf_op jit(solution)/shard_map/all_to_all | solution.py:291
  97.8 4.0 %collective-permute-start.6 = (bf16[32,256]{1,0:T(8,128)(2,1)S(1)}, bf16[32,256]{1,0:T(8,128)(2,1)S(1)}, u32[]{:S(2)}, u32[]{:S(2)}) collective-permute-start(bf16[32,256]{1,0:T(8,128)(2,1)S(1)} %fusion.30), channel_id=1, source_target_pairs={{0,1},{1,0},{2,3},{3,2},{4,5},{5,4},{6,7},{7,6},{8,9},{9,8},{10,11... | collective-permute-start | bytes 49160 | tf_op jit(solution)/shard_map/ppermute | solution.py:209
  102.5 3.0 %collective-permute-done.6 = bf16[32,256]{1,0:T(8,128)(2,1)S(1)} collective-permute-done((bf16[32,256]{1,0:T(8,128)(2,1)S(1)}, bf16[32,256]{1,0:T(8,128)(2,1)S(1)}, u32[]{:S(2)}, u32[]{:S(2)}) %collective-permute-start.6) | collective-permute-done | bytes 16416 | tf_op jit(solution)/shard_map/ppermute | solution.py:209
  (64 shorter events, 8.9 us)
Async XLA Ops:
  0.6 36.7 %copy-start = (bf16[4,96,1024]{2,1,0:T(8,128)(2,1)S(1)}, bf16[4,96,1024]{2,1,0:T(8,128)(2,1)}, u32[]{:S(2)}) copy-start(bf16[4,96,1024]{2,1,0:T(8,128)(2,1)} %param.13) | copy-start | bytes 2359300
  2.3 13.2 %copy-start.3 = (bf16[8,8,3,3]{1,0,3,2:T(8,128)(2,1)S(1)}, bf16[8,8,3,3]{1,0,3,2:T(8,128)(2,1)}, u32[]{:S(2)}) copy-start(bf16[8,8,3,3]{1,0,3,2:T(8,128)(2,1)} %param.16) | copy-start | bytes 3460
  2.3 13.2 %copy-start.6 = (bf16[8,3,3]{0,2,1:T(4,128)(2,1)S(1)}, bf16[8,3,3]{0,2,1:T(4,128)(2,1)}, u32[]{:S(2)}) copy-start(bf16[8,3,3]{0,2,1:T(4,128)(2,1)} %param.14) | copy-start | bytes 436
  2.3 35.0 %all-to-all-start = ((bf16[32,32,256]{2,1,0:T(8,128)(2,1)}), bf16[32,32,256]{2,1,0:T(8,128)(2,1)S(1)}, u32[]{:S(2)}, u32[]{:S(2)}) async-start(bf16[32,32,256]{2,1,0:T(8,128)(2,1)} %broadcast_in_dim.20), calls=%async_computation | async-start | bytes 1048576 | tf_op jit(solution)/shard_map/all_to_all | solution.py:234
  15.5 0.9 copy-start.10
  16.4 0.7 copy-start.5
  19.4 2.9 %copy-start.1 = (bf16[4,96,2,128]{3,2,1,0:T(2,128)(2,1)S(1)}, bf16[4,96,2,128]{3,2,1,0:T(2,128)(2,1)}, u32[]{:S(2)}) copy-start(bf16[4,96,2,128]{3,2,1,0:T(2,128)(2,1)} %param.19) | copy-start | bytes 589828
  20.2 0.7 copy-start.4
  20.9 0.7 copy-start.8
  21.6 0.7 copy-start.7
  37.8 16.4 %collective-permute-start = (bf16[576,128]{1,0:T(8,128)(2,1)S(1)}, bf16[576,128]{1,0:T(8,128)(2,1)S(1)}, u32[]{:S(2)}, u32[]{:S(2)}) collective-permute-start(bf16[576,128]{1,0:T(8,128)(2,1)S(1)} %pad_maximum_fusion.3), channel_id=1, source_target_pairs={{0,1},{1,2},{2,3},{3,4},{4,5},{5,6},{6,7},{7,8},{8,9},{9,10},{10,1... | collective-permute-start | bytes 442376 | tf_op jit(solution)/shard_map/ppermute | solution.py:209
  40.2 14.0 %collective-permute-start.1 = (bf16[576,128]{1,0:T(8,128)(2,1)S(1)}, bf16[576,128]{1,0:T(8,128)(2,1)S(1)}, u32[]{:S(2)}, u32[]{:S(2)}) collective-permute-start(bf16[576,128]{1,0:T(8,128)(2,1)S(1)} %pad_maximum_fusion.4), channel_id=1, source_target_pairs={{1,0},{2,1},{3,2},{4,3},{5,4},{6,5},{7,6},{8,7},{9,8},{10,9},{11,1... | collective-permute-start | bytes 442376 | tf_op jit(solution)/shard_map/ppermute | solution.py:209
  54.3 3.1 %copy-start.9 = (f32[8]{0:T(128)S(1)}, f32[8]{0:T(128)}, u32[]{:S(2)}) copy-start(f32[8]{0:T(128)} %param.17) | copy-start | bytes 100
  54.3 7.0 %collective-permute-start.2 = (bf16[768,128]{1,0:T(8,128)(2,1)S(1)}, bf16[768,128]{1,0:T(8,128)(2,1)S(1)}, u32[]{:S(2)}, u32[]{:S(2)}) collective-permute-start(bf16[768,128]{1,0:T(8,128)(2,1)S(1)} %get-tuple-element.25), channel_id=1, source_target_pairs={{32,64},{33,65},{34,66},{35,67},{36,68},{37,69},{38,70},{39,71},{4... | collective-permute-start | bytes 589832 | tf_op jit(solution)/shard_map/ppermute | solution.py:209
  56.2 5.1 %collective-permute-start.3 = (bf16[768,128]{1,0:T(8,128)(2,1)S(1)}, bf16[768,128]{1,0:T(8,128)(2,1)S(1)}, u32[]{:S(2)}, u32[]{:S(2)}) collective-permute-start(bf16[768,128]{1,0:T(8,128)(2,1)S(1)} %get-tuple-element.24), channel_id=1, source_target_pairs={{0,32},{1,33},{2,34},{3,35},{4,36},{5,37},{6,38},{7,39},{8,40},{9,... | collective-permute-start | bytes 589832 | tf_op jit(solution)/shard_map/ppermute | solution.py:209
  61.4 0.7 copy-start.2
  70.6 5.9 %collective-permute-start.4 = (bf16[384,128]{1,0:T(8,128)(2,1)S(1)}, bf16[384,128]{1,0:T(8,128)(2,1)S(1)}, u32[]{:S(2)}, u32[]{:S(2)}) collective-permute-start(bf16[384,128]{1,0:T(8,128)(2,1)S(1)} %get-tuple-element.9), channel_id=1, source_target_pairs={{32,64},{33,65},{34,66},{35,67},{36,68},{37,69},{38,70},{39,71},{4... | collective-permute-start | bytes 294920 | tf_op jit(solution)/shard_map/ppermute | solution.py:209
  72.6 4.0 %collective-permute-start.5 = (bf16[384,128]{1,0:T(8,128)(2,1)S(1)}, bf16[384,128]{1,0:T(8,128)(2,1)S(1)}, u32[]{:S(2)}, u32[]{:S(2)}) collective-permute-start(bf16[384,128]{1,0:T(8,128)(2,1)S(1)} %get-tuple-element.10), channel_id=1, source_target_pairs={{0,32},{1,33},{2,34},{3,35},{4,36},{5,37},{6,38},{7,39},{8,40},{9,... | collective-permute-start | bytes 294920 | tf_op jit(solution)/shard_map/ppermute | solution.py:209
  76.9 8.5 %collective-permute-start.7 = (bf16[384,512]{1,0:T(8,128)(2,1)S(1)}, bf16[384,512]{1,0:T(8,128)(2,1)S(1)}, u32[]{:S(2)}, u32[]{:S(2)}) collective-permute-start(bf16[384,512]{1,0:T(8,128)(2,1)S(1)} %fusion.2), channel_id=1, source_target_pairs={{0,32},{1,33},{2,34},{3,35},{4,36},{5,37},{6,38},{7,39},{8,40},{9,... | collective-permute-start | bytes 1179656 | tf_op jit(solution)/shard_map/ppermute | solution.py:209
  78.5 19.1 %all-to-all-start.1 = ((bf16[16,64,256]{2,1,0:T(8,128)(2,1)}), bf16[16,64,256]{2,1,0:T(8,128)(2,1)S(1)}, u32[]{:S(2)}, u32[]{:S(2)}) async-start(bf16[16,64,256]{2,1,0:T(8,128)(2,1)} %bitcast.33), calls=%async_computation.1 | async-start | bytes 1048576 | tf_op jit(solution)/shard_map/all_to_all | solution.py:291
  85.8 15.9 %collective-permute-start.10 = (bf16[384,128]{1,0:T(8,128)(2,1)S(1)}, bf16[384,128]{1,0:T(8,128)(2,1)S(1)}, u32[]{:S(2)}, u32[]{:S(2)}) collective-permute-start(bf16[384,128]{1,0:T(8,128)(2,1)S(1)} %get-tuple-element.22), channel_id=1, source_target_pairs={{0,192},{1,193},{2,194},{3,195},{4,196},{5,197},{6,198},{7,199},{8... | collective-permute-start | bytes 294920 | tf_op jit(solution)/shard_map/ppermute | solution.py:209
  86.9 14.9 %collective-permute-start.9 = (bf16[384,128]{1,0:T(8,128)(2,1)S(1)}, bf16[384,128]{1,0:T(8,128)(2,1)S(1)}, u32[]{:S(2)}, u32[]{:S(2)}) collective-permute-start(bf16[384,128]{1,0:T(8,128)(2,1)S(1)} %get-tuple-element.23), channel_id=1, source_target_pairs={{0,128},{1,129},{2,130},{3,131},{4,132},{5,133},{6,134},{7,135},{8... | collective-permute-start | bytes 294920 | tf_op jit(solution)/shard_map/ppermute | solution.py:209
  88.7 13.1 %collective-permute-start.8 = (bf16[384,128]{1,0:T(8,128)(2,1)S(1)}, bf16[384,128]{1,0:T(8,128)(2,1)S(1)}, u32[]{:S(2)}, u32[]{:S(2)}) collective-permute-start(bf16[384,128]{1,0:T(8,128)(2,1)S(1)} %get-tuple-element.21), channel_id=1, source_target_pairs={{0,64},{1,65},{2,66},{3,67},{4,68},{5,69},{6,70},{7,71},{8,72},{9,... | collective-permute-start | bytes 294920 | tf_op jit(solution)/shard_map/ppermute | solution.py:209
  97.8 7.7 %collective-permute-start.6 = (bf16[32,256]{1,0:T(8,128)(2,1)S(1)}, bf16[32,256]{1,0:T(8,128)(2,1)S(1)}, u32[]{:S(2)}, u32[]{:S(2)}) collective-permute-start(bf16[32,256]{1,0:T(8,128)(2,1)S(1)} %fusion.30), channel_id=1, source_target_pairs={{0,1},{1,0},{2,3},{3,2},{4,5},{5,4},{6,7},{7,6},{8,9},{9,8},{10,11... | collective-permute-start | bytes 49160 | tf_op jit(solution)/shard_map/ppermute | solution.py:209

commit v3 on v2

--- a/solution.py
+++ b/solution.py
@@ -22,32 +22,47 @@
 
 def conv_kernel(
     cols,
-    core_ref, wout_ref, wf_ref, wb_ref, bias_ref,
-    own_ref, up_ref, dn_ref, far_ref, near_ref, cot_ref,
-    score_ref, g_ref, far_out, near_out,
-    cs, rows, cotf, cots, gp, sc, gs,
+    scale, spot_ref, wf_ref, wb_ref, bias_ref, tgt_ref, src_ref, far_ref, near_ref, up_ref, dn_ref, cot_ref,
+    *more,
 ):
-    first = core_ref[0] == 0
-
-    for k in range(8):
-        if 2 <= k < 6:
-            left = own_ref[pl.ds((k - 2) * cols, cols), pl.ds(0, 128)]
-            right = own_ref[pl.ds((k - 2) * cols, cols), pl.ds(128, 128)]
-        else:
-            ref, at = (up_ref, k) if k < 2 else (dn_ref, k - 6)
-            left = ref[pl.ds(at * cols, cols), :]
-            right = ref[pl.ds((at + 2) * cols, cols), :]
-        here = pl.ds(k * cols, cols)
-        far, near = far_ref[here, :].astype(F32), near_ref[here, :].astype(F32)
-        where = pl.ds(k, cols, stride=8)
-        cs[0, where, :] = jnp.where(first, far, near)
-        cs[1, where, :] = left.astype(F32)
-        cs[2, where, :] = right.astype(F32)
-        cs[3, where, :] = jnp.where(first, near, far)
+    n_more = len(more) - 11
+    halo_refs = more[:n_more]
+    score_ref, g_ref, far_out, near_out, cs, rows, cotf, cots, gp, sc, gs = more[n_more:]
+    hop, core = spot_ref[0], spot_ref[1]
+    first = core == 0
+
+    def put(part, at, ks):
+        part = (part * scale).astype(BF).astype(F32)
+        for n, k in enumerate(ks):
+            cs[at, pl.ds(k, cols, stride=8), :] = part[n * cols:(n + 1) * cols]
+
+    def fill(product, ks):
+        far, near = product(far_ref), product(near_ref)
+        put(jnp.where(first, far, near), 0, ks)
+        put(jnp.where(first, near, far), 3, ks)
+        mid = product(src_ref)
+        put(mid[:, :128], 1, ks)
+        put(mid[:, 128:], 2, ks)
+
+    def over_all(ref):
+        return jnp.dot(tgt_ref[...], ref[...], preferred_element_type=F32)
+
+    def over_pieces(ref):
+        total = None
+        for n, piece in enumerate(halo_refs):
+            block = (hop ^ (n // 2)) * 2 + (core ^ (n % 2))
+            part = jnp.dot(
+                piece[...], ref[pl.ds(pl.multiple_of(block * 128, 128), 128), :], preferred_element_type=F32
+            )
+            total = part if total is None else total + part
+        return total
+
+    fill(over_all, (2, 3, 4, 5))
+    fill(over_pieces, (0, 1, 6, 7))
     zeros = jnp.zeros((cols, 128), F32)
-    cotf[pl.ds(0, 2 * cols), :] = up_ref[pl.ds(4 * cols, 2 * cols), :].astype(F32)
+    cotf[pl.ds(0, 2 * cols), :] = up_ref[pl.ds(2 * cols, 2 * cols), :].astype(F32)
     cotf[pl.ds(2 * cols, 8 * cols), :] = cot_ref[...].astype(F32)
-    cotf[pl.ds(10 * cols, 2 * cols), :] = dn_ref[pl.ds(4 * cols, 2 * cols), :].astype(F32)
+    cotf[pl.ds(10 * cols, 2 * cols), :] = dn_ref[pl.ds(2 * cols, 2 * cols), :].astype(F32)
     for i in range(2):
         cots[i, pl.ds(0, cols, stride=8), :] = zeros
         cots[i, pl.ds(7, cols, stride=8), :] = zeros
@@ -71,7 +86,7 @@
             rows[pl.ds(pl.multiple_of((l + 1) * group, 16), group), pl.ds(i * 128, 128)] = jnp.concatenate(block, 0).astype(BF)
         return 0
 
-    lax.fori_loop(0, cols, spread, 0, unroll=16)
+    lax.fori_loop(0, cols, spread, 0, unroll=48)
 
     wf = wf_ref[...]
     wb = wb_ref[...]
@@ -90,7 +105,7 @@
         total = jnp.zeros((8, 256), F32)
         out = []
         for o in range(8):
-            w = wout_ref[o]
+            w = bias_ref[pl.ds(192 + o * 8, 8), :]
             total = total + w * s[o * 8:o * 8 + 8]
             out.append(g[o * 8:o * 8 + 8] * (cot * (0.5 * w)))
         gp[pl.ds(pl.multiple_of((l + 1) * 64, 64), 64), :] = jnp.concatenate(out, 0).astype(BF)
@@ -98,7 +113,7 @@
         sc[1, pl.ds(at, 8), :] = total[:, 128:]
         return 0
 
-    lax.fori_loop(0, cols, forward, 0, unroll=32)
+    lax.fori_loop(0, cols, forward, 0, unroll=96)
 
     def backward(m, _):
         window = gp[pl.ds(pl.multiple_of(m * 128, 128), 256), :]
@@ -116,7 +131,7 @@
             gs[io, pl.ds(at, 8), :] = shift_lanes(part[0], -1) + part[1] + shift_lanes(part[2], 1)
         return 0
 
-    lax.fori_loop(0, cols // 2, backward, 0, unroll=16)
+    lax.fori_loop(0, cols // 2, backward, 0, unroll=48)
 
     for k in range(4):
         for i in range(2):
@@ -131,19 +146,19 @@
         near_out[here, :] = jnp.where(first, hi, lo).astype(BF)
 
 
-def conv(cols, core, w_out, weights, own, up, dn, far, near, cot):
+def conv(cols, scale, spot, weights, tgt, src, far, near, up, dn, cot, halos):
     vmem = pl.BlockSpec(memory_space=pltpu.VMEM)
     smem = pl.BlockSpec(memory_space=pltpu.SMEM)
     n = 4 * cols
     return pl.pallas_call(
-        functools.partial(conv_kernel, cols),
+        functools.partial(conv_kernel, cols, scale),
         out_shape=(
             jax.ShapeDtypeStruct((8 * cols, 128), BF),
             jax.ShapeDtypeStruct((n, 256), F32),
             jax.ShapeDtypeStruct((n, 128), BF),
             jax.ShapeDtypeStruct((n, 128), BF),
         ),
-        in_specs=[smem, smem] + [vmem] * 9,
+        in_specs=[smem] + [vmem] * (10 + len(halos)),
         out_specs=(vmem,) * 4,
         scratch_shapes=[
             pltpu.VMEM((4, 8 * cols, 128), F32),
@@ -156,10 +171,10 @@
         ],
         compiler_params=pltpu.CompilerParams(vmem_limit_bytes=40 * 2**20),
         cost_estimate=pl.CostEstimate(flops=4 * 10**9, transcendentals=10**7, bytes_accessed=4 * 10**6),
-    )(core, w_out, *weights, own, up, dn, far, near, cot)
-
-
-def filters(w_src, b_src, w_tgt, b_tgt, first_row, total_rows):
+    )(spot, *weights, tgt, src, far, near, up, dn, cot, *halos)
+
+
+def filters(w_src, b_src, w_tgt, b_tgt, w_out, first_row, total_rows):
     both = jnp.einsum(
         "opde,pab->odeab", w_tgt.astype(F32), w_src.astype(F32), precision=lax.Precision.HIGHEST
     )
@@ -189,7 +204,8 @@
     along = jnp.einsum("ode,te->tod", lift, edge, precision=lax.Precision.HIGHEST)
     reach = jnp.einsum("dmk,k->md", up, inside, precision=lax.Precision.HIGHEST)
     bias = b_tgt[None, :, None] + jnp.einsum("tod,md->tom", along, reach, precision=lax.Precision.HIGHEST)
-    bias = jnp.broadcast_to((0.5 * bias).reshape(192, 1), (192, 256))
+    bias = jnp.concatenate([(0.5 * bias).reshape(192), jnp.repeat(w_out, 8)])
+    bias = jnp.broadcast_to(bias[:, None], (256, 256))
     return wf, wb, bias
 
 
@@ -222,38 +238,44 @@
     chans = tgt_feat.shape[2]
     scale = chans ** (-0.5)
     n_src, n_tgt = lax.axis_size(SRC), lax.axis_size(TGT)
-    t, z, core, zh = (lax.axis_index(a) for a in (TGT, "z", "core", "zh"))
+    s, t, z, core, zh = (lax.axis_index(a) for a in (SRC, TGT, "z", "core", "zh"))
     first = core == 0
     block = chans // n_tgt
     pixels = rows_i * cols_j
 
-    weights = filters(w_src, b_src, w_tgt, b_tgt, t * rows_k, rows_k * n_tgt)
+    weights = filters(w_src, b_src, w_tgt, b_tgt, w_out, t * rows_k, rows_k * n_tgt)
     tgt_flat = tgt_feat.reshape(rows_k * cols, chans)
-
-    piece = src_feat.reshape(pixels, block).T
-    src_t = lax.all_to_all(
-        jnp.broadcast_to(piece[None], (n_tgt, block, pixels)), TGT, 0, 0, tiled=True
-    ).reshape(chans, pixels)
-
-    raw = jnp.dot(tgt_flat, src_t, preferred_element_type=F32)
-    own = (raw * scale).astype(BF)
     cot = cotangent.reshape(rows_k * cols * rows_i, cols_j)
+    width = chans // n_src
+    hops = n_src // 2
 
     def edge(k, cot_k):
-        part = own[k * cols:(k + 2) * cols]
-        line = cot[cot_k * cols * rows_i:(cot_k + 1) * cols * rows_i]
-        return jnp.concatenate([part[:, :cols_j], part[:, cols_j:], line], 0)
+        part = lax.dynamic_slice_in_dim(tgt_flat[k * cols:(k + 2) * cols], s * width, width, 1)
+        return jnp.concatenate([part, cot[cot_k * cols * rows_i:(cot_k + 1) * cols * rows_i]], 0)
 
     up = moved(edge(rows_k - 2, rows_k - 1), lambda a, b: (a, b + 1))
     dn = moved(edge(0, 0), lambda a, b: (a, b - 1))
     two = 2 * cols
-    low = jnp.concatenate([up[:two], own[:, :cols_j], dn[:two]], 0)
-    high = jnp.concatenate([up[two:2 * two], own[:, cols_j:], dn[two:2 * two]], 0)
+    share = jnp.concatenate([up[:two], dn[:two]], 0)
+    halos = []
+    for m in range(hops):
+        mine = share if m == 0 else moved(share, lambda a, b, m=m: (a ^ (2 * m), b))
+        halos += [mine, moved(mine, near_row)]
+
+    piece = src_feat.reshape(pixels, block).T
+    other = moved(piece, lambda a, b: (a, b ^ 1))
+    pair = jnp.where(zh == 0, jnp.concatenate([piece, other], 0), jnp.concatenate([other, piece], 0))
+    plane = n_tgt // 2
+    src_t = lax.all_to_all(
+        jnp.broadcast_to(pair[None], (plane, 2 * block, pixels)), ("y", "x"), 0, 0, tiled=True
+    ).reshape(chans, pixels)
+    low, high = src_t[:, :cols_j], src_t[:, cols_j:]
     near = moved(jnp.where(first, high, low), near_row)
     far = moved(jnp.where(first, low, high), far_row)
 
+    spot = jnp.stack([z, core]).astype(jnp.int32)
     score, g_own, to_far, to_near = conv(
-        cols, core.astype(jnp.int32)[None], w_out, weights, own, up, dn, far, near, cot
+        cols, scale, spot, weights, tgt_flat, src_t, far, near, up, dn, cot, halos
     )
     from_near = moved(to_near, near_row)
     from_far = moved(to_far, far_row)
@@ -265,8 +287,7 @@
         1,
     ).astype(BF)
 
-    cut = src_t.reshape(n_src, chans // n_src, pixels)
-    hops = n_src // 2
+    cut = src_t.reshape(n_src, width, pixels)
 
     def blocks(side):
         return jnp.concatenate(
@@ -278,7 +299,6 @@
     got = moved(other.astype(BF), near_row)
     mine = lax.dot_general(g, blocks(core), over, preferred_element_type=F32) * scale
     both = mine + got.astype(F32)
-    width = chans // n_src
     total = both[:, :width]
     for m in range(1, hops):
         total = total + moved(
@@ -287,7 +307,6 @@
     grad_tgt = total.reshape(rows_k, cols, width)
 
     part = lax.dot_general(tgt_flat, g, (((0,), (0,)), ((), ())), preferred_element_type=F32) * scale
-    plane = n_tgt // 2
     parts = lax.all_to_all(
         part.astype(BF).reshape(plane, 2 * block, pixels), ("y", "x"), 0, 0, tiled=True
     )

time: 107 us -> 106 us (level)
  waiting for transfers between devices: 45.1 us -> 36.2 us
  starting transfers between devices: 37.7 us -> 41.6 us
  local copies, waits for them, and re-layouts: 9.68 us -> 13 us
    all_to_all x1, waiting for transfers between devices: 14.8 us -> 8.33 us  [body(): lax.all_to_all(jnp.broadcast_to(pair[None], (plane, 2 * block, pixels)),...]
    ppermute x11 -> x19, starting transfers between devices: 17.6 us -> 23.4 us  [moved(): return lax.ppermute(x, SRC + TGT, pairs)]
    all_to_all x1, starting transfers between devices: 6.94 us -> 3.57 us  [body(): lax.all_to_all(part.astype(BF).reshape(plane, 2 * block, pixels), ('y', '...]
    slice x5, local copies, waits for them, and re-layouts: 0.14 us -> 2.86 us  [the longest x1 1.17 us: edge(): tgt_flat[k * cols:(k + 2) * cols]]
    ppermute x11 -> x19, waiting for transfers between devices: 22 us -> 19.5 us  [moved(): return lax.ppermute(x, SRC + TGT, pairs)]
    all_to_all x1, starting transfers between devices: 13.2 us -> 14.6 us  [body(): lax.all_to_all(jnp.broadcast_to(pair[None], (plane, 2 * block, pixels)),...]
    convert_element_type x2, local copies, waits for them, and re-layouts: 0.8 us -> 1.94 us  [filters(): jnp.einsum('odeab,desklm->baskyom'.replace('y', 'l'), both, spots)]
    unnamed x22 -> x26, local copies, waits for them, and re-layouts: 3.08 us -> 2.39 us
  transfers between devices with their start and end apart: 13 -> 21, of which waited for: 6 -> 8; matrix products, arithmetic and copies ran while one was open for 7% -> 12% of each run, Pallas kernels for 0% -> 0%
where the time goes in v3:
time: 106 us; the launch traced here: 105 us
  starting transfers between devices  41.6 us (39%)
  waiting for transfers between devices  36.2 us (34%)
  local copies, waits for them, and re-layouts  13 us (12%)
  Pallas kernels  8.9 us (8%)
  matrix products  3.52 us (3%)
  between operations  1.1 us (1%)
  other arithmetic  1.08 us (1%)
    ppermute x19, starting transfers between devices, moved(): return lax.ppermute(x, SRC + TGT, pairs)  23.4 us
    ppermute x19, waiting for transfers between devices, moved(): return lax.ppermute(x, SRC + TGT, pairs)  19.5 us
    all_to_all x1, starting transfers between devices, body(): lax.all_to_all(jnp.broadcast_to(pair[None], (plane, 2 * block, pixels)),...  14.6 us
    pallas_call x1, Pallas kernels, conv(): pl.pallas_call(functools.partial(conv_kernel, cols, scale), out_shape=(ja...  8.9 us
    all_to_all x1, waiting for transfers between devices, body(): lax.all_to_all(part.astype(BF).reshape(plane, 2 * block, pixels), ('y', '...  8.33 us
    all_to_all x1, waiting for transfers between devices, body(): lax.all_to_all(jnp.broadcast_to(pair[None], (plane, 2 * block, pixels)),...  8.33 us
    all_to_all x1, starting transfers between devices, body(): lax.all_to_all(part.astype(BF).reshape(plane, 2 * block, pixels), ('y', '...  3.57 us
    unnamed x26, local copies, waits for them, and re-layouts  2.39 us
  transfers between devices with their start and end apart: 21, of which 8 were waited for; matrix products, arithmetic and copies ran while one was open for 12% of the time, Pallas kernels for 0%

profile of v3, /device:TPU:32, one launch (start us, length us, event | category | flops | bytes accessed | tf_op | source)
XLA Modules:
  0.0 105.3 jit_solution(17358642164370824213)
XLA Ops:
  1.4 6.3 %collective-permute-start = (bf16[32,256]{1,0:T(8,128)(2,1)S(1)}, bf16[32,256]{1,0:T(8,128)(2,1)S(1)}, u32[]{:S(2)}, u32[]{:S(2)}) collective-permute-start(bf16[32,256]{1,0:T(8,128)(2,1)S(1)} %bitcast_bitcast_fusion), channel_id=1, source_target_pairs={{0,1},{1,0},{2,3},{3,2},{4,5},{5,4},{6,7},{7,6},{8,9},{9,8},{10,11... | collective-permute-start | bytes 49160 | tf_op jit(solution)/shard_map/ppermute | solution.py:225
  8.6 1.2 %fusion.50 = (bf16[2,96,1024]{2,1,0:T(8,128)(2,1)S(1)}, bf16[2,96,1024]{2,1,0:T(8,128)(2,1)S(1)}) fusion(bf16[4,96,1024]{2,1,0:T(8,128)(2,1)} %param.13), kind=kLoop, calls=%fused_computation.84 | loop fusion | bytes 1572864 | tf_op jit(solution)/shard_map/slice | solution.py:253
  9.8 1.9 %collective-permute-start.3 = (bf16[384,128]{1,0:T(8,128)(2,1)S(1)}, bf16[384,128]{1,0:T(8,128)(2,1)S(1)}, u32[]{:S(2)}, u32[]{:S(2)}) collective-permute-start(bf16[384,128]{1,0:T(8,128)(2,1)S(1)} %pad_maximum_fusion.1), channel_id=1, source_target_pairs={{0,1},{1,2},{2,3},{3,4},{4,5},{5,6},{6,7},{7,8},{8,9},{9,10},{10,1... | collective-permute-start | bytes 294920 | tf_op jit(solution)/shard_map/ppermute | solution.py:225
  11.8 1.3 %collective-permute-start.4 = (bf16[384,128]{1,0:T(8,128)(2,1)S(1)}, bf16[384,128]{1,0:T(8,128)(2,1)S(1)}, u32[]{:S(2)}, u32[]{:S(2)}) collective-permute-start(bf16[384,128]{1,0:T(8,128)(2,1)S(1)} %pad_maximum_fusion.2), channel_id=1, source_target_pairs={{1,0},{2,1},{3,2},{4,3},{5,4},{6,5},{7,6},{8,7},{9,8},{10,9},{11,1... | collective-permute-start | bytes 294920 | tf_op jit(solution)/shard_map/ppermute | solution.py:225
  14.9 1.2 %fusion.3 = bf16[3,3,2,4,4,8,8]{6,5,4,3,2,0,1:T(8,128)(2,1)} fusion(bf16[3,3,2,4,4,8,1,1]{5,1,0,4,3,2,7,6:T(4,128)(2,1)S(1)} %copy-done.12, bf16[8,3,3,3,3,1,1,1]{0,4,3,2,1,7,6,5:T(4,128)(2,1)S(1)} %bitcast.119), kind=kOutput, calls=%fused_computation.8 | convolution fusion | flops 331776 | bytes 42768 | tf_op jit(solution)/shard_map/odeab,desklm->basklom/dot_general | solution.py:195
  17.3 14.6 %all-to-all-start = ((bf16[16,64,256]{2,1,0:T(8,128)(2,1)}), bf16[16,64,256]{2,1,0:T(8,128)(2,1)S(1)}, u32[]{:S(2)}, u32[]{:S(2)}) async-start(bf16[16,64,256]{2,1,0:T(8,128)(2,1)} %broadcast_in_dim.8), calls=%async_computation | async-start | bytes 1048576 | tf_op jit(solution)/shard_map/all_to_all | solution.py:269
  34.4 8.3 %all-to-all-done = bf16[16,64,256]{2,1,0:T(8,128)(2,1)S(1)} async-done(((bf16[16,64,256]{2,1,0:T(8,128)(2,1)}), bf16[16,64,256]{2,1,0:T(8,128)(2,1)S(1)}, u32[]{:S(2)}, u32[]{:S(2)}) %all-to-all-start) | async-done | bytes 524320 | tf_op jit(solution)/shard_map/all_to_all | solution.py:269
  42.8 1.9 %collective-permute-start.1 = (bf16[1024,128]{1,0:T(8,128)(2,1)S(1)}, bf16[1024,128]{1,0:T(8,128)(2,1)S(1)}, u32[]{:S(2)}, u32[]{:S(2)}) collective-permute-start(bf16[1024,128]{1,0:T(8,128)(2,1)S(1)} %get-tuple-element.24), channel_id=1, source_target_pairs={{32,64},{33,65},{34,66},{35,67},{36,68},{37,69},{38,70},{39,71},{4... | collective-permute-start | bytes 786440 | tf_op jit(solution)/shard_map/ppermute | solution.py:225
  44.7 1.2 %collective-permute-start.2 = (bf16[1024,128]{1,0:T(8,128)(2,1)S(1)}, bf16[1024,128]{1,0:T(8,128)(2,1)S(1)}, u32[]{:S(2)}, u32[]{:S(2)}) collective-permute-start(bf16[1024,128]{1,0:T(8,128)(2,1)S(1)} %get-tuple-element.23), channel_id=1, source_target_pairs={{0,32},{1,33},{2,34},{3,35},{4,36},{5,37},{6,38},{7,39},{8,40},{9,... | collective-permute-start | bytes 786440 | tf_op jit(solution)/shard_map/ppermute | solution.py:225
  46.1 1.5 %copy.21 = bf16[8,8,3,10,8]{1,0,4,3,2:T(8,128)(2,1)S(1)} copy(bf16[8,8,3,10,8]{3,4,1,2,0:T(8,128)(2,1)S(1)} %fusion.6) | data formatting | bytes 61440 | tf_op jit(solution)/shard_map/convert_element_type | solution.py:186
  48.1 1.2 %copy.23 = bf16[3,3,2,4,4,8,8]{6,5,4,3,2,1,0:T(8,128)(2,1)S(1)} copy(bf16[3,3,2,4,4,8,8]{6,5,4,3,2,0,1:T(8,128)(2,1)} %fusion.3) | data formatting | bytes 73728 | tf_op jit(solution)/shard_map/convert_element_type | solution.py:195
  51.4 1.5 %collective-permute-start.8 = (bf16[384,128]{1,0:T(8,128)(2,1)S(1)}, bf16[384,128]{1,0:T(8,128)(2,1)S(1)}, u32[]{:S(2)}, u32[]{:S(2)}) collective-permute-start(bf16[384,128]{1,0:T(8,128)(2,1)S(1)} %pad_maximum_fusion.3.more_0_), channel_id=1, source_target_pairs={{0,128},{1,129},{2,130},{3,131},{4,132},{5,133},{6,134},{7,135},{8... | collective-permute-start | bytes 294920 | tf_op jit(solution)/shard_map/ppermute | solution.py:225
  54.0 2.1 %collective-permute-done.6.more_2_ = bf16[384,128]{1,0:T(8,128)(2,1)S(1)} collective-permute-done((bf16[384,128]{1,0:T(8,128)(2,1)S(1)}, bf16[384,128]{1,0:T(8,128)(2,1)S(1)}, u32[]{:S(2)}, u32[]{:S(2)}) %collective-permute-start.6) | collective-permute-done | bytes 98336 | tf_op jit(solution)/shard_map/ppermute | solution.py:225
  56.1 3.9 %collective-permute-done.8.more_4_ = bf16[384,128]{1,0:T(8,128)(2,1)S(1)} collective-permute-done((bf16[384,128]{1,0:T(8,128)(2,1)S(1)}, bf16[384,128]{1,0:T(8,128)(2,1)S(1)}, u32[]{:S(2)}, u32[]{:S(2)}) %collective-permute-start.8) | collective-permute-done | bytes 98336 | tf_op jit(solution)/shard_map/ppermute | solution.py:225
  60.0 2.7 %collective-permute-done.10.more_6_ = bf16[384,128]{1,0:T(8,128)(2,1)S(1)} collective-permute-done((bf16[384,128]{1,0:T(8,128)(2,1)S(1)}, bf16[384,128]{1,0:T(8,128)(2,1)S(1)}, u32[]{:S(2)}, u32[]{:S(2)}) %collective-permute-start.10) | collective-permute-done | bytes 98336 | tf_op jit(solution)/shard_map/ppermute | solution.py:225
  62.8 1.2 %collective-permute-done.11.more_7_ = bf16[384,128]{1,0:T(8,128)(2,1)S(1)} collective-permute-done((bf16[384,128]{1,0:T(8,128)(2,1)S(1)}, bf16[384,128]{1,0:T(8,128)(2,1)S(1)}, u32[]{:S(2)}, u32[]{:S(2)}) %collective-permute-start.11) | collective-permute-done | bytes 98336 | tf_op jit(solution)/shard_map/ppermute | solution.py:225
  64.1 8.9 %shard_map.139 = (bf16[768,128]{1,0:T(8,128)(2,1)}, f32[384,256]{1,0:T(8,128)S(1)}, bf16[384,128]{1,0:T(8,128)(2,1)S(1)}, bf16[384,128]{1,0:T(8,128)(2,1)S(1)}) custom-call(s32[2]{0:T(128)S(1)} %pad_add_fusion.spot_ref, bf16[64,240]{1,0:T(8,128)(2,1)S(1)} %copy.25.wf_ref, bf16[72,256]{1,0:T(8,128)(2,1)S(1)} %convert_element_type.68.wb_ref, ...), custom_call_target="tpu_custom_call" | custom-call | flops 4000000000 | bytes 4000000 | tf_op jit(solution)/shard_map/pallas_call | solution.py:153
  73.0 2.2 %collective-permute-start.12 = (bf16[384,128]{1,0:T(8,128)(2,1)S(1)}, bf16[384,128]{1,0:T(8,128)(2,1)S(1)}, u32[]{:S(2)}, u32[]{:S(2)}) collective-permute-start(bf16[384,128]{1,0:T(8,128)(2,1)S(1)} %get-tuple-element.9), channel_id=1, source_target_pairs={{32,64},{33,65},{34,66},{35,67},{36,68},{37,69},{38,70},{39,71},{4... | collective-permute-start | bytes 294920 | tf_op jit(solution)/shard_map/ppermute | solution.py:225
  76.2 2.7 %collective-permute-done.12 = bf16[384,128]{1,0:T(8,128)(2,1)S(1)} collective-permute-done((bf16[384,128]{1,0:T(8,128)(2,1)S(1)}, bf16[384,128]{1,0:T(8,128)(2,1)S(1)}, u32[]{:S(2)}, u32[]{:S(2)}) %collective-permute-start.12) | collective-permute-done | bytes 98336 | tf_op jit(solution)/shard_map/ppermute | solution.py:225
  81.0 3.6 %all-to-all-start.1 = ((bf16[16,64,256]{2,1,0:T(8,128)(2,1)}), bf16[16,64,256]{2,1,0:T(8,128)(2,1)S(1)}, u32[]{:S(2)}, u32[]{:S(2)}) async-start(bf16[16,64,256]{2,1,0:T(8,128)(2,1)} %bitcast.36), calls=%async_computation.1 | async-start | bytes 1048576 | tf_op jit(solution)/shard_map/all_to_all | solution.py:310
  84.9 1.1 %collective-permute-start.18 = (bf16[384,128]{1,0:T(8,128)(2,1)S(1)}, bf16[384,128]{1,0:T(8,128)(2,1)S(1)}, u32[]{:S(2)}, u32[]{:S(2)}) collective-permute-start(bf16[384,128]{1,0:T(8,128)(2,1)S(1)} %get-tuple-element.26), channel_id=1, source_target_pairs={{0,192},{1,193},{2,194},{3,195},{4,196},{5,197},{6,198},{7,199},{8... | collective-permute-start | bytes 294920 | tf_op jit(solution)/shard_map/ppermute | solution.py:225
  86.1 1.9 %collective-permute-start.17 = (bf16[384,128]{1,0:T(8,128)(2,1)S(1)}, bf16[384,128]{1,0:T(8,128)(2,1)S(1)}, u32[]{:S(2)}, u32[]{:S(2)}) collective-permute-start(bf16[384,128]{1,0:T(8,128)(2,1)S(1)} %get-tuple-element.27), channel_id=1, source_target_pairs={{0,128},{1,129},{2,130},{3,131},{4,132},{5,133},{6,134},{7,135},{8... | collective-permute-start | bytes 294920 | tf_op jit(solution)/shard_map/ppermute | solution.py:225
  88.5 8.3 %all-to-all-done.1 = bf16[16,64,256]{2,1,0:T(8,128)(2,1)S(1)} async-done(((bf16[16,64,256]{2,1,0:T(8,128)(2,1)}), bf16[16,64,256]{2,1,0:T(8,128)(2,1)S(1)}, u32[]{:S(2)}, u32[]{:S(2)}) %all-to-all-start.1) | async-done | bytes 524320 | tf_op jit(solution)/shard_map/all_to_all | solution.py:310
  97.8 6.9 %collective-permute-done.14 = bf16[32,256]{1,0:T(8,128)(2,1)S(1)} collective-permute-done((bf16[32,256]{1,0:T(8,128)(2,1)S(1)}, bf16[32,256]{1,0:T(8,128)(2,1)S(1)}, u32[]{:S(2)}, u32[]{:S(2)}) %collective-permute-start.14) | collective-permute-done | bytes 16416 | tf_op jit(solution)/shard_map/ppermute | solution.py:225
  (91 shorter events, 16.6 us)
Async XLA Ops:
  1.4 15.1 %collective-permute-start = (bf16[32,256]{1,0:T(8,128)(2,1)S(1)}, bf16[32,256]{1,0:T(8,128)(2,1)S(1)}, u32[]{:S(2)}, u32[]{:S(2)}) collective-permute-start(bf16[32,256]{1,0:T(8,128)(2,1)S(1)} %bitcast_bitcast_fusion), channel_id=1, source_target_pairs={{0,1},{1,0},{2,3},{3,2},{4,5},{5,4},{6,7},{7,6},{8,9},{9,8},{10,11... | collective-permute-start | bytes 49160 | tf_op jit(solution)/shard_map/ppermute | solution.py:225
  9.8 23.7 %collective-permute-start.3 = (bf16[384,128]{1,0:T(8,128)(2,1)S(1)}, bf16[384,128]{1,0:T(8,128)(2,1)S(1)}, u32[]{:S(2)}, u32[]{:S(2)}) collective-permute-start(bf16[384,128]{1,0:T(8,128)(2,1)S(1)} %pad_maximum_fusion.1), channel_id=1, source_target_pairs={{0,1},{1,2},{2,3},{3,4},{4,5},{5,6},{6,7},{7,8},{8,9},{9,10},{10,1... | collective-permute-start | bytes 294920 | tf_op jit(solution)/shard_map/ppermute | solution.py:225
  11.8 21.1 %collective-permute-start.4 = (bf16[384,128]{1,0:T(8,128)(2,1)S(1)}, bf16[384,128]{1,0:T(8,128)(2,1)S(1)}, u32[]{:S(2)}, u32[]{:S(2)}) collective-permute-start(bf16[384,128]{1,0:T(8,128)(2,1)S(1)} %pad_maximum_fusion.2), channel_id=1, source_target_pairs={{1,0},{2,1},{3,2},{4,3},{5,4},{6,5},{7,6},{8,7},{9,8},{10,9},{11,1... | collective-permute-start | bytes 294920 | tf_op jit(solution)/shard_map/ppermute | solution.py:225
  17.3 14.6 %copy-start.8 = (f32[3,3,1]{1,0,2:T(4,128)S(1)}, f32[3,3,1]{1,0,2:T(4,128)}, u32[]{:S(2)}) copy-start(f32[3,3,1]{1,0,2:T(4,128)} %constant.89) | copy-start | bytes 112
  17.3 25.4 %all-to-all-start = ((bf16[16,64,256]{2,1,0:T(8,128)(2,1)}), bf16[16,64,256]{2,1,0:T(8,128)(2,1)S(1)}, u32[]{:S(2)}, u32[]{:S(2)}) async-start(bf16[16,64,256]{2,1,0:T(8,128)(2,1)} %broadcast_in_dim.8), calls=%async_computation | async-start | bytes 1048576 | tf_op jit(solution)/shard_map/all_to_all | solution.py:269
  34.3 18.7 %collective-permute-start.5 = (bf16[384,128]{1,0:T(8,128)(2,1)S(1)}, bf16[384,128]{1,0:T(8,128)(2,1)S(1)}, u32[]{:S(2)}, u32[]{:S(2)}) collective-permute-start(bf16[384,128]{1,0:T(8,128)(2,1)S(1)} %pad_maximum_fusion.3.more_0_), channel_id=1, source_target_pairs={{0,32},{1,33},{2,34},{3,35},{4,36},{5,37},{6,38},{7,39},{8,40},{9,... | collective-permute-start | bytes 294920 | tf_op jit(solution)/shard_map/ppermute | solution.py:225
  42.8 21.2 %collective-permute-start.1 = (bf16[1024,128]{1,0:T(8,128)(2,1)S(1)}, bf16[1024,128]{1,0:T(8,128)(2,1)S(1)}, u32[]{:S(2)}, u32[]{:S(2)}) collective-permute-start(bf16[1024,128]{1,0:T(8,128)(2,1)S(1)} %get-tuple-element.24), channel_id=1, source_target_pairs={{32,64},{33,65},{34,66},{35,67},{36,68},{37,69},{38,70},{39,71},{4... | collective-permute-start | bytes 786440 | tf_op jit(solution)/shard_map/ppermute | solution.py:225
  44.7 19.3 %collective-permute-start.2 = (bf16[1024,128]{1,0:T(8,128)(2,1)S(1)}, bf16[1024,128]{1,0:T(8,128)(2,1)S(1)}, u32[]{:S(2)}, u32[]{:S(2)}) collective-permute-start(bf16[1024,128]{1,0:T(8,128)(2,1)S(1)} %get-tuple-element.23), channel_id=1, source_target_pairs={{0,32},{1,33},{2,34},{3,35},{4,36},{5,37},{6,38},{7,39},{8,40},{9,... | collective-permute-start | bytes 786440 | tf_op jit(solution)/shard_map/ppermute | solution.py:225
  48.1 16.0 %copy-start.1 = (bf16[4,96,1024]{2,1,0:T(8,128)(2,1)S(1)}, bf16[4,96,1024]{2,1,0:T(8,128)(2,1)}, u32[]{:S(2)}) copy-start(bf16[4,96,1024]{2,1,0:T(8,128)(2,1)} %param.13) | copy-start | bytes 2359300
  50.1 14.0 %copy-start.2 = (bf16[4,96,2,128]{3,2,1,0:T(2,128)(2,1)S(1)}, bf16[4,96,2,128]{3,2,1,0:T(2,128)(2,1)}, u32[]{:S(2)}) copy-start(bf16[4,96,2,128]{3,2,1,0:T(2,128)(2,1)} %param.19) | copy-start | bytes 589828
  50.3 5.7 %collective-permute-start.6 = (bf16[384,128]{1,0:T(8,128)(2,1)S(1)}, bf16[384,128]{1,0:T(8,128)(2,1)S(1)}, u32[]{:S(2)}, u32[]{:S(2)}) collective-permute-start(bf16[384,128]{1,0:T(8,128)(2,1)S(1)} %pad_maximum_fusion.3.more_0_), channel_id=1, source_target_pairs={{0,64},{1,65},{2,66},{3,67},{4,68},{5,69},{6,70},{7,71},{8,72},{9,... | collective-permute-start | bytes 294920 | tf_op jit(solution)/shard_map/ppermute | solution.py:225
  51.4 8.5 %collective-permute-start.8 = (bf16[384,128]{1,0:T(8,128)(2,1)S(1)}, bf16[384,128]{1,0:T(8,128)(2,1)S(1)}, u32[]{:S(2)}, u32[]{:S(2)}) collective-permute-start(bf16[384,128]{1,0:T(8,128)(2,1)S(1)} %pad_maximum_fusion.3.more_0_), channel_id=1, source_target_pairs={{0,128},{1,129},{2,130},{3,131},{4,132},{5,133},{6,134},{7,135},{8... | collective-permute-start | bytes 294920 | tf_op jit(solution)/shard_map/ppermute | solution.py:225
  52.9 9.7 %collective-permute-start.10 = (bf16[384,128]{1,0:T(8,128)(2,1)S(1)}, bf16[384,128]{1,0:T(8,128)(2,1)S(1)}, u32[]{:S(2)}, u32[]{:S(2)}) collective-permute-start(bf16[384,128]{1,0:T(8,128)(2,1)S(1)} %pad_maximum_fusion.3.more_0_), channel_id=1, source_target_pairs={{0,192},{1,193},{2,194},{3,195},{4,196},{5,197},{6,198},{7,199},{8... | collective-permute-start | bytes 294920 | tf_op jit(solution)/shard_map/ppermute | solution.py:225
  56.1 6.7 %collective-permute-start.7 = (bf16[384,128]{1,0:T(8,128)(2,1)S(1)}, bf16[384,128]{1,0:T(8,128)(2,1)S(1)}, u32[]{:S(2)}, u32[]{:S(2)}) collective-permute-start(bf16[384,128]{1,0:T(8,128)(2,1)S(1)} %collective-permute-done.6.more_2_), channel_id=1, source_target_pairs={{0,32},{1,33},{2,34},{3,35},{4,36},{5,37},{6,38},{7,39},{8,40},{9,... | collective-permute-start | bytes 294920 | tf_op jit(solution)/shard_map/ppermute | solution.py:225
  59.9 2.8 %collective-permute-start.9 = (bf16[384,128]{1,0:T(8,128)(2,1)S(1)}, bf16[384,128]{1,0:T(8,128)(2,1)S(1)}, u32[]{:S(2)}, u32[]{:S(2)}) collective-permute-start(bf16[384,128]{1,0:T(8,128)(2,1)S(1)} %collective-permute-done.8.more_4_), channel_id=1, source_target_pairs={{0,32},{1,33},{2,34},{3,35},{4,36},{5,37},{6,38},{7,39},{8,40},{9,... | collective-permute-start | bytes 294920 | tf_op jit(solution)/shard_map/ppermute | solution.py:225
  62.7 1.3 %collective-permute-start.11 = (bf16[384,128]{1,0:T(8,128)(2,1)S(1)}, bf16[384,128]{1,0:T(8,128)(2,1)S(1)}, u32[]{:S(2)}, u32[]{:S(2)}) collective-permute-start(bf16[384,128]{1,0:T(8,128)(2,1)S(1)} %collective-permute-done.10.more_6_), channel_id=1, source_target_pairs={{0,32},{1,33},{2,34},{3,35},{4,36},{5,37},{6,38},{7,39},{8,40},{9,... | collective-permute-start | bytes 294920 | tf_op jit(solution)/shard_map/ppermute | solution.py:225
  73.0 5.9 %collective-permute-start.12 = (bf16[384,128]{1,0:T(8,128)(2,1)S(1)}, bf16[384,128]{1,0:T(8,128)(2,1)S(1)}, u32[]{:S(2)}, u32[]{:S(2)}) collective-permute-start(bf16[384,128]{1,0:T(8,128)(2,1)S(1)} %get-tuple-element.9), channel_id=1, source_target_pairs={{32,64},{33,65},{34,66},{35,67},{36,68},{37,69},{38,70},{39,71},{4... | collective-permute-start | bytes 294920 | tf_op jit(solution)/shard_map/ppermute | solution.py:225
  75.2 3.7 %collective-permute-start.13 = (bf16[384,128]{1,0:T(8,128)(2,1)S(1)}, bf16[384,128]{1,0:T(8,128)(2,1)S(1)}, u32[]{:S(2)}, u32[]{:S(2)}) collective-permute-start(bf16[384,128]{1,0:T(8,128)(2,1)S(1)} %get-tuple-element.10), channel_id=1, source_target_pairs={{0,32},{1,33},{2,34},{3,35},{4,36},{5,37},{6,38},{7,39},{8,40},{9,... | collective-permute-start | bytes 294920 | tf_op jit(solution)/shard_map/ppermute | solution.py:225
  79.3 5.3 %collective-permute-start.15 = (bf16[384,512]{1,0:T(8,128)(2,1)S(1)}, bf16[384,512]{1,0:T(8,128)(2,1)S(1)}, u32[]{:S(2)}, u32[]{:S(2)}) collective-permute-start(bf16[384,512]{1,0:T(8,128)(2,1)S(1)} %fusion.2), channel_id=1, source_target_pairs={{0,32},{1,33},{2,34},{3,35},{4,36},{5,37},{6,38},{7,39},{8,40},{9,... | collective-permute-start | bytes 1179656 | tf_op jit(solution)/shard_map/ppermute | solution.py:225
  81.0 15.9 %all-to-all-start.1 = ((bf16[16,64,256]{2,1,0:T(8,128)(2,1)}), bf16[16,64,256]{2,1,0:T(8,128)(2,1)S(1)}, u32[]{:S(2)}, u32[]{:S(2)}) async-start(bf16[16,64,256]{2,1,0:T(8,128)(2,1)} %bitcast.36), calls=%async_computation.1 | async-start | bytes 1048576 | tf_op jit(solution)/shard_map/all_to_all | solution.py:310
  84.9 12.2 %collective-permute-start.18 = (bf16[384,128]{1,0:T(8,128)(2,1)S(1)}, bf16[384,128]{1,0:T(8,128)(2,1)S(1)}, u32[]{:S(2)}, u32[]{:S(2)}) collective-permute-start(bf16[384,128]{1,0:T(8,128)(2,1)S(1)} %get-tuple-element.26), channel_id=1, source_target_pairs={{0,192},{1,193},{2,194},{3,195},{4,196},{5,197},{6,198},{7,199},{8... | collective-permute-start | bytes 294920 | tf_op jit(solution)/shard_map/ppermute | solution.py:225
  86.1 11.0 %collective-permute-start.17 = (bf16[384,128]{1,0:T(8,128)(2,1)S(1)}, bf16[384,128]{1,0:T(8,128)(2,1)S(1)}, u32[]{:S(2)}, u32[]{:S(2)}) collective-permute-start(bf16[384,128]{1,0:T(8,128)(2,1)S(1)} %get-tuple-element.27), channel_id=1, source_target_pairs={{0,128},{1,129},{2,130},{3,131},{4,132},{5,133},{6,134},{7,135},{8... | collective-permute-start | bytes 294920 | tf_op jit(solution)/shard_map/ppermute | solution.py:225
  88.0 9.1 %collective-permute-start.16 = (bf16[384,128]{1,0:T(8,128)(2,1)S(1)}, bf16[384,128]{1,0:T(8,128)(2,1)S(1)}, u32[]{:S(2)}, u32[]{:S(2)}) collective-permute-start(bf16[384,128]{1,0:T(8,128)(2,1)S(1)} %get-tuple-element.25), channel_id=1, source_target_pairs={{0,64},{1,65},{2,66},{3,67},{4,68},{5,69},{6,70},{7,71},{8,72},{9,... | collective-permute-start | bytes 294920 | tf_op jit(solution)/shard_map/ppermute | solution.py:225
  97.0 7.7 %collective-permute-start.14 = (bf16[32,256]{1,0:T(8,128)(2,1)S(1)}, bf16[32,256]{1,0:T(8,128)(2,1)S(1)}, u32[]{:S(2)}, u32[]{:S(2)}) collective-permute-start(bf16[32,256]{1,0:T(8,128)(2,1)S(1)} %fusion.29), channel_id=1, source_target_pairs={{0,1},{1,0},{2,3},{3,2},{4,5},{5,4},{6,7},{7,6},{8,9},{9,8},{10,11... | collective-permute-start | bytes 49160 | tf_op jit(solution)/shard_map/ppermute | solution.py:225
  (11 other events, 24.0 us)

commit v4 on v3

--- a/solution.py
+++ b/solution.py
@@ -22,7 +22,7 @@
 
 def conv_kernel(
     cols,
-    scale, spot_ref, wf_ref, wb_ref, bias_ref, tgt_ref, src_ref, far_ref, near_ref, up_ref, dn_ref, cot_ref,
+    scale, spot_ref, wf_ref, wb_ref, bias_ref, tgt_ref, src_ref, far_ref, near_ref, pair_ref, next_ref, cot_ref,
     *more,
 ):
     n_more = len(more) - 11
@@ -30,6 +30,7 @@
     score_ref, g_ref, far_out, near_out, cs, rows, cotf, cots, gp, sc, gs = more[n_more:]
     hop, core = spot_ref[0], spot_ref[1]
     first = core == 0
+    even = spot_ref[2] == 0
 
     def put(part, at, ks):
         part = (part * scale).astype(BF).astype(F32)
@@ -55,14 +56,17 @@
                 piece[...], ref[pl.ds(pl.multiple_of(block * 128, 128), 128), :], preferred_element_type=F32
             )
             total = part if total is None else total + part
-        return total
+        pair, next_ = total[:2 * cols], total[2 * cols:]
+        return jnp.concatenate([jnp.where(even, next_, pair), jnp.where(even, pair, next_)], 0)
 
     fill(over_all, (2, 3, 4, 5))
     fill(over_pieces, (0, 1, 6, 7))
     zeros = jnp.zeros((cols, 128), F32)
-    cotf[pl.ds(0, 2 * cols), :] = up_ref[pl.ds(2 * cols, 2 * cols), :].astype(F32)
+    line = pl.ds(2 * cols, 2 * cols)
+    pair, next_ = pair_ref[line, :].astype(F32), next_ref[line, :].astype(F32)
+    cotf[pl.ds(0, 2 * cols), :] = jnp.where(even, next_, pair)
     cotf[pl.ds(2 * cols, 8 * cols), :] = cot_ref[...].astype(F32)
-    cotf[pl.ds(10 * cols, 2 * cols), :] = dn_ref[pl.ds(2 * cols, 2 * cols), :].astype(F32)
+    cotf[pl.ds(10 * cols, 2 * cols), :] = jnp.where(even, pair, next_)
     for i in range(2):
         cots[i, pl.ds(0, cols, stride=8), :] = zeros
         cots[i, pl.ds(7, cols, stride=8), :] = zeros
@@ -146,7 +150,7 @@
         near_out[here, :] = jnp.where(first, hi, lo).astype(BF)
 
 
-def conv(cols, scale, spot, weights, tgt, src, far, near, up, dn, cot, halos):
+def conv(cols, scale, spot, weights, tgt, src, far, near, pair, next_, cot, halos):
     vmem = pl.BlockSpec(memory_space=pltpu.VMEM)
     smem = pl.BlockSpec(memory_space=pltpu.SMEM)
     n = 4 * cols
@@ -171,7 +175,7 @@
         ],
         compiler_params=pltpu.CompilerParams(vmem_limit_bytes=40 * 2**20),
         cost_estimate=pl.CostEstimate(flops=4 * 10**9, transcendentals=10**7, bytes_accessed=4 * 10**6),
-    )(spot, *weights, tgt, src, far, near, up, dn, cot, *halos)
+    )(spot, *weights, tgt, src, far, near, pair, next_, cot, *halos)
 
 
 def filters(w_src, b_src, w_tgt, b_tgt, w_out, first_row, total_rows):
@@ -243,39 +247,49 @@
     block = chans // n_tgt
     pixels = rows_i * cols_j
 
-    weights = filters(w_src, b_src, w_tgt, b_tgt, w_out, t * rows_k, rows_k * n_tgt)
     tgt_flat = tgt_feat.reshape(rows_k * cols, chans)
     cot = cotangent.reshape(rows_k * cols * rows_i, cols_j)
     width = chans // n_src
     hops = n_src // 2
 
-    def edge(k, cot_k):
-        part = lax.dynamic_slice_in_dim(tgt_flat[k * cols:(k + 2) * cols], s * width, width, 1)
-        return jnp.concatenate([part, cot[cot_k * cols * rows_i:(cot_k + 1) * cols * rows_i]], 0)
-
-    up = moved(edge(rows_k - 2, rows_k - 1), lambda a, b: (a, b + 1))
-    dn = moved(edge(0, 0), lambda a, b: (a, b - 1))
+    piece = src_feat.reshape(pixels, block).T
+    line = cols * rows_i
+
+    def edge(last, *extra):
+        k = jnp.where(last, rows_k - 2, 0)
+        part = lax.dynamic_slice(tgt_feat, (k, 0, s * width), (2, cols, width)).reshape(2 * cols, width)
+        k = jnp.where(last, rows_k - 1, 0)
+        return jnp.concatenate([part, lax.dynamic_slice(cot, (k * line, 0), (line, cols_j)), *extra], 0)
+
+    even = zh == 0
+    pair = moved(edge(even, piece[:, :cols_j], piece[:, cols_j:]), lambda a, b: (a, b ^ 1))
+    next_ = moved(edge(~even), lambda a, b: (a, b + 1 if b % 2 else b - 1))
     two = 2 * cols
-    share = jnp.concatenate([up[:two], dn[:two]], 0)
-    halos = []
-    for m in range(hops):
-        mine = share if m == 0 else moved(share, lambda a, b, m=m: (a ^ (2 * m), b))
-        halos += [mine, moved(mine, near_row)]
-
-    piece = src_feat.reshape(pixels, block).T
-    other = moved(piece, lambda a, b: (a, b ^ 1))
-    pair = jnp.where(zh == 0, jnp.concatenate([piece, other], 0), jnp.concatenate([other, piece], 0))
+    share = jnp.concatenate([pair[:two], next_[:two]], 0)
+    shares = [share]
+    for m in range(1, hops):
+        shares.append(moved(share, lambda a, b, m=m: (a ^ (2 * m), b)))
+    w_src, b_src, w_tgt, b_tgt, share = lax.optimization_barrier((w_src, b_src, w_tgt, b_tgt, share))
+    weights = filters(w_src, b_src, w_tgt, b_tgt, w_out, t * rows_k, rows_k * n_tgt)
+
+    start = two + line
+    other = jnp.concatenate([pair[start:start + block], pair[start + block:]], 1)
+    both = jnp.where(even, jnp.concatenate([piece, other], 0), jnp.concatenate([other, piece], 0))
     plane = n_tgt // 2
     src_t = lax.all_to_all(
-        jnp.broadcast_to(pair[None], (plane, 2 * block, pixels)), ("y", "x"), 0, 0, tiled=True
+        jnp.broadcast_to(both[None], (plane, 2 * block, pixels)), ("y", "x"), 0, 0, tiled=True
     ).reshape(chans, pixels)
+    src_t, *shares = lax.optimization_barrier((src_t, *shares))
+    halos = []
+    for mine in shares:
+        halos += [mine, moved(mine, near_row)]
     low, high = src_t[:, :cols_j], src_t[:, cols_j:]
     near = moved(jnp.where(first, high, low), near_row)
     far = moved(jnp.where(first, low, high), far_row)
 
-    spot = jnp.stack([z, core]).astype(jnp.int32)
+    spot = jnp.stack([z, core, zh]).astype(jnp.int32)
     score, g_own, to_far, to_near = conv(
-        cols, scale, spot, weights, tgt_flat, src_t, far, near, up, dn, cot, halos
+        cols, scale, spot, weights, tgt_flat, src_t, far, near, pair, next_, cot, halos
     )
     from_near = moved(to_near, near_row)
     from_far = moved(to_far, far_row)

time: 106 us -> 97.3 us (0.918)
  waiting for transfers between devices: 36.2 us -> 26.4 us
  local copies, waits for them, and re-layouts: 13 us -> 11.2 us
  starting transfers between devices: 41.6 us -> 43.4 us
    ppermute x19 -> x18, waiting for transfers between devices: 19.5 us -> 10.6 us  [moved(): return lax.ppermute(x, SRC + TGT, pairs)]
    ppermute x19 -> x18, starting transfers between devices: 23.4 us -> 31.1 us  [moved(): return lax.ppermute(x, SRC + TGT, pairs)]
    all_to_all x1, starting transfers between devices: 14.6 us -> 8.71 us  [body(): lax.all_to_all(jnp.broadcast_to(both[None], (plane, 2 * block, pixels)),...]
    slice x5, local copies, waits for them, and re-layouts: 2.86 us -> 0.81 us  [the longest x3 0.8 us: body(): share = jnp.concatenate([pair[:two], next_[:two]], 0)]
    dynamic_slice x2, local copies, waits for them, and re-layouts: 0.05 us -> 1.67 us  [the longest x1 0.84 us: edge(): lax.dynamic_slice(cot, (k * line, 0), (line, cols_j))]
    unnamed x26 -> x28, local copies, waits for them, and re-layouts: 2.39 us -> 1.72 us
  transfers between devices with their start and end apart: 21 -> 20, of which waited for: 8 -> 8; matrix products, arithmetic and copies ran while one was open for 12% -> 11% of each run, Pallas kernels for 0% -> 0%
where the time goes in v4:
time: 97.3 us; the launch traced here: 96.2 us
  starting transfers between devices  43.4 us (45%)
  waiting for transfers between devices  26.4 us (27%)
  local copies, waits for them, and re-layouts  11.2 us (12%)
  Pallas kernels  8.84 us (9%)
  matrix products  3.54 us (4%)
  other arithmetic  1.91 us (2%)
  between operations  1.02 us (1%)
    ppermute x18, starting transfers between devices, moved(): return lax.ppermute(x, SRC + TGT, pairs)  31.1 us
    ppermute x18, waiting for transfers between devices, moved(): return lax.ppermute(x, SRC + TGT, pairs)  10.6 us
    pallas_call x1, Pallas kernels, conv(): pl.pallas_call(functools.partial(conv_kernel, cols, scale), out_shape=(ja...  8.84 us
    all_to_all x1, starting transfers between devices, body(): lax.all_to_all(jnp.broadcast_to(both[None], (plane, 2 * block, pixels)),...  8.71 us
    all_to_all x1, waiting for transfers between devices, body(): lax.all_to_all(part.astype(BF).reshape(plane, 2 * block, pixels), ('y', '...  7.98 us
    all_to_all x1, waiting for transfers between devices, body(): lax.all_to_all(jnp.broadcast_to(both[None], (plane, 2 * block, pixels)),...  7.74 us
    all_to_all x1, starting transfers between devices, body(): lax.all_to_all(part.astype(BF).reshape(plane, 2 * block, pixels), ('y', '...  3.57 us
  transfers between devices with their start and end apart: 20, of which 8 were waited for; matrix products, arithmetic and copies ran while one was open for 11% of the time, Pallas kernels for 0%

profile of v4, /device:TPU:32, one launch (start us, length us, event | category | flops | bytes accessed | tf_op | source)
XLA Modules:
  0.0 96.2 jit_solution(1009759940003032678)
XLA Ops:
  0.7 0.8 constant_dynamic-slice_fusion.2
  1.5 0.8 constant_dynamic-slice_fusion.3
  3.1 8.2 %collective-permute-start = (bf16[448,128]{1,0:T(8,128)(2,1)S(1)}, bf16[448,128]{1,0:T(8,128)(2,1)S(1)}, u32[]{:S(2)}, u32[]{:S(2)}) collective-permute-start(bf16[448,128]{1,0:T(8,128)(2,1)S(1)} %pad_maximum_fusion.1), channel_id=1, source_target_pairs={{0,1},{1,0},{2,3},{3,2},{4,5},{5,4},{6,7},{7,6},{8,9},{9,8},{10,11... | collective-permute-start | bytes 344072 | tf_op jit(solution)/shard_map/ppermute | solution.py:229
  13.0 5.9 %collective-permute-done.pair_ref = bf16[448,128]{1,0:T(8,128)(2,1)S(1)} collective-permute-done((bf16[448,128]{1,0:T(8,128)(2,1)S(1)}, bf16[448,128]{1,0:T(8,128)(2,1)S(1)}, u32[]{:S(2)}, u32[]{:S(2)}) %collective-permute-start) | collective-permute-done | bytes 114720 | tf_op jit(solution)/shard_map/ppermute | solution.py:229
  19.8 4.9 %collective-permute-start.3 = (bf16[384,128]{1,0:T(8,128)(2,1)S(1)}, bf16[384,128]{1,0:T(8,128)(2,1)S(1)}, u32[]{:S(2)}, u32[]{:S(2)}) collective-permute-start(bf16[384,128]{1,0:T(8,128)(2,1)S(1)} %pad_maximum_fusion.3.more_0_), channel_id=1, source_target_pairs={{0,128},{1,129},{2,130},{3,131},{4,132},{5,133},{6,134},{7,135},{8... | collective-permute-start | bytes 294920 | tf_op jit(solution)/shard_map/ppermute | solution.py:229
  25.0 0.9 broadcast_in_dim.8
  25.9 8.7 %all-to-all-start = ((bf16[16,64,256]{2,1,0:T(8,128)(2,1)}), bf16[16,64,256]{2,1,0:T(8,128)(2,1)S(1)}, u32[]{:S(2)}, u32[]{:S(2)}) async-start(bf16[16,64,256]{2,1,0:T(8,128)(2,1)} %broadcast_in_dim.8), calls=%async_computation | async-start | bytes 1048576 | tf_op jit(solution)/shard_map/all_to_all | solution.py:279
  35.6 1.2 %fusion.3 = bf16[3,3,2,4,4,8,8]{6,5,4,3,2,0,1:T(8,128)(2,1)} fusion(bf16[3,3,2,4,4,8,1,1]{5,1,0,4,3,2,7,6:T(4,128)(2,1)S(1)} %copy-done.13, bf16[8,3,3,3,3,1,1,1]{0,4,3,2,1,7,6,5:T(4,128)(2,1)S(1)} %bitcast.117), kind=kOutput, calls=%fused_computation.8 | convolution fusion | flops 331776 | bytes 42768 | tf_op jit(solution)/shard_map/odeab,desklm->basklom/dot_general | solution.py:199
  37.0 7.7 %all-to-all-done = bf16[16,64,256]{2,1,0:T(8,128)(2,1)S(1)} async-done(((bf16[16,64,256]{2,1,0:T(8,128)(2,1)}), bf16[16,64,256]{2,1,0:T(8,128)(2,1)S(1)}, u32[]{:S(2)}, u32[]{:S(2)}) %all-to-all-start) | async-done | bytes 524320 | tf_op jit(solution)/shard_map/all_to_all | solution.py:279
  44.8 0.9 broadcast_select_fusion
  45.6 2.0 %collective-permute-start.5 = (bf16[1024,128]{1,0:T(8,128)(2,1)}, bf16[1024,128]{1,0:T(8,128)(2,1)S(1)}, u32[]{:S(2)}, u32[]{:S(2)}) collective-permute-start(bf16[1024,128]{1,0:T(8,128)(2,1)} %get-tuple-element.42), channel_id=1, source_target_pairs={{32,64},{33,65},{34,66},{35,67},{36,68},{37,69},{38,70},{39,71},{4... | collective-permute-start | bytes 786440 | tf_op jit(solution)/shard_map/ppermute | solution.py:229
  47.7 0.9 collective-permute-start.6
  48.9 1.5 %copy.23 = bf16[8,8,3,10,8]{1,0,4,3,2:T(8,128)(2,1)S(1)} copy(bf16[8,8,3,10,8]{3,4,1,2,0:T(8,128)(2,1)S(1)} %fusion.6) | data formatting | bytes 61440 | tf_op jit(solution)/shard_map/convert_element_type | solution.py:190
  50.9 1.2 %copy.25 = bf16[3,3,2,4,4,8,8]{6,5,4,3,2,1,0:T(8,128)(2,1)S(1)} copy(bf16[3,3,2,4,4,8,8]{6,5,4,3,2,0,1:T(8,128)(2,1)} %fusion.3) | data formatting | bytes 73728 | tf_op jit(solution)/shard_map/convert_element_type | solution.py:199
  55.0 8.8 %shard_map.139 = (bf16[768,128]{1,0:T(8,128)(2,1)}, f32[384,256]{1,0:T(8,128)S(1)}, bf16[384,128]{1,0:T(8,128)(2,1)S(1)}, bf16[384,128]{1,0:T(8,128)(2,1)S(1)}) custom-call(s32[3]{0:T(128)S(1)} %pad_add_fusion.spot_ref, bf16[64,240]{1,0:T(8,128)(2,1)S(1)} %copy.26.wf_ref, bf16[72,256]{1,0:T(8,128)(2,1)S(1)} %convert_element_type.68.wb_ref, ...), custom_call_target="tpu_custom_call" | custom-call | flops 4000000000 | bytes 4000000 | tf_op jit(solution)/shard_map/pallas_call | solution.py:157
  63.9 3.1 %collective-permute-start.11 = (bf16[384,128]{1,0:T(8,128)(2,1)S(1)}, bf16[384,128]{1,0:T(8,128)(2,1)S(1)}, u32[]{:S(2)}, u32[]{:S(2)}) collective-permute-start(bf16[384,128]{1,0:T(8,128)(2,1)S(1)} %get-tuple-element.27), channel_id=1, source_target_pairs={{32,64},{33,65},{34,66},{35,67},{36,68},{37,69},{38,70},{39,71},{4... | collective-permute-start | bytes 294920 | tf_op jit(solution)/shard_map/ppermute | solution.py:229
  67.2 2.6 %collective-permute-done.11 = bf16[384,128]{1,0:T(8,128)(2,1)S(1)} collective-permute-done((bf16[384,128]{1,0:T(8,128)(2,1)S(1)}, bf16[384,128]{1,0:T(8,128)(2,1)S(1)}, u32[]{:S(2)}, u32[]{:S(2)}) %collective-permute-start.11) | collective-permute-done | bytes 98336 | tf_op jit(solution)/shard_map/ppermute | solution.py:229
  71.1 1.0 %copy.27 = bf16[1024,256]{1,0:T(8,128)(2,1)} copy(bf16[1024,256]{0,1:T(8,128)(2,1)S(1)} %fusion.5) | data formatting | bytes 1048576 | tf_op jit(solution)/shard_map/convert_element_type | solution.py:325
  72.1 3.6 %all-to-all-start.1 = ((bf16[16,64,256]{2,1,0:T(8,128)(2,1)}), bf16[16,64,256]{2,1,0:T(8,128)(2,1)S(1)}, u32[]{:S(2)}, u32[]{:S(2)}) async-start(bf16[16,64,256]{2,1,0:T(8,128)(2,1)} %bitcast.35), calls=%async_computation.1 | async-start | bytes 1048576 | tf_op jit(solution)/shard_map/all_to_all | solution.py:324
  76.0 1.1 %collective-permute-start.17 = (bf16[384,128]{1,0:T(8,128)(2,1)S(1)}, bf16[384,128]{1,0:T(8,128)(2,1)S(1)}, u32[]{:S(2)}, u32[]{:S(2)}) collective-permute-start(bf16[384,128]{1,0:T(8,128)(2,1)S(1)} %get-tuple-element.44), channel_id=1, source_target_pairs={{0,192},{1,193},{2,194},{3,195},{4,196},{5,197},{6,198},{7,199},{8... | collective-permute-start | bytes 294920 | tf_op jit(solution)/shard_map/ppermute | solution.py:229
  77.2 2.6 %collective-permute-start.16 = (bf16[384,128]{1,0:T(8,128)(2,1)S(1)}, bf16[384,128]{1,0:T(8,128)(2,1)S(1)}, u32[]{:S(2)}, u32[]{:S(2)}) collective-permute-start(bf16[384,128]{1,0:T(8,128)(2,1)S(1)} %get-tuple-element.45), channel_id=1, source_target_pairs={{0,128},{1,129},{2,130},{3,131},{4,132},{5,133},{6,134},{7,135},{8... | collective-permute-start | bytes 294920 | tf_op jit(solution)/shard_map/ppermute | solution.py:229
  79.8 8.0 %all-to-all-done.1 = bf16[16,64,256]{2,1,0:T(8,128)(2,1)S(1)} async-done(((bf16[16,64,256]{2,1,0:T(8,128)(2,1)}), bf16[16,64,256]{2,1,0:T(8,128)(2,1)S(1)}, u32[]{:S(2)}, u32[]{:S(2)}) %all-to-all-start.1) | async-done | bytes 524320 | tf_op jit(solution)/shard_map/all_to_all | solution.py:324
  87.8 5.8 %collective-permute-start.13 = (bf16[32,256]{1,0:T(8,128)(2,1)S(1)}, bf16[32,256]{1,0:T(8,128)(2,1)S(1)}, u32[]{:S(2)}, u32[]{:S(2)}) collective-permute-start(bf16[32,256]{1,0:T(8,128)(2,1)S(1)} %fusion.29), channel_id=1, source_target_pairs={{0,1},{1,0},{2,3},{3,2},{4,5},{5,4},{6,7},{7,6},{8,9},{9,8},{10,11... | collective-permute-start | bytes 49160 | tf_op jit(solution)/shard_map/ppermute | solution.py:229
  94.3 1.2 %collective-permute-done.13 = bf16[32,256]{1,0:T(8,128)(2,1)S(1)} collective-permute-done((bf16[32,256]{1,0:T(8,128)(2,1)S(1)}, bf16[32,256]{1,0:T(8,128)(2,1)S(1)}, u32[]{:S(2)}, u32[]{:S(2)}) %collective-permute-start.13) | collective-permute-done | bytes 16416 | tf_op jit(solution)/shard_map/ppermute | solution.py:229
  (91 shorter events, 11.6 us)
Async XLA Ops:
  0.6 24.0 %copy-start = (bf16[8,8,3,3]{1,0,3,2:T(8,128)(2,1)S(1)}, bf16[8,8,3,3]{1,0,3,2:T(8,128)(2,1)}, u32[]{:S(2)}) copy-start(bf16[8,8,3,3]{1,0,3,2:T(8,128)(2,1)} %param.16) | copy-start | bytes 3460
  2.4 9.9 %collective-permute-start.1 = (bf16[384,128]{1,0:T(8,128)(2,1)S(1)}, bf16[384,128]{1,0:T(8,128)(2,1)S(1)}, u32[]{:S(2)}, u32[]{:S(2)}) collective-permute-start(bf16[384,128]{1,0:T(8,128)(2,1)S(1)} %pad_maximum_fusion.2), channel_id=1, source_target_pairs={{1,2},{2,1},{3,4},{4,3},{5,6},{6,5},{7,8},{8,7},{9,10},{10,9},{11,... | collective-permute-start | bytes 294920 | tf_op jit(solution)/shard_map/ppermute | solution.py:229
  3.1 8.2 %copy-start.6 = (f32[3,8,8]{1,2,0:T(8,128)S(1)}, f32[3,8,8]{1,2,0:T(8,128)}, u32[]{:S(2)}) copy-start(f32[3,8,8]{1,2,0:T(8,128)} %constant.96) | copy-start | bytes 2308
  3.1 15.7 %collective-permute-start = (bf16[448,128]{1,0:T(8,128)(2,1)S(1)}, bf16[448,128]{1,0:T(8,128)(2,1)S(1)}, u32[]{:S(2)}, u32[]{:S(2)}) collective-permute-start(bf16[448,128]{1,0:T(8,128)(2,1)S(1)} %pad_maximum_fusion.1), channel_id=1, source_target_pairs={{0,1},{1,0},{2,3},{3,2},{4,5},{5,4},{6,7},{7,6},{8,9},{9,8},{10,11... | collective-permute-start | bytes 344072 | tf_op jit(solution)/shard_map/ppermute | solution.py:229
  19.6 5.0 %copy-start.8 = (bf16[8,3,3]{0,2,1:T(4,128)(2,1)S(1)}, bf16[8,3,3]{0,2,1:T(4,128)(2,1)}, u32[]{:S(2)}) copy-start(bf16[8,3,3]{0,2,1:T(4,128)(2,1)} %param.14) | copy-start | bytes 436
  19.7 17.3 %collective-permute-start.2 = (bf16[384,128]{1,0:T(8,128)(2,1)S(1)}, bf16[384,128]{1,0:T(8,128)(2,1)S(1)}, u32[]{:S(2)}, u32[]{:S(2)}) collective-permute-start(bf16[384,128]{1,0:T(8,128)(2,1)S(1)} %pad_maximum_fusion.3.more_0_), channel_id=1, source_target_pairs={{0,64},{1,65},{2,66},{3,67},{4,68},{5,69},{6,70},{7,71},{8,72},{9,... | collective-permute-start | bytes 294920 | tf_op jit(solution)/shard_map/ppermute | solution.py:229
  19.8 17.3 %collective-permute-start.3 = (bf16[384,128]{1,0:T(8,128)(2,1)S(1)}, bf16[384,128]{1,0:T(8,128)(2,1)S(1)}, u32[]{:S(2)}, u32[]{:S(2)}) collective-permute-start(bf16[384,128]{1,0:T(8,128)(2,1)S(1)} %pad_maximum_fusion.3.more_0_), channel_id=1, source_target_pairs={{0,128},{1,129},{2,130},{3,131},{4,132},{5,133},{6,134},{7,135},{8... | collective-permute-start | bytes 294920 | tf_op jit(solution)/shard_map/ppermute | solution.py:229
  24.6 12.4 %collective-permute-start.4 = (bf16[384,128]{1,0:T(8,128)(2,1)S(1)}, bf16[384,128]{1,0:T(8,128)(2,1)S(1)}, u32[]{:S(2)}, u32[]{:S(2)}) collective-permute-start(bf16[384,128]{1,0:T(8,128)(2,1)S(1)} %pad_maximum_fusion.3.more_0_), channel_id=1, source_target_pairs={{0,192},{1,193},{2,194},{3,195},{4,196},{5,197},{6,198},{7,199},{8... | collective-permute-start | bytes 294920 | tf_op jit(solution)/shard_map/ppermute | solution.py:229
  25.9 8.7 %copy-start.7 = (bf16[3,8,8,1,1]{2,0,1,4,3:T(4,128)(2,1)S(1)}, bf16[3,8,8,1,1]{2,0,1,4,3:T(4,128)(2,1)}, u32[]{:S(2)}) copy-start(bf16[3,8,8,1,1]{2,0,1,4,3:T(4,128)(2,1)} %constant.167) | copy-start | bytes 1156
  25.9 18.9 %all-to-all-start = ((bf16[16,64,256]{2,1,0:T(8,128)(2,1)}), bf16[16,64,256]{2,1,0:T(8,128)(2,1)S(1)}, u32[]{:S(2)}, u32[]{:S(2)}) async-start(bf16[16,64,256]{2,1,0:T(8,128)(2,1)} %broadcast_in_dim.8), calls=%async_computation | async-start | bytes 1048576 | tf_op jit(solution)/shard_map/all_to_all | solution.py:279
  45.6 9.2 %collective-permute-start.5 = (bf16[1024,128]{1,0:T(8,128)(2,1)}, bf16[1024,128]{1,0:T(8,128)(2,1)S(1)}, u32[]{:S(2)}, u32[]{:S(2)}) collective-permute-start(bf16[1024,128]{1,0:T(8,128)(2,1)} %get-tuple-element.42), channel_id=1, source_target_pairs={{32,64},{33,65},{34,66},{35,67},{36,68},{37,69},{38,70},{39,71},{4... | collective-permute-start | bytes 786440 | tf_op jit(solution)/shard_map/ppermute | solution.py:229
  47.7 7.2 %collective-permute-start.6 = (bf16[1024,128]{1,0:T(8,128)(2,1)}, bf16[1024,128]{1,0:T(8,128)(2,1)S(1)}, u32[]{:S(2)}, u32[]{:S(2)}) collective-permute-start(bf16[1024,128]{1,0:T(8,128)(2,1)} %get-tuple-element.41), channel_id=1, source_target_pairs={{0,32},{1,33},{2,34},{3,35},{4,36},{5,37},{6,38},{7,39},{8,40},{9,... | collective-permute-start | bytes 786440 | tf_op jit(solution)/shard_map/ppermute | solution.py:229
  48.6 4.9 %collective-permute-start.7 = (bf16[384,128]{1,0:T(8,128)(2,1)S(1)}, bf16[384,128]{1,0:T(8,128)(2,1)S(1)}, u32[]{:S(2)}, u32[]{:S(2)}) collective-permute-start(bf16[384,128]{1,0:T(8,128)(2,1)S(1)} %pad_maximum_fusion.3.more_0_), channel_id=1, source_target_pairs={{0,32},{1,33},{2,34},{3,35},{4,36},{5,37},{6,38},{7,39},{8,40},{9,... | collective-permute-start | bytes 294920 | tf_op jit(solution)/shard_map/ppermute | solution.py:229
  52.9 1.4 %collective-permute-start.8 = (bf16[384,128]{1,0:T(8,128)(2,1)S(1)}, bf16[384,128]{1,0:T(8,128)(2,1)S(1)}, u32[]{:S(2)}, u32[]{:S(2)}) collective-permute-start(bf16[384,128]{1,0:T(8,128)(2,1)S(1)} %collective-permute-done.2.more_2_), channel_id=1, source_target_pairs={{0,32},{1,33},{2,34},{3,35},{4,36},{5,37},{6,38},{7,39},{8,40},{9,... | collective-permute-start | bytes 294920 | tf_op jit(solution)/shard_map/ppermute | solution.py:229
  53.4 1.3 %collective-permute-start.9 = (bf16[384,128]{1,0:T(8,128)(2,1)S(1)}, bf16[384,128]{1,0:T(8,128)(2,1)S(1)}, u32[]{:S(2)}, u32[]{:S(2)}) collective-permute-start(bf16[384,128]{1,0:T(8,128)(2,1)S(1)} %collective-permute-done.3.more_4_), channel_id=1, source_target_pairs={{0,32},{1,33},{2,34},{3,35},{4,36},{5,37},{6,38},{7,39},{8,40},{9,... | collective-permute-start | bytes 294920 | tf_op jit(solution)/shard_map/ppermute | solution.py:229
  53.5 1.4 %collective-permute-start.10 = (bf16[384,128]{1,0:T(8,128)(2,1)S(1)}, bf16[384,128]{1,0:T(8,128)(2,1)S(1)}, u32[]{:S(2)}, u32[]{:S(2)}) collective-permute-start(bf16[384,128]{1,0:T(8,128)(2,1)S(1)} %collective-permute-done.4.more_6_), channel_id=1, source_target_pairs={{0,32},{1,33},{2,34},{3,35},{4,36},{5,37},{6,38},{7,39},{8,40},{9,... | collective-permute-start | bytes 294920 | tf_op jit(solution)/shard_map/ppermute | solution.py:229
  63.9 5.9 %collective-permute-start.11 = (bf16[384,128]{1,0:T(8,128)(2,1)S(1)}, bf16[384,128]{1,0:T(8,128)(2,1)S(1)}, u32[]{:S(2)}, u32[]{:S(2)}) collective-permute-start(bf16[384,128]{1,0:T(8,128)(2,1)S(1)} %get-tuple-element.27), channel_id=1, source_target_pairs={{32,64},{33,65},{34,66},{35,67},{36,68},{37,69},{38,70},{39,71},{4... | collective-permute-start | bytes 294920 | tf_op jit(solution)/shard_map/ppermute | solution.py:229
  67.0 2.8 %collective-permute-start.12 = (bf16[384,128]{1,0:T(8,128)(2,1)S(1)}, bf16[384,128]{1,0:T(8,128)(2,1)S(1)}, u32[]{:S(2)}, u32[]{:S(2)}) collective-permute-start(bf16[384,128]{1,0:T(8,128)(2,1)S(1)} %get-tuple-element.28), channel_id=1, source_target_pairs={{0,32},{1,33},{2,34},{3,35},{4,36},{5,37},{6,38},{7,39},{8,40},{9,... | collective-permute-start | bytes 294920 | tf_op jit(solution)/shard_map/ppermute | solution.py:229
  70.2 5.5 %collective-permute-start.14 = (bf16[384,512]{1,0:T(8,128)(2,1)S(1)}, bf16[384,512]{1,0:T(8,128)(2,1)S(1)}, u32[]{:S(2)}, u32[]{:S(2)}) collective-permute-start(bf16[384,512]{1,0:T(8,128)(2,1)S(1)} %fusion.2), channel_id=1, source_target_pairs={{0,32},{1,33},{2,34},{3,35},{4,36},{5,37},{6,38},{7,39},{8,40},{9,... | collective-permute-start | bytes 1179656 | tf_op jit(solution)/shard_map/ppermute | solution.py:229
  72.1 15.7 %all-to-all-start.1 = ((bf16[16,64,256]{2,1,0:T(8,128)(2,1)}), bf16[16,64,256]{2,1,0:T(8,128)(2,1)S(1)}, u32[]{:S(2)}, u32[]{:S(2)}) async-start(bf16[16,64,256]{2,1,0:T(8,128)(2,1)} %bitcast.35), calls=%async_computation.1 | async-start | bytes 1048576 | tf_op jit(solution)/shard_map/all_to_all | solution.py:324
  76.0 17.6 %collective-permute-start.17 = (bf16[384,128]{1,0:T(8,128)(2,1)S(1)}, bf16[384,128]{1,0:T(8,128)(2,1)S(1)}, u32[]{:S(2)}, u32[]{:S(2)}) collective-permute-start(bf16[384,128]{1,0:T(8,128)(2,1)S(1)} %get-tuple-element.44), channel_id=1, source_target_pairs={{0,192},{1,193},{2,194},{3,195},{4,196},{5,197},{6,198},{7,199},{8... | collective-permute-start | bytes 294920 | tf_op jit(solution)/shard_map/ppermute | solution.py:229
  77.2 16.4 %collective-permute-start.16 = (bf16[384,128]{1,0:T(8,128)(2,1)S(1)}, bf16[384,128]{1,0:T(8,128)(2,1)S(1)}, u32[]{:S(2)}, u32[]{:S(2)}) collective-permute-start(bf16[384,128]{1,0:T(8,128)(2,1)S(1)} %get-tuple-element.45), channel_id=1, source_target_pairs={{0,128},{1,129},{2,130},{3,131},{4,132},{5,133},{6,134},{7,135},{8... | collective-permute-start | bytes 294920 | tf_op jit(solution)/shard_map/ppermute | solution.py:229
  79.7 13.9 %collective-permute-start.15 = (bf16[384,128]{1,0:T(8,128)(2,1)S(1)}, bf16[384,128]{1,0:T(8,128)(2,1)S(1)}, u32[]{:S(2)}, u32[]{:S(2)}) collective-permute-start(bf16[384,128]{1,0:T(8,128)(2,1)S(1)} %get-tuple-element.43), channel_id=1, source_target_pairs={{0,64},{1,65},{2,66},{3,67},{4,68},{5,69},{6,70},{7,71},{8,72},{9,... | collective-permute-start | bytes 294920 | tf_op jit(solution)/shard_map/ppermute | solution.py:229
  87.8 7.7 %collective-permute-start.13 = (bf16[32,256]{1,0:T(8,128)(2,1)S(1)}, bf16[32,256]{1,0:T(8,128)(2,1)S(1)}, u32[]{:S(2)}, u32[]{:S(2)}) collective-permute-start(bf16[32,256]{1,0:T(8,128)(2,1)S(1)} %fusion.29), channel_id=1, source_target_pairs={{0,1},{1,0},{2,3},{3,2},{4,5},{5,4},{6,7},{7,6},{8,9},{9,8},{10,11... | collective-permute-start | bytes 49160 | tf_op jit(solution)/shard_map/ppermute | solution.py:229
  (11 other events, 18.0 us)

commit v5 on v4

--- a/solution.py
+++ b/solution.py
@@ -262,8 +262,11 @@
         return jnp.concatenate([part, lax.dynamic_slice(cot, (k * line, 0), (line, cols_j)), *extra], 0)
 
     even = zh == 0
-    pair = moved(edge(even, piece[:, :cols_j], piece[:, cols_j:]), lambda a, b: (a, b ^ 1))
-    next_ = moved(edge(~even), lambda a, b: (a, b + 1 if b % 2 else b - 1))
+    other = moved(piece, lambda a, b: (a, b ^ 1))
+    pair_e, next_e = edge(even), edge(~even)
+    next_e, other = lax.optimization_barrier((next_e, other))
+    pair = moved(pair_e, lambda a, b: (a, b ^ 1))
+    next_ = moved(next_e, lambda a, b: (a, b + 1 if b % 2 else b - 1))
     two = 2 * cols
     share = jnp.concatenate([pair[:two], next_[:two]], 0)
     shares = [share]
@@ -272,8 +275,6 @@
     w_src, b_src, w_tgt, b_tgt, share = lax.optimization_barrier((w_src, b_src, w_tgt, b_tgt, share))
     weights = filters(w_src, b_src, w_tgt, b_tgt, w_out, t * rows_k, rows_k * n_tgt)
 
-    start = two + line
-    other = jnp.concatenate([pair[start:start + block], pair[start + block:]], 1)
     both = jnp.where(even, jnp.concatenate([piece, other], 0), jnp.concatenate([other, piece], 0))
     plane = n_tgt // 2
     src_t = lax.all_to_all(

time: 97.3 us -> 95 us (0.976)
  waiting for transfers between devices: 26.4 us -> 19.6 us
  starting transfers between devices: 43.4 us -> 46.3 us
  local copies, waits for them, and re-layouts: 11.2 us -> 13.1 us
    all_to_all x1, waiting for transfers between devices: 7.74 us -> 0.01 us  [body(): lax.all_to_all(jnp.broadcast_to(both[None], (plane, 2 * block, pixels)),...]
    ppermute x18 -> x19, starting transfers between devices: 31.1 us -> 25.2 us  [moved(): return lax.ppermute(x, SRC + TGT, pairs)]
    all_to_all x1, starting transfers between devices: 8.71 us -> 14.2 us  [body(): lax.all_to_all(jnp.broadcast_to(both[None], (plane, 2 * block, pixels)),...]
    all_to_all x1, starting transfers between devices: 3.57 us -> 6.94 us  [body(): lax.all_to_all(part.astype(BF).reshape(plane, 2 * block, pixels), ('y', '...]
    unnamed x28 -> x26, local copies, waits for them, and re-layouts: 1.72 us -> 2.92 us
    ppermute x18 -> x19, waiting for transfers between devices: 10.6 us -> 11.7 us  [moved(): return lax.ppermute(x, SRC + TGT, pairs)]
  transfers between devices with their start and end apart: 20 -> 21, of which waited for: 8 -> 8; matrix products, arithmetic and copies ran while one was open for 11% -> 13% of each run, Pallas kernels for 0% -> 0%
where the time goes in v5:
time: 95 us; the launch traced here: 94.3 us
  starting transfers between devices  46.3 us (49%)
  waiting for transfers between devices  19.6 us (21%)
  local copies, waits for them, and re-layouts  13.1 us (14%)
  Pallas kernels  8.83 us (9%)
  matrix products  3.52 us (4%)
  other arithmetic  1.91 us (2%)
  between operations  0.99 us (1%)
    ppermute x19, starting transfers between devices, moved(): return lax.ppermute(x, SRC + TGT, pairs)  25.2 us
    all_to_all x1, starting transfers between devices, body(): lax.all_to_all(jnp.broadcast_to(both[None], (plane, 2 * block, pixels)),...  14.2 us
    ppermute x19, waiting for transfers between devices, moved(): return lax.ppermute(x, SRC + TGT, pairs)  11.7 us
    pallas_call x1, Pallas kernels, conv(): pl.pallas_call(functools.partial(conv_kernel, cols, scale), out_shape=(ja...  8.83 us
    all_to_all x1, waiting for transfers between devices, body(): lax.all_to_all(part.astype(BF).reshape(plane, 2 * block, pixels), ('y', '...  7.9 us
    all_to_all x1, starting transfers between devices, body(): lax.all_to_all(part.astype(BF).reshape(plane, 2 * block, pixels), ('y', '...  6.94 us
    unnamed x26, local copies, waits for them, and re-layouts  2.92 us
    convert_element_type x3, local copies, waits for them, and re-layouts, filters(): (0.5 * jnp.einsum('odex,dmk->omexk', flat, up)).reshape(64, 3 * TAPS * 8)  1.95 us
  transfers between devices with their start and end apart: 21, of which 8 were waited for; matrix products, arithmetic and copies ran while one was open for 13% of the time, Pallas kernels for 0%

profile of v5, /device:TPU:32, one launch (start us, length us, event | category | flops | bytes accessed | tf_op | source)
XLA Modules:
  0.0 94.3 jit_solution(17289778958193284988)
XLA Ops:
  1.4 6.3 %collective-permute-start.1 = (bf16[32,256]{1,0:T(8,128)(2,1)S(1)}, bf16[32,256]{1,0:T(8,128)(2,1)S(1)}, u32[]{:S(2)}, u32[]{:S(2)}) collective-permute-start(bf16[32,256]{1,0:T(8,128)(2,1)S(1)} %bitcast_bitcast_fusion), channel_id=1, source_target_pairs={{0,1},{1,0},{2,3},{3,2},{4,5},{5,4},{6,7},{7,6},{8,9},{9,8},{10,11... | collective-permute-start | bytes 49160 | tf_op jit(solution)/shard_map/ppermute | solution.py:229
  8.5 0.8 constant_dynamic-slice_fusion.3
  11.9 0.9 broadcast_in_dim.8
  12.8 14.2 %all-to-all-start = ((bf16[16,64,256]{2,1,0:T(8,128)(2,1)}), bf16[16,64,256]{2,1,0:T(8,128)(2,1)S(1)}, u32[]{:S(2)}, u32[]{:S(2)}) async-start(bf16[16,64,256]{2,1,0:T(8,128)(2,1)} %broadcast_in_dim.8), calls=%async_computation | async-start | bytes 1048576 | tf_op jit(solution)/shard_map/all_to_all | solution.py:280
  28.4 1.1 %collective-permute-start.3 = (bf16[384,128]{1,0:T(8,128)(2,1)S(1)}, bf16[384,128]{1,0:T(8,128)(2,1)S(1)}, u32[]{:S(2)}, u32[]{:S(2)}) collective-permute-start(bf16[384,128]{1,0:T(8,128)(2,1)S(1)} %pad_maximum_fusion.3.more_0_), channel_id=1, source_target_pairs={{0,64},{1,65},{2,66},{3,67},{4,68},{5,69},{6,70},{7,71},{8,72},{9,... | collective-permute-start | bytes 294920 | tf_op jit(solution)/shard_map/ppermute | solution.py:229
  29.5 1.5 %collective-permute-start.4 = (bf16[384,128]{1,0:T(8,128)(2,1)S(1)}, bf16[384,128]{1,0:T(8,128)(2,1)S(1)}, u32[]{:S(2)}, u32[]{:S(2)}) collective-permute-start(bf16[384,128]{1,0:T(8,128)(2,1)S(1)} %pad_maximum_fusion.3.more_0_), channel_id=1, source_target_pairs={{0,128},{1,129},{2,130},{3,131},{4,132},{5,133},{6,134},{7,135},{8... | collective-permute-start | bytes 294920 | tf_op jit(solution)/shard_map/ppermute | solution.py:229
  31.0 1.0 %collective-permute-start.5 = (bf16[384,128]{1,0:T(8,128)(2,1)S(1)}, bf16[384,128]{1,0:T(8,128)(2,1)S(1)}, u32[]{:S(2)}, u32[]{:S(2)}) collective-permute-start(bf16[384,128]{1,0:T(8,128)(2,1)S(1)} %pad_maximum_fusion.3.more_0_), channel_id=1, source_target_pairs={{0,192},{1,193},{2,194},{3,195},{4,196},{5,197},{6,198},{7,199},{8... | collective-permute-start | bytes 294920 | tf_op jit(solution)/shard_map/ppermute | solution.py:229
  33.9 1.2 %fusion.3 = bf16[3,3,2,4,4,8,8]{6,5,4,3,2,0,1:T(8,128)(2,1)} fusion(bf16[3,3,2,4,4,8,1,1]{5,1,0,4,3,2,7,6:T(4,128)(2,1)S(1)} %copy-done.12, bf16[8,3,3,3,3,1,1,1]{0,4,3,2,1,7,6,5:T(4,128)(2,1)S(1)} %bitcast.117), kind=kOutput, calls=%fused_computation.8 | convolution fusion | flops 331776 | bytes 42768 | tf_op jit(solution)/shard_map/odeab,desklm->basklom/dot_general | solution.py:199
  35.3 1.6 %collective-permute-done.4.more_4_ = bf16[384,128]{1,0:T(8,128)(2,1)S(1)} collective-permute-done((bf16[384,128]{1,0:T(8,128)(2,1)S(1)}, bf16[384,128]{1,0:T(8,128)(2,1)S(1)}, u32[]{:S(2)}, u32[]{:S(2)}) %collective-permute-start.4) | collective-permute-done | bytes 98336 | tf_op jit(solution)/shard_map/ppermute | solution.py:229
  36.9 2.5 %collective-permute-done.5.more_6_ = bf16[384,128]{1,0:T(8,128)(2,1)S(1)} collective-permute-done((bf16[384,128]{1,0:T(8,128)(2,1)S(1)}, bf16[384,128]{1,0:T(8,128)(2,1)S(1)}, u32[]{:S(2)}, u32[]{:S(2)}) %collective-permute-start.5) | collective-permute-done | bytes 98336 | tf_op jit(solution)/shard_map/ppermute | solution.py:229
  39.4 0.9 broadcast_select_fusion
  40.3 2.0 %collective-permute-start.6 = (bf16[1024,128]{1,0:T(8,128)(2,1)}, bf16[1024,128]{1,0:T(8,128)(2,1)S(1)}, u32[]{:S(2)}, u32[]{:S(2)}) collective-permute-start(bf16[1024,128]{1,0:T(8,128)(2,1)} %get-tuple-element.46), channel_id=1, source_target_pairs={{32,64},{33,65},{34,66},{35,67},{36,68},{37,69},{38,70},{39,71},{4... | collective-permute-start | bytes 786440 | tf_op jit(solution)/shard_map/ppermute | solution.py:229
  42.3 1.2 %collective-permute-start.7 = (bf16[1024,128]{1,0:T(8,128)(2,1)}, bf16[1024,128]{1,0:T(8,128)(2,1)S(1)}, u32[]{:S(2)}, u32[]{:S(2)}) collective-permute-start(bf16[1024,128]{1,0:T(8,128)(2,1)} %get-tuple-element.45), channel_id=1, source_target_pairs={{0,32},{1,33},{2,34},{3,35},{4,36},{5,37},{6,38},{7,39},{8,40},{9,... | collective-permute-start | bytes 786440 | tf_op jit(solution)/shard_map/ppermute | solution.py:229
  43.9 1.5 %copy.22 = bf16[8,8,3,10,8]{1,0,4,3,2:T(8,128)(2,1)S(1)} copy(bf16[8,8,3,10,8]{3,4,1,2,0:T(8,128)(2,1)S(1)} %fusion.6) | data formatting | bytes 61440 | tf_op jit(solution)/shard_map/convert_element_type | solution.py:190
  45.8 1.2 %copy.24 = bf16[3,3,2,4,4,8,8]{6,5,4,3,2,1,0:T(8,128)(2,1)S(1)} copy(bf16[3,3,2,4,4,8,8]{6,5,4,3,2,0,1:T(8,128)(2,1)} %fusion.3) | data formatting | bytes 73728 | tf_op jit(solution)/shard_map/convert_element_type | solution.py:199
  50.0 8.8 %shard_map.139 = (bf16[768,128]{1,0:T(8,128)(2,1)}, f32[384,256]{1,0:T(8,128)S(1)}, bf16[384,128]{1,0:T(8,128)(2,1)S(1)}, bf16[384,128]{1,0:T(8,128)(2,1)S(1)}) custom-call(s32[3]{0:T(128)S(1)} %pad_add_fusion.spot_ref, bf16[64,240]{1,0:T(8,128)(2,1)S(1)} %copy.25.wf_ref, bf16[72,256]{1,0:T(8,128)(2,1)S(1)} %convert_element_type.68.wb_ref, ...), custom_call_target="tpu_custom_call" | custom-call | flops 4000000000 | bytes 4000000 | tf_op jit(solution)/shard_map/pallas_call | solution.py:157
  58.8 2.9 %collective-permute-start.12 = (bf16[384,128]{1,0:T(8,128)(2,1)S(1)}, bf16[384,128]{1,0:T(8,128)(2,1)S(1)}, u32[]{:S(2)}, u32[]{:S(2)}) collective-permute-start(bf16[384,128]{1,0:T(8,128)(2,1)S(1)} %get-tuple-element.31), channel_id=1, source_target_pairs={{32,64},{33,65},{34,66},{35,67},{36,68},{37,69},{38,70},{39,71},{4... | collective-permute-start | bytes 294920 | tf_op jit(solution)/shard_map/ppermute | solution.py:229
  61.8 2.9 %collective-permute-done.12 = bf16[384,128]{1,0:T(8,128)(2,1)S(1)} collective-permute-done((bf16[384,128]{1,0:T(8,128)(2,1)S(1)}, bf16[384,128]{1,0:T(8,128)(2,1)S(1)}, u32[]{:S(2)}, u32[]{:S(2)}) %collective-permute-start.12) | collective-permute-done | bytes 98336 | tf_op jit(solution)/shard_map/ppermute | solution.py:229
  66.0 1.0 %copy.26 = bf16[1024,256]{1,0:T(8,128)(2,1)} copy(bf16[1024,256]{0,1:T(8,128)(2,1)S(1)} %fusion.5) | data formatting | bytes 1048576 | tf_op jit(solution)/shard_map/convert_element_type | solution.py:326
  67.0 6.9 %all-to-all-start.1 = ((bf16[16,64,256]{2,1,0:T(8,128)(2,1)}), bf16[16,64,256]{2,1,0:T(8,128)(2,1)S(1)}, u32[]{:S(2)}, u32[]{:S(2)}) async-start(bf16[16,64,256]{2,1,0:T(8,128)(2,1)} %bitcast.35), calls=%async_computation.1 | async-start | bytes 1048576 | tf_op jit(solution)/shard_map/all_to_all | solution.py:325
  74.8 3.0 %collective-permute-start.17 = (bf16[384,128]{1,0:T(8,128)(2,1)S(1)}, bf16[384,128]{1,0:T(8,128)(2,1)S(1)}, u32[]{:S(2)}, u32[]{:S(2)}) collective-permute-start(bf16[384,128]{1,0:T(8,128)(2,1)S(1)} %get-tuple-element.49), channel_id=1, source_target_pairs={{0,128},{1,129},{2,130},{3,131},{4,132},{5,133},{6,134},{7,135},{8... | collective-permute-start | bytes 294920 | tf_op jit(solution)/shard_map/ppermute | solution.py:229
  77.9 7.9 %all-to-all-done.1 = bf16[16,64,256]{2,1,0:T(8,128)(2,1)S(1)} async-done(((bf16[16,64,256]{2,1,0:T(8,128)(2,1)}), bf16[16,64,256]{2,1,0:T(8,128)(2,1)S(1)}, u32[]{:S(2)}, u32[]{:S(2)}) %all-to-all-start.1) | async-done | bytes 524320 | tf_op jit(solution)/shard_map/all_to_all | solution.py:325
  85.9 3.2 %collective-permute-start.14 = (bf16[32,256]{1,0:T(8,128)(2,1)S(1)}, bf16[32,256]{1,0:T(8,128)(2,1)S(1)}, u32[]{:S(2)}, u32[]{:S(2)}) collective-permute-start(bf16[32,256]{1,0:T(8,128)(2,1)S(1)} %fusion.29), channel_id=1, source_target_pairs={{0,1},{1,0},{2,3},{3,2},{4,5},{5,4},{6,7},{7,6},{8,9},{9,8},{10,11... | collective-permute-start | bytes 49160 | tf_op jit(solution)/shard_map/ppermute | solution.py:229
  89.8 3.8 %collective-permute-done.14 = bf16[32,256]{1,0:T(8,128)(2,1)S(1)} collective-permute-done((bf16[32,256]{1,0:T(8,128)(2,1)S(1)}, bf16[32,256]{1,0:T(8,128)(2,1)S(1)}, u32[]{:S(2)}, u32[]{:S(2)}) %collective-permute-start.14) | collective-permute-done | bytes 16416 | tf_op jit(solution)/shard_map/ppermute | solution.py:229
  (89 shorter events, 14.9 us)
Async XLA Ops:
  0.6 31.4 %copy-start = (bf16[8,8,3,3]{1,0,3,2:T(8,128)(2,1)S(1)}, bf16[8,8,3,3]{1,0,3,2:T(8,128)(2,1)}, u32[]{:S(2)}) copy-start(bf16[8,8,3,3]{1,0,3,2:T(8,128)(2,1)} %param.16) | copy-start | bytes 3460
  1.4 9.8 %collective-permute-start.1 = (bf16[32,256]{1,0:T(8,128)(2,1)S(1)}, bf16[32,256]{1,0:T(8,128)(2,1)S(1)}, u32[]{:S(2)}, u32[]{:S(2)}) collective-permute-start(bf16[32,256]{1,0:T(8,128)(2,1)S(1)} %bitcast_bitcast_fusion), channel_id=1, source_target_pairs={{0,1},{1,0},{2,3},{3,2},{4,5},{5,4},{6,7},{7,6},{8,9},{9,8},{10,11... | collective-permute-start | bytes 49160 | tf_op jit(solution)/shard_map/ppermute | solution.py:229
  9.3 17.6 %collective-permute-start = (bf16[384,128]{1,0:T(8,128)(2,1)S(1)}, bf16[384,128]{1,0:T(8,128)(2,1)S(1)}, u32[]{:S(2)}, u32[]{:S(2)}) collective-permute-start(bf16[384,128]{1,0:T(8,128)(2,1)S(1)} %pad_maximum_fusion.1), channel_id=1, source_target_pairs={{0,1},{1,0},{2,3},{3,2},{4,5},{5,4},{6,7},{7,6},{8,9},{9,8},{10,11... | collective-permute-start | bytes 294920 | tf_op jit(solution)/shard_map/ppermute | solution.py:229
  11.2 16.4 %collective-permute-start.2 = (bf16[384,128]{1,0:T(8,128)(2,1)S(1)}, bf16[384,128]{1,0:T(8,128)(2,1)S(1)}, u32[]{:S(2)}, u32[]{:S(2)}) collective-permute-start(bf16[384,128]{1,0:T(8,128)(2,1)S(1)} %pad_maximum_fusion.2), channel_id=1, source_target_pairs={{1,2},{2,1},{3,4},{4,3},{5,6},{6,5},{7,8},{8,7},{9,10},{10,9},{11,... | collective-permute-start | bytes 294920 | tf_op jit(solution)/shard_map/ppermute | solution.py:229
  12.8 26.7 %all-to-all-start = ((bf16[16,64,256]{2,1,0:T(8,128)(2,1)}), bf16[16,64,256]{2,1,0:T(8,128)(2,1)S(1)}, u32[]{:S(2)}, u32[]{:S(2)}) async-start(bf16[16,64,256]{2,1,0:T(8,128)(2,1)} %broadcast_in_dim.8), calls=%async_computation | async-start | bytes 1048576 | tf_op jit(solution)/shard_map/all_to_all | solution.py:280
  28.4 3.6 %copy-start.7 = (bf16[8,3,3]{0,2,1:T(4,128)(2,1)S(1)}, bf16[8,3,3]{0,2,1:T(4,128)(2,1)}, u32[]{:S(2)}) copy-start(bf16[8,3,3]{0,2,1:T(4,128)(2,1)} %param.14) | copy-start | bytes 436
  28.4 6.8 %collective-permute-start.3 = (bf16[384,128]{1,0:T(8,128)(2,1)S(1)}, bf16[384,128]{1,0:T(8,128)(2,1)S(1)}, u32[]{:S(2)}, u32[]{:S(2)}) collective-permute-start(bf16[384,128]{1,0:T(8,128)(2,1)S(1)} %pad_maximum_fusion.3.more_0_), channel_id=1, source_target_pairs={{0,64},{1,65},{2,66},{3,67},{4,68},{5,69},{6,70},{7,71},{8,72},{9,... | collective-permute-start | bytes 294920 | tf_op jit(solution)/shard_map/ppermute | solution.py:229
  29.5 7.4 %collective-permute-start.4 = (bf16[384,128]{1,0:T(8,128)(2,1)S(1)}, bf16[384,128]{1,0:T(8,128)(2,1)S(1)}, u32[]{:S(2)}, u32[]{:S(2)}) collective-permute-start(bf16[384,128]{1,0:T(8,128)(2,1)S(1)} %pad_maximum_fusion.3.more_0_), channel_id=1, source_target_pairs={{0,128},{1,129},{2,130},{3,131},{4,132},{5,133},{6,134},{7,135},{8... | collective-permute-start | bytes 294920 | tf_op jit(solution)/shard_map/ppermute | solution.py:229
  31.0 8.4 %collective-permute-start.5 = (bf16[384,128]{1,0:T(8,128)(2,1)S(1)}, bf16[384,128]{1,0:T(8,128)(2,1)S(1)}, u32[]{:S(2)}, u32[]{:S(2)}) collective-permute-start(bf16[384,128]{1,0:T(8,128)(2,1)S(1)} %pad_maximum_fusion.3.more_0_), channel_id=1, source_target_pairs={{0,192},{1,193},{2,194},{3,195},{4,196},{5,197},{6,198},{7,199},{8... | collective-permute-start | bytes 294920 | tf_op jit(solution)/shard_map/ppermute | solution.py:229
  40.3 9.5 %collective-permute-start.6 = (bf16[1024,128]{1,0:T(8,128)(2,1)}, bf16[1024,128]{1,0:T(8,128)(2,1)S(1)}, u32[]{:S(2)}, u32[]{:S(2)}) collective-permute-start(bf16[1024,128]{1,0:T(8,128)(2,1)} %get-tuple-element.46), channel_id=1, source_target_pairs={{32,64},{33,65},{34,66},{35,67},{36,68},{37,69},{38,70},{39,71},{4... | collective-permute-start | bytes 786440 | tf_op jit(solution)/shard_map/ppermute | solution.py:229
  42.3 7.5 %collective-permute-start.7 = (bf16[1024,128]{1,0:T(8,128)(2,1)}, bf16[1024,128]{1,0:T(8,128)(2,1)S(1)}, u32[]{:S(2)}, u32[]{:S(2)}) collective-permute-start(bf16[1024,128]{1,0:T(8,128)(2,1)} %get-tuple-element.45), channel_id=1, source_target_pairs={{0,32},{1,33},{2,34},{3,35},{4,36},{5,37},{6,38},{7,39},{8,40},{9,... | collective-permute-start | bytes 786440 | tf_op jit(solution)/shard_map/ppermute | solution.py:229
  43.5 4.9 %collective-permute-start.8 = (bf16[384,128]{1,0:T(8,128)(2,1)S(1)}, bf16[384,128]{1,0:T(8,128)(2,1)S(1)}, u32[]{:S(2)}, u32[]{:S(2)}) collective-permute-start(bf16[384,128]{1,0:T(8,128)(2,1)S(1)} %pad_maximum_fusion.3.more_0_), channel_id=1, source_target_pairs={{0,32},{1,33},{2,34},{3,35},{4,36},{5,37},{6,38},{7,39},{8,40},{9,... | collective-permute-start | bytes 294920 | tf_op jit(solution)/shard_map/ppermute | solution.py:229
  45.8 4.1 %copy-start.4 = (bf16[4,96,1024]{2,1,0:T(8,128)(2,1)S(1)}, bf16[4,96,1024]{2,1,0:T(8,128)(2,1)}, u32[]{:S(2)}) copy-start(bf16[4,96,1024]{2,1,0:T(8,128)(2,1)} %param.13) | copy-start | bytes 2359300
  47.9 1.4 %collective-permute-start.9 = (bf16[384,128]{1,0:T(8,128)(2,1)S(1)}, bf16[384,128]{1,0:T(8,128)(2,1)S(1)}, u32[]{:S(2)}, u32[]{:S(2)}) collective-permute-start(bf16[384,128]{1,0:T(8,128)(2,1)S(1)} %collective-permute-done.3.more_2_), channel_id=1, source_target_pairs={{0,32},{1,33},{2,34},{3,35},{4,36},{5,37},{6,38},{7,39},{8,40},{9,... | collective-permute-start | bytes 294920 | tf_op jit(solution)/shard_map/ppermute | solution.py:229
  48.4 1.3 %collective-permute-start.10 = (bf16[384,128]{1,0:T(8,128)(2,1)S(1)}, bf16[384,128]{1,0:T(8,128)(2,1)S(1)}, u32[]{:S(2)}, u32[]{:S(2)}) collective-permute-start(bf16[384,128]{1,0:T(8,128)(2,1)S(1)} %collective-permute-done.4.more_4_), channel_id=1, source_target_pairs={{0,32},{1,33},{2,34},{3,35},{4,36},{5,37},{6,38},{7,39},{8,40},{9,... | collective-permute-start | bytes 294920 | tf_op jit(solution)/shard_map/ppermute | solution.py:229
  48.5 1.4 %collective-permute-start.11 = (bf16[384,128]{1,0:T(8,128)(2,1)S(1)}, bf16[384,128]{1,0:T(8,128)(2,1)S(1)}, u32[]{:S(2)}, u32[]{:S(2)}) collective-permute-start(bf16[384,128]{1,0:T(8,128)(2,1)S(1)} %collective-permute-done.5.more_6_), channel_id=1, source_target_pairs={{0,32},{1,33},{2,34},{3,35},{4,36},{5,37},{6,38},{7,39},{8,40},{9,... | collective-permute-start | bytes 294920 | tf_op jit(solution)/shard_map/ppermute | solution.py:229
  58.8 5.9 %collective-permute-start.12 = (bf16[384,128]{1,0:T(8,128)(2,1)S(1)}, bf16[384,128]{1,0:T(8,128)(2,1)S(1)}, u32[]{:S(2)}, u32[]{:S(2)}) collective-permute-start(bf16[384,128]{1,0:T(8,128)(2,1)S(1)} %get-tuple-element.31), channel_id=1, source_target_pairs={{32,64},{33,65},{34,66},{35,67},{36,68},{37,69},{38,70},{39,71},{4... | collective-permute-start | bytes 294920 | tf_op jit(solution)/shard_map/ppermute | solution.py:229
  61.7 3.0 %collective-permute-start.13 = (bf16[384,128]{1,0:T(8,128)(2,1)S(1)}, bf16[384,128]{1,0:T(8,128)(2,1)S(1)}, u32[]{:S(2)}, u32[]{:S(2)}) collective-permute-start(bf16[384,128]{1,0:T(8,128)(2,1)S(1)} %get-tuple-element.32), channel_id=1, source_target_pairs={{0,32},{1,33},{2,34},{3,35},{4,36},{5,37},{6,38},{7,39},{8,40},{9,... | collective-permute-start | bytes 294920 | tf_op jit(solution)/shard_map/ppermute | solution.py:229
  65.1 8.9 %collective-permute-start.15 = (bf16[384,512]{1,0:T(8,128)(2,1)S(1)}, bf16[384,512]{1,0:T(8,128)(2,1)S(1)}, u32[]{:S(2)}, u32[]{:S(2)}) collective-permute-start(bf16[384,512]{1,0:T(8,128)(2,1)S(1)} %fusion.2), channel_id=1, source_target_pairs={{0,32},{1,33},{2,34},{3,35},{4,36},{5,37},{6,38},{7,39},{8,40},{9,... | collective-permute-start | bytes 1179656 | tf_op jit(solution)/shard_map/ppermute | solution.py:229
  67.0 18.8 %all-to-all-start.1 = ((bf16[16,64,256]{2,1,0:T(8,128)(2,1)}), bf16[16,64,256]{2,1,0:T(8,128)(2,1)S(1)}, u32[]{:S(2)}, u32[]{:S(2)}) async-start(bf16[16,64,256]{2,1,0:T(8,128)(2,1)} %bitcast.35), calls=%async_computation.1 | async-start | bytes 1048576 | tf_op jit(solution)/shard_map/all_to_all | solution.py:325
  74.3 14.8 %collective-permute-start.18 = (bf16[384,128]{1,0:T(8,128)(2,1)S(1)}, bf16[384,128]{1,0:T(8,128)(2,1)S(1)}, u32[]{:S(2)}, u32[]{:S(2)}) collective-permute-start(bf16[384,128]{1,0:T(8,128)(2,1)S(1)} %get-tuple-element.48), channel_id=1, source_target_pairs={{0,192},{1,193},{2,194},{3,195},{4,196},{5,197},{6,198},{7,199},{8... | collective-permute-start | bytes 294920 | tf_op jit(solution)/shard_map/ppermute | solution.py:229
  74.8 14.3 %collective-permute-start.17 = (bf16[384,128]{1,0:T(8,128)(2,1)S(1)}, bf16[384,128]{1,0:T(8,128)(2,1)S(1)}, u32[]{:S(2)}, u32[]{:S(2)}) collective-permute-start(bf16[384,128]{1,0:T(8,128)(2,1)S(1)} %get-tuple-element.49), channel_id=1, source_target_pairs={{0,128},{1,129},{2,130},{3,131},{4,132},{5,133},{6,134},{7,135},{8... | collective-permute-start | bytes 294920 | tf_op jit(solution)/shard_map/ppermute | solution.py:229
  77.8 11.3 %collective-permute-start.16 = (bf16[384,128]{1,0:T(8,128)(2,1)S(1)}, bf16[384,128]{1,0:T(8,128)(2,1)S(1)}, u32[]{:S(2)}, u32[]{:S(2)}) collective-permute-start(bf16[384,128]{1,0:T(8,128)(2,1)S(1)} %get-tuple-element.47), channel_id=1, source_target_pairs={{0,64},{1,65},{2,66},{3,67},{4,68},{5,69},{6,70},{7,71},{8,72},{9,... | collective-permute-start | bytes 294920 | tf_op jit(solution)/shard_map/ppermute | solution.py:229
  85.9 7.7 %collective-permute-start.14 = (bf16[32,256]{1,0:T(8,128)(2,1)S(1)}, bf16[32,256]{1,0:T(8,128)(2,1)S(1)}, u32[]{:S(2)}, u32[]{:S(2)}) collective-permute-start(bf16[32,256]{1,0:T(8,128)(2,1)S(1)} %fusion.29), channel_id=1, source_target_pairs={{0,1},{1,0},{2,3},{3,2},{4,5},{5,4},{6,7},{7,6},{8,9},{9,8},{10,11... | collective-permute-start | bytes 49160 | tf_op jit(solution)/shard_map/ppermute | solution.py:229
  (11 other events, 14.9 us)

commit v6 on v5

--- a/solution.py
+++ b/solution.py
@@ -62,8 +62,8 @@
     fill(over_all, (2, 3, 4, 5))
     fill(over_pieces, (0, 1, 6, 7))
     zeros = jnp.zeros((cols, 128), F32)
-    line = pl.ds(2 * cols, 2 * cols)
-    pair, next_ = pair_ref[line, :].astype(F32), next_ref[line, :].astype(F32)
+    pair = pair_ref[pl.ds(2 * cols, 2 * cols), :].astype(F32)
+    next_ = next_ref[pl.ds(0, 2 * cols), :].astype(F32)
     cotf[pl.ds(0, 2 * cols), :] = jnp.where(even, next_, pair)
     cotf[pl.ds(2 * cols, 8 * cols), :] = cot_ref[...].astype(F32)
     cotf[pl.ds(10 * cols, 2 * cols), :] = jnp.where(even, pair, next_)
@@ -79,7 +79,7 @@
         gp[pl.ds(end * 64, 64), :] = jnp.zeros((64, 256), BF)
 
     def spread(l, _):
-        at = pl.multiple_of(l * 8, 8)
+        at = l * 8
         taps = []
         for i in range(4):
             v = cs[i, pl.ds(at, 8), :]
@@ -87,24 +87,23 @@
         for i in range(2):
             block = [taps[i + a][b] for a in range(3) for b in range(3)]
             block.append(jnp.zeros((8, 128), F32))
-            rows[pl.ds(pl.multiple_of((l + 1) * group, 16), group), pl.ds(i * 128, 128)] = jnp.concatenate(block, 0).astype(BF)
+            rows[pl.ds((l + 1) * group, group), pl.ds(i * 128, 128)] = jnp.concatenate(block, 0).astype(BF)
         return 0
 
-    lax.fori_loop(0, cols, spread, 0, unroll=48)
 
     wf = wf_ref[...]
     wb = wb_ref[...]
 
     def forward(l, _):
-        kind = jnp.where(l == 0, 0, jnp.where(l == cols - 1, 2, 1))
-        window = rows[pl.ds(pl.multiple_of(l * group, 16), 3 * group), :]
+        kind = 0 if l == 0 else 2 if l == cols - 1 else 1
+        window = rows[pl.ds(l * group, 3 * group), :]
         u = jnp.dot(wf, window, preferred_element_type=F32)
-        u = u + bias_ref[pl.ds(pl.multiple_of(kind * 64, 64), 64), :]
+        u = u + bias_ref[pl.ds(kind * 64, 64), :]
         th = jnp.tanh(u)
         q = u * th
         g = (1.0 + u) + th * (1.0 - q)
         s = u + q
-        at = pl.multiple_of(l * 8, 8)
+        at = l * 8
         cot = jnp.concatenate([cots[0, pl.ds(at, 8), :], cots[1, pl.ds(at, 8), :]], 1)
         total = jnp.zeros((8, 256), F32)
         out = []
@@ -112,17 +111,16 @@
             w = bias_ref[pl.ds(192 + o * 8, 8), :]
             total = total + w * s[o * 8:o * 8 + 8]
             out.append(g[o * 8:o * 8 + 8] * (cot * (0.5 * w)))
-        gp[pl.ds(pl.multiple_of((l + 1) * 64, 64), 64), :] = jnp.concatenate(out, 0).astype(BF)
+        gp[pl.ds((l + 1) * 64, 64), :] = jnp.concatenate(out, 0).astype(BF)
         sc[0, pl.ds(at, 8), :] = total[:, :128]
         sc[1, pl.ds(at, 8), :] = total[:, 128:]
         return 0
 
-    lax.fori_loop(0, cols, forward, 0, unroll=96)
 
     def backward(m, _):
-        window = gp[pl.ds(pl.multiple_of(m * 128, 128), 256), :]
+        window = gp[pl.ds(m * 128, 256), :]
         t = jnp.dot(wb, window, preferred_element_type=F32)
-        at = pl.multiple_of(m * 8, 8)
+        at = m * 8
         for io in range(4):
             part = []
             for b in range(3):
@@ -135,7 +133,14 @@
             gs[io, pl.ds(at, 8), :] = shift_lanes(part[0], -1) + part[1] + shift_lanes(part[2], 1)
         return 0
 
-    lax.fori_loop(0, cols // 2, backward, 0, unroll=48)
+    lag = 8
+    for l in range(cols + 2 * lag):
+        if l < cols:
+            spread(l, 0)
+        if lag <= l < cols + lag:
+            forward(l - lag, 0)
+        if l >= 2 * lag and l % 2 == 1:
+            backward((l - 2 * lag) // 2, 0)
 
     for k in range(4):
         for i in range(2):
@@ -162,7 +167,7 @@
             jax.ShapeDtypeStruct((n, 128), BF),
             jax.ShapeDtypeStruct((n, 128), BF),
         ),
-        in_specs=[smem] + [vmem] * (10 + len(halos)),
+        in_specs=[smem] + [pl.BlockSpec()] * 3 + [vmem] * (7 + len(halos)),
         out_specs=(vmem,) * 4,
         scratch_shapes=[
             pltpu.VMEM((4, 8 * cols, 128), F32),
@@ -178,39 +183,104 @@
     )(spot, *weights, tgt, src, far, near, pair, next_, cot, *halos)
 
 
+def tables():
+    spread = np.zeros((9, 8, 256), np.float32)
+    mask = np.zeros((9, 8, 256), np.float32)
+    place = np.zeros((9, 8, 8, 256), np.float32)
+    for d in range(3):
+        for e in range(3):
+            for m in range(1, 7):
+                for x in range(9):
+                    lane = (e * TAPS + x) * 8 + m + d - 1
+                    spread[x, m, (e * TAPS + x) * 8:(e * TAPS + x) * 8 + 8] = 1
+                    mask[d * 3 + e, m, lane] = 1
+            for s in range(2):
+                for k in range(4):
+                    for o in range(8):
+                        place[d * 3 + e, o, s * 4 + k, (s + 2 - e) * 64 + o * 8 + k + 3 - d] = 1
+    return (
+        jnp.asarray(spread.reshape(3, 3, 2048), BF),
+        jnp.asarray(mask.reshape(9, 1, 2048), F32),
+        jnp.asarray(place.reshape(9, 8, 2048), BF),
+    )
+
+
+def filters_kernel(
+    total_rows,
+    row_ref, wt_ref, ws_ref, b_src_ref, b_tgt_ref, w_out_ref, spread_ref, mask_ref, place_ref,
+    wf_ref, wb_ref, bias_ref, forward, adjoint, bias,
+):
+    over_first = (((0,), (0,)), ((), ()))
+    source = lanes = None
+    for a in range(3):
+        part = lax.dot_general(ws_ref[a], spread_ref[a], over_first, preferred_element_type=F32)
+        source = part if source is None else source + part
+    out = None
+    for n in range(9):
+        part = jnp.dot(wt_ref[n], (source * mask_ref[n]).astype(BF), preferred_element_type=F32)
+        out = part if out is None else out + part
+        part = lax.dot_general(wt_ref[n], place_ref[n], over_first, preferred_element_type=F32)
+        lanes = part if lanes is None else lanes + part
+    for m in range(8):
+        for h in range(2):
+            at = m * 256 + h * 128
+            forward[h, pl.ds(m, 8, stride=8), :] = 0.5 * out[:, at:at + 128]
+    wf_ref[...] = jnp.concatenate([forward[0], forward[1, :, :3 * TAPS * 8 - 128]], 1).astype(BF)
+    lanes = lanes.astype(BF)
+    for a in range(3):
+        part = jnp.dot(ws_ref[a], lanes, preferred_element_type=F32)
+        for c in range(8):
+            for h in range(2):
+                at = c * 256 + h * 128
+                adjoint[h, pl.ds(a * 8 + c, 3, stride=24), :] = part[:, at:at + 128]
+    wb_ref[...] = jnp.concatenate([adjoint[0], adjoint[1]], 1).astype(BF)
+
+    def column(ref):
+        v = jnp.broadcast_to(ref[...], (8, 8))
+        same = lax.broadcasted_iota(jnp.int32, (8, 8), 0) == lax.broadcasted_iota(jnp.int32, (8, 8), 1)
+        return jnp.sum(jnp.where(same, v, 0.0), 1, keepdims=True)
+
+    b_tgt, w_out = column(b_tgt_ref), column(w_out_ref)
+    lift = [jnp.sum(wt_ref[n].astype(F32) * b_src_ref[...], 1, keepdims=True) for n in range(9)]
+    for kind in range(3):
+        along = []
+        for d in range(3):
+            parts = [lift[d * 3 + e] for e in range(3) if (kind, e) not in ((0, 0), (2, 2))]
+            along.append(functools.reduce(jnp.add, parts))
+        for m in range(8):
+            total = b_tgt
+            for d in range(3):
+                if 1 <= m <= 6:
+                    row = row_ref[0] + (m + d - 3)
+                    inside = jnp.logical_and(row >= 0, row < total_rows)
+                    total = total + jnp.where(inside, along[d], 0.0)
+            bias[pl.ds(kind * 64 + m, 8, stride=8), :] = jnp.broadcast_to(0.5 * total, (8, 128))
+    for m in range(8):
+        bias[pl.ds(192 + m, 8, stride=8), :] = jnp.broadcast_to(w_out, (8, 128))
+    bias_ref[...] = jnp.concatenate([bias[...], bias[...]], 1)
+
+
 def filters(w_src, b_src, w_tgt, b_tgt, w_out, first_row, total_rows):
-    both = jnp.einsum(
-        "opde,pab->odeab", w_tgt.astype(F32), w_src.astype(F32), precision=lax.Precision.HIGHEST
-    )
-    up = np.zeros((3, 8, 8), np.float32)
-    for d in range(3):
-        for m in range(1, 7):
-            up[d, m, m + d - 1] = 1
-    flat = jnp.pad(both.reshape(8, 3, 3, 9), ((0, 0), (0, 0), (0, 0), (0, TAPS - 9)))
-    wf = (0.5 * jnp.einsum("odex,dmk->omexk", flat, up)).reshape(64, 3 * TAPS * 8).astype(BF)
-    back = np.zeros((3, 4, 8), np.float32)
-    side = np.zeros((3, 2, 4), np.float32)
-    for d in range(3):
-        for k in range(4):
-            back[d, k, k + 3 - d] = 1
-        for s in range(2):
-            side[d, s, s + 2 - d] = 1
-    spots = np.einsum("dkm,esl->desklm", back, side)
-    wb = jnp.einsum("odeab,desklm->baskyom".replace("y", "l"), both, spots).reshape(72, 256).astype(BF)
-    lift = jnp.einsum(
-        "opde,p->ode", w_tgt.astype(F32), b_src, precision=lax.Precision.HIGHEST
-    )
-    row = first_row - 2 + jnp.arange(8)
-    inside = ((row >= 0) & (row < total_rows)).astype(F32)
-    edge = np.ones((3, 3), np.float32)
-    edge[0, 0] = 0
-    edge[2, 2] = 0
-    along = jnp.einsum("ode,te->tod", lift, edge, precision=lax.Precision.HIGHEST)
-    reach = jnp.einsum("dmk,k->md", up, inside, precision=lax.Precision.HIGHEST)
-    bias = b_tgt[None, :, None] + jnp.einsum("tod,md->tom", along, reach, precision=lax.Precision.HIGHEST)
-    bias = jnp.concatenate([(0.5 * bias).reshape(192), jnp.repeat(w_out, 8)])
-    bias = jnp.broadcast_to(bias[:, None], (256, 256))
-    return wf, wb, bias
+    vmem = pl.BlockSpec(memory_space=pltpu.VMEM)
+    smem = pl.BlockSpec(memory_space=pltpu.SMEM)
+    return pl.pallas_call(
+        functools.partial(filters_kernel, total_rows),
+        out_shape=(
+            jax.ShapeDtypeStruct((64, 3 * TAPS * 8), BF),
+            jax.ShapeDtypeStruct((72, 256), BF),
+            jax.ShapeDtypeStruct((256, 256), F32),
+        ),
+        in_specs=[smem] + [vmem] * 8,
+        out_specs=(vmem,) * 3,
+        scratch_shapes=[pltpu.VMEM((2, 64, 128), F32), pltpu.VMEM((2, 72, 128), F32), pltpu.VMEM((256, 128), F32)],
+        cost_estimate=pl.CostEstimate(flops=10**9, transcendentals=0, bytes_accessed=10**6),
+    )(
+        first_row.astype(jnp.int32)[None],
+        w_tgt.transpose(2, 3, 0, 1).reshape(9, 8, 8),
+        w_src.transpose(1, 2, 0),
+        b_src[None], b_tgt[None], w_out[None],
+        *tables(),
+    )
 
 
 SRC = ("z", "core")
@@ -255,24 +325,26 @@
     piece = src_feat.reshape(pixels, block).T
     line = cols * rows_i
 
-    def edge(last, *extra):
+    def edge(last, swap):
         k = jnp.where(last, rows_k - 2, 0)
         part = lax.dynamic_slice(tgt_feat, (k, 0, s * width), (2, cols, width)).reshape(2 * cols, width)
         k = jnp.where(last, rows_k - 1, 0)
-        return jnp.concatenate([part, lax.dynamic_slice(cot, (k * line, 0), (line, cols_j)), *extra], 0)
+        parts = [part, lax.dynamic_slice(cot, (k * line, 0), (line, cols_j))]
+        return jnp.concatenate(parts[::-1] if swap else parts, 0)
 
     even = zh == 0
     other = moved(piece, lambda a, b: (a, b ^ 1))
-    pair_e, next_e = edge(even), edge(~even)
+    pair_e, next_e = edge(even, False), edge(~even, True)
     next_e, other = lax.optimization_barrier((next_e, other))
     pair = moved(pair_e, lambda a, b: (a, b ^ 1))
     next_ = moved(next_e, lambda a, b: (a, b + 1 if b % 2 else b - 1))
-    two = 2 * cols
-    share = jnp.concatenate([pair[:two], next_[:two]], 0)
+    upper = lax.broadcasted_iota(jnp.int32, pair.shape, 0) < 2 * cols
+    share = jnp.where(upper, pair, next_)
     shares = [share]
     for m in range(1, hops):
         shares.append(moved(share, lambda a, b, m=m: (a ^ (2 * m), b)))
-    w_src, b_src, w_tgt, b_tgt, share = lax.optimization_barrier((w_src, b_src, w_tgt, b_tgt, share))
+    late = tgt_flat
+    tgt_t = lax.optimization_barrier(late.T)
     weights = filters(w_src, b_src, w_tgt, b_tgt, w_out, t * rows_k, rows_k * n_tgt)
 
     both = jnp.where(even, jnp.concatenate([piece, other], 0), jnp.concatenate([other, piece], 0))
@@ -280,7 +352,6 @@
     src_t = lax.all_to_all(
         jnp.broadcast_to(both[None], (plane, 2 * block, pixels)), ("y", "x"), 0, 0, tiled=True
     ).reshape(chans, pixels)
-    src_t, *shares = lax.optimization_barrier((src_t, *shares))
     halos = []
     for mine in shares:
         halos += [mine, moved(mine, near_row)]
@@ -321,7 +392,7 @@
         ).astype(F32)
     grad_tgt = total.reshape(rows_k, cols, width)
 
-    part = lax.dot_general(tgt_flat, g, (((0,), (0,)), ((), ())), preferred_element_type=F32) * scale
+    part = jnp.dot(tgt_t, g, preferred_element_type=F32) * scale
     parts = lax.all_to_all(
         part.astype(BF).reshape(plane, 2 * block, pixels), ("y", "x"), 0, 0, tiled=True
     )

time: 95 us -> 96.6 us (1.017)
  local copies, waits for them, and re-layouts: 13.1 us -> 7.44 us
  starting transfers between devices: 46.3 us -> 51.9 us
  matrix products: 3.52 us -> 1.05 us
  Pallas kernels: 8.83 us -> 11 us
  waiting for transfers between devices: 19.6 us -> 21.2 us
    all_to_all x1, starting transfers between devices: 6.94 us -> 14.6 us  [body(): lax.all_to_all(part.astype(BF).reshape(plane, 2 * block, pixels), ('y', '...]
    all_to_all x1, starting transfers between devices: 14.2 us -> 7.03 us  [body(): lax.all_to_all(jnp.broadcast_to(both[None], (plane, 2 * block, pixels)),...]
    ppermute x19, starting transfers between devices: 25.2 us -> 30.3 us  [moved(): return lax.ppermute(x, SRC + TGT, pairs)]
    convert_element_type x5 -> x0, local copies, waits for them, and re-layouts: 3.88 us -> none  [the longest x3 1.95 us: filters(): (0.5 * jnp.einsum('odex,dmk->omexk', flat, up)).reshape(64, 3 * TAPS * 8)]
    pallas_call x0 -> x1, Pallas kernels: none -> 2.74 us  [filters(): pl.pallas_call(functools.partial(filters_kernel, total_rows), out_shape=(...]
    dot_general x8 -> x1, matrix products: 2.93 us -> 0.46 us  [body(): part = jnp.dot(tgt_t, g, preferred_element_type=F32) * scale]
    ppermute x19, waiting for transfers between devices: 11.7 us -> 13.1 us  [moved(): return lax.ppermute(x, SRC + TGT, pairs)]
    unnamed x26 -> x12, local copies, waits for them, and re-layouts: 2.92 us -> 3.19 us
  transfers between devices with their start and end apart: 21 -> 21, of which waited for: 8 -> 5; matrix products, arithmetic and copies ran while one was open for 13% -> 6% of each run, Pallas kernels for 0% -> 3%
where the time goes in v6:
time: 96.6 us; the launch traced here: 95.3 us
  starting transfers between devices  51.9 us (54%)
  waiting for transfers between devices  21.2 us (22%)
  Pallas kernels  11 us (11%)
  local copies, waits for them, and re-layouts  7.44 us (8%)
  other arithmetic  1.82 us (2%)
  matrix products  1.05 us (1%)
    ppermute x19, starting transfers between devices, moved(): return lax.ppermute(x, SRC + TGT, pairs)  30.3 us
    all_to_all x1, starting transfers between devices, body(): lax.all_to_all(part.astype(BF).reshape(plane, 2 * block, pixels), ('y', '...  14.6 us
    ppermute x19, waiting for transfers between devices, moved(): return lax.ppermute(x, SRC + TGT, pairs)  13.1 us
    pallas_call x1, Pallas kernels, conv(): pl.pallas_call(functools.partial(conv_kernel, cols, scale), out_shape=(ja...  8.3 us
    all_to_all x1, waiting for transfers between devices, body(): lax.all_to_all(part.astype(BF).reshape(plane, 2 * block, pixels), ('y', '...  8.08 us
    all_to_all x1, starting transfers between devices, body(): lax.all_to_all(jnp.broadcast_to(both[None], (plane, 2 * block, pixels)),...  7.03 us
    unnamed x12, local copies, waits for them, and re-layouts  3.19 us
    pallas_call x1, Pallas kernels, filters(): pl.pallas_call(functools.partial(filters_kernel, total_rows), out_shape=(...  2.74 us
  transfers between devices with their start and end apart: 21, of which 5 were waited for; matrix products, arithmetic and copies ran while one was open for 6% of the time, Pallas kernels for 3%

profile of v6, /device:TPU:32, one launch (start us, length us, event | category | flops | bytes accessed | tf_op | source)
XLA Modules:
  0.0 95.3 jit_solution(14582434190818830591)
XLA Ops:
  1.4 6.3 %collective-permute-start = (bf16[32,256]{1,0:T(8,128)(2,1)S(1)}, bf16[32,256]{1,0:T(8,128)(2,1)S(1)}, u32[]{:S(2)}, u32[]{:S(2)}) collective-permute-start(bf16[32,256]{1,0:T(8,128)(2,1)S(1)} %bitcast_bitcast_fusion), channel_id=1, source_target_pairs={{0,1},{1,0},{2,3},{3,2},{4,5},{5,4},{6,7},{7,6},{8,9},{9,8},{10,11... | collective-permute-start | bytes 49160 | tf_op jit(solution)/shard_map/ppermute | solution.py:299
  7.6 0.8 constant_dynamic-slice_fusion
  8.5 0.8 constant_dynamic-slice_fusion.1
  9.4 0.8 broadcast_in_dim.22
  10.2 7.0 %all-to-all-start = ((bf16[16,64,256]{2,1,0:T(8,128)(2,1)}), bf16[16,64,256]{2,1,0:T(8,128)(2,1)S(1)}, u32[]{:S(2)}, u32[]{:S(2)}) async-start(bf16[16,64,256]{2,1,0:T(8,128)(2,1)} %broadcast_in_dim.22), calls=%async_computation | async-start | bytes 1048576 | tf_op jit(solution)/shard_map/all_to_all | solution.py:352
  17.3 6.0 %collective-permute-start.3 = (bf16[384,128]{1,0:T(8,128)(2,1)S(1)}, bf16[384,128]{1,0:T(8,128)(2,1)S(1)}, u32[]{:S(2)}, u32[]{:S(2)}) collective-permute-start(bf16[384,128]{1,0:T(8,128)(2,1)S(1)} %pad_maximum_fusion.2), channel_id=1, source_target_pairs={{0,1},{1,0},{2,3},{3,2},{4,5},{5,4},{6,7},{7,6},{8,9},{9,8},{10,11... | collective-permute-start | bytes 294920 | tf_op jit(solution)/shard_map/ppermute | solution.py:299
  24.0 2.8 %collective-permute-done.3.pair_ref = bf16[384,128]{1,0:T(8,128)(2,1)S(1)} collective-permute-done((bf16[384,128]{1,0:T(8,128)(2,1)S(1)}, bf16[384,128]{1,0:T(8,128)(2,1)S(1)}, u32[]{:S(2)}, u32[]{:S(2)}) %collective-permute-start.3) | collective-permute-done | bytes 98336 | tf_op jit(solution)/shard_map/ppermute | solution.py:299
  26.9 1.9 %collective-permute-start.10 = (bf16[384,128]{1,0:T(8,128)(2,1)S(1)}, bf16[384,128]{1,0:T(8,128)(2,1)S(1)}, u32[]{:S(2)}, u32[]{:S(2)}) collective-permute-start(bf16[384,128]{1,0:T(8,128)(2,1)S(1)} %broadcast_select_fusion.2.more_0_), channel_id=1, source_target_pairs={{0,192},{1,193},{2,194},{3,195},{4,196},{5,197},{6,198},{7,199},{8... | collective-permute-start | bytes 294920 | tf_op jit(solution)/shard_map/ppermute | solution.py:299
  28.8 2.7 %collective-permute-start.6 = (bf16[384,128]{1,0:T(8,128)(2,1)S(1)}, bf16[384,128]{1,0:T(8,128)(2,1)S(1)}, u32[]{:S(2)}, u32[]{:S(2)}) collective-permute-start(bf16[384,128]{1,0:T(8,128)(2,1)S(1)} %broadcast_select_fusion.2.more_0_), channel_id=1, source_target_pairs={{0,64},{1,65},{2,66},{3,67},{4,68},{5,69},{6,70},{7,71},{8,72},{9,... | collective-permute-start | bytes 294920 | tf_op jit(solution)/shard_map/ppermute | solution.py:299
  32.3 2.7 %collective-permute-start.1 = (bf16[1024,128]{1,0:T(8,128)(2,1)}, bf16[1024,128]{1,0:T(8,128)(2,1)S(1)}, u32[]{:S(2)}, u32[]{:S(2)}) collective-permute-start(bf16[1024,128]{1,0:T(8,128)(2,1)} %get-tuple-element.34), channel_id=1, source_target_pairs={{32,64},{33,65},{34,66},{35,67},{36,68},{37,69},{38,70},{39,71},{4... | collective-permute-start | bytes 786440 | tf_op jit(solution)/shard_map/ppermute | solution.py:299
  34.9 2.3 %collective-permute-done.10.more_6_ = bf16[384,128]{1,0:T(8,128)(2,1)S(1)} collective-permute-done((bf16[384,128]{1,0:T(8,128)(2,1)S(1)}, bf16[384,128]{1,0:T(8,128)(2,1)S(1)}, u32[]{:S(2)}, u32[]{:S(2)}) %collective-permute-start.10) | collective-permute-done | bytes 98336 | tf_op jit(solution)/shard_map/ppermute | solution.py:299
  38.4 2.7 %shard_map.130 = (bf16[64,240]{1,0:T(8,128)(2,1)}, bf16[72,256]{1,0:T(8,128)(2,1)}, f32[256,256]{1,0:T(8,128)}) custom-call(s32[1]{0:T(128)} %bitcast.3.row_ref, bf16[9,8,8]{2,1,0:T(8,128)(2,1)} %bitcast.65, bf16[3,3,8]{2,1,0:T(4,128)(2,1)} %bitcast.66, f32[1,8]{1,0:T(1,128)} %bitcast.67, f32[1,8]{1,0:T(1,128)} %bitcast.68, f32[1,8]{1,0:T(1,128)} %bitcast.69, ...), custom_call_target="tpu_custom_call" | custom-call | flops 1000000000 | bytes 1000000 | tf_op jit(solution)/shard_map/pallas_call | solution.py:266
  41.2 0.9 copy-done.3
  42.1 0.8 copy-done.4
  43.6 8.3 %shard_map.131 = (bf16[768,128]{1,0:T(8,128)(2,1)}, f32[384,256]{1,0:T(8,128)S(1)}, bf16[384,128]{1,0:T(8,128)(2,1)S(1)}, bf16[384,128]{1,0:T(8,128)(2,1)S(1)}) custom-call(s32[3]{0:T(128)S(1)} %pad_add_fusion.spot_ref, bf16[64,240]{1,0:T(8,128)(2,1)S(1)} %copy-done.5, bf16[72,256]{1,0:T(8,128)(2,1)S(1)} %copy-done.4, f32[256,256]{1,0:T(8,128)S(1)} %copy-done.3, ...), custom_call_target="tpu_custom_call" | custom-call | flops 4000000000 | bytes 4000000 | tf_op jit(solution)/shard_map/pallas_call | solution.py:162
  52.0 3.6 %collective-permute-start.12 = (bf16[384,128]{1,0:T(8,128)(2,1)S(1)}, bf16[384,128]{1,0:T(8,128)(2,1)S(1)}, u32[]{:S(2)}, u32[]{:S(2)}) collective-permute-start(bf16[384,128]{1,0:T(8,128)(2,1)S(1)} %get-tuple-element.19), channel_id=1, source_target_pairs={{32,64},{33,65},{34,66},{35,67},{36,68},{37,69},{38,70},{39,71},{4... | collective-permute-start | bytes 294920 | tf_op jit(solution)/shard_map/ppermute | solution.py:299
  55.7 2.2 %collective-permute-done.12 = bf16[384,128]{1,0:T(8,128)(2,1)S(1)} collective-permute-done((bf16[384,128]{1,0:T(8,128)(2,1)S(1)}, bf16[384,128]{1,0:T(8,128)(2,1)S(1)}, u32[]{:S(2)}, u32[]{:S(2)}) %collective-permute-start.12) | collective-permute-done | bytes 98336 | tf_op jit(solution)/shard_map/ppermute | solution.py:299
  59.1 1.0 %copy.15 = bf16[1024,256]{1,0:T(8,128)(2,1)} copy(bf16[1024,256]{0,1:T(8,128)(2,1)S(1)} %fusion.2) | data formatting | bytes 1048576 | tf_op jit(solution)/shard_map/convert_element_type | solution.py:397
  60.1 14.6 %all-to-all-start.1 = ((bf16[16,64,256]{2,1,0:T(8,128)(2,1)}), bf16[16,64,256]{2,1,0:T(8,128)(2,1)S(1)}, u32[]{:S(2)}, u32[]{:S(2)}) async-start(bf16[16,64,256]{2,1,0:T(8,128)(2,1)} %bitcast.19), calls=%async_computation.1 | async-start | bytes 1048576 | tf_op jit(solution)/shard_map/all_to_all | solution.py:396
  75.1 2.1 %collective-permute-start.16 = (bf16[384,128]{1,0:T(8,128)(2,1)S(1)}, bf16[384,128]{1,0:T(8,128)(2,1)S(1)}, u32[]{:S(2)}, u32[]{:S(2)}) collective-permute-start(bf16[384,128]{1,0:T(8,128)(2,1)S(1)} %get-tuple-element.35), channel_id=1, source_target_pairs={{0,64},{1,65},{2,66},{3,67},{4,68},{5,69},{6,70},{7,71},{8,72},{9,... | collective-permute-start | bytes 294920 | tf_op jit(solution)/shard_map/ppermute | solution.py:299
  77.2 1.6 %collective-permute-start.18 = (bf16[384,128]{1,0:T(8,128)(2,1)S(1)}, bf16[384,128]{1,0:T(8,128)(2,1)S(1)}, u32[]{:S(2)}, u32[]{:S(2)}) collective-permute-start(bf16[384,128]{1,0:T(8,128)(2,1)S(1)} %get-tuple-element.36), channel_id=1, source_target_pairs={{0,192},{1,193},{2,194},{3,195},{4,196},{5,197},{6,198},{7,199},{8... | collective-permute-start | bytes 294920 | tf_op jit(solution)/shard_map/ppermute | solution.py:299
  78.7 8.1 %all-to-all-done.1 = bf16[16,64,256]{2,1,0:T(8,128)(2,1)S(1)} async-done(((bf16[16,64,256]{2,1,0:T(8,128)(2,1)}), bf16[16,64,256]{2,1,0:T(8,128)(2,1)S(1)}, u32[]{:S(2)}, u32[]{:S(2)}) %all-to-all-start.1) | async-done | bytes 524320 | tf_op jit(solution)/shard_map/all_to_all | solution.py:396
  86.9 1.3 %collective-permute-start.14 = (bf16[32,256]{1,0:T(8,128)(2,1)S(1)}, bf16[32,256]{1,0:T(8,128)(2,1)S(1)}, u32[]{:S(2)}, u32[]{:S(2)}) collective-permute-start(bf16[32,256]{1,0:T(8,128)(2,1)S(1)} %fusion.19), channel_id=1, source_target_pairs={{0,1},{1,0},{2,3},{3,2},{4,5},{5,4},{6,7},{7,6},{8,9},{9,8},{10,11... | collective-permute-start | bytes 49160 | tf_op jit(solution)/shard_map/ppermute | solution.py:299
  88.9 5.7 %collective-permute-done.14 = bf16[32,256]{1,0:T(8,128)(2,1)S(1)} collective-permute-done((bf16[32,256]{1,0:T(8,128)(2,1)S(1)}, bf16[32,256]{1,0:T(8,128)(2,1)S(1)}, u32[]{:S(2)}, u32[]{:S(2)}) %collective-permute-start.14) | collective-permute-done | bytes 16416 | tf_op jit(solution)/shard_map/ppermute | solution.py:299
  (55 shorter events, 7.3 us)
Async XLA Ops:
  1.4 8.0 %collective-permute-start = (bf16[32,256]{1,0:T(8,128)(2,1)S(1)}, bf16[32,256]{1,0:T(8,128)(2,1)S(1)}, u32[]{:S(2)}, u32[]{:S(2)}) collective-permute-start(bf16[32,256]{1,0:T(8,128)(2,1)S(1)} %bitcast_bitcast_fusion), channel_id=1, source_target_pairs={{0,1},{1,0},{2,3},{3,2},{4,5},{5,4},{6,7},{7,6},{8,9},{9,8},{10,11... | collective-permute-start | bytes 49160 | tf_op jit(solution)/shard_map/ppermute | solution.py:299
  10.2 21.3 %all-to-all-start = ((bf16[16,64,256]{2,1,0:T(8,128)(2,1)}), bf16[16,64,256]{2,1,0:T(8,128)(2,1)S(1)}, u32[]{:S(2)}, u32[]{:S(2)}) async-start(bf16[16,64,256]{2,1,0:T(8,128)(2,1)} %broadcast_in_dim.22), calls=%async_computation | async-start | bytes 1048576 | tf_op jit(solution)/shard_map/all_to_all | solution.py:352
  17.3 9.5 %collective-permute-start.3 = (bf16[384,128]{1,0:T(8,128)(2,1)S(1)}, bf16[384,128]{1,0:T(8,128)(2,1)S(1)}, u32[]{:S(2)}, u32[]{:S(2)}) collective-permute-start(bf16[384,128]{1,0:T(8,128)(2,1)S(1)} %pad_maximum_fusion.2), channel_id=1, source_target_pairs={{0,1},{1,0},{2,3},{3,2},{4,5},{5,4},{6,7},{7,6},{8,9},{9,8},{10,11... | collective-permute-start | bytes 294920 | tf_op jit(solution)/shard_map/ppermute | solution.py:299
  23.3 3.5 %collective-permute-start.4 = (bf16[384,128]{1,0:T(8,128)(2,1)S(1)}, bf16[384,128]{1,0:T(8,128)(2,1)S(1)}, u32[]{:S(2)}, u32[]{:S(2)}) collective-permute-start(bf16[384,128]{1,0:T(8,128)(2,1)S(1)} %pad_maximum_fusion.1), channel_id=1, source_target_pairs={{1,2},{2,1},{3,4},{4,3},{5,6},{6,5},{7,8},{8,7},{9,10},{10,9},{11,... | collective-permute-start | bytes 294920 | tf_op jit(solution)/shard_map/ppermute | solution.py:299
  26.9 10.4 %collective-permute-start.10 = (bf16[384,128]{1,0:T(8,128)(2,1)S(1)}, bf16[384,128]{1,0:T(8,128)(2,1)S(1)}, u32[]{:S(2)}, u32[]{:S(2)}) collective-permute-start(bf16[384,128]{1,0:T(8,128)(2,1)S(1)} %broadcast_select_fusion.2.more_0_), channel_id=1, source_target_pairs={{0,192},{1,193},{2,194},{3,195},{4,196},{5,197},{6,198},{7,199},{8... | collective-permute-start | bytes 294920 | tf_op jit(solution)/shard_map/ppermute | solution.py:299
  28.8 8.4 %collective-permute-start.6 = (bf16[384,128]{1,0:T(8,128)(2,1)S(1)}, bf16[384,128]{1,0:T(8,128)(2,1)S(1)}, u32[]{:S(2)}, u32[]{:S(2)}) collective-permute-start(bf16[384,128]{1,0:T(8,128)(2,1)S(1)} %broadcast_select_fusion.2.more_0_), channel_id=1, source_target_pairs={{0,64},{1,65},{2,66},{3,67},{4,68},{5,69},{6,70},{7,71},{8,72},{9,... | collective-permute-start | bytes 294920 | tf_op jit(solution)/shard_map/ppermute | solution.py:299
  31.5 6.2 %collective-permute-start.8 = (bf16[384,128]{1,0:T(8,128)(2,1)S(1)}, bf16[384,128]{1,0:T(8,128)(2,1)S(1)}, u32[]{:S(2)}, u32[]{:S(2)}) collective-permute-start(bf16[384,128]{1,0:T(8,128)(2,1)S(1)} %broadcast_select_fusion.2.more_0_), channel_id=1, source_target_pairs={{0,128},{1,129},{2,130},{3,131},{4,132},{5,133},{6,134},{7,135},{8... | collective-permute-start | bytes 294920 | tf_op jit(solution)/shard_map/ppermute | solution.py:299
  31.5 6.3 %collective-permute-start.5 = (bf16[384,128]{1,0:T(8,128)(2,1)S(1)}, bf16[384,128]{1,0:T(8,128)(2,1)S(1)}, u32[]{:S(2)}, u32[]{:S(2)}) collective-permute-start(bf16[384,128]{1,0:T(8,128)(2,1)S(1)} %broadcast_select_fusion.2.more_0_), channel_id=1, source_target_pairs={{0,32},{1,33},{2,34},{3,35},{4,36},{5,37},{6,38},{7,39},{8,40},{9,... | collective-permute-start | bytes 294920 | tf_op jit(solution)/shard_map/ppermute | solution.py:299
  32.3 8.9 %collective-permute-start.1 = (bf16[1024,128]{1,0:T(8,128)(2,1)}, bf16[1024,128]{1,0:T(8,128)(2,1)S(1)}, u32[]{:S(2)}, u32[]{:S(2)}) collective-permute-start(bf16[1024,128]{1,0:T(8,128)(2,1)} %get-tuple-element.34), channel_id=1, source_target_pairs={{32,64},{33,65},{34,66},{35,67},{36,68},{37,69},{38,70},{39,71},{4... | collective-permute-start | bytes 786440 | tf_op jit(solution)/shard_map/ppermute | solution.py:299
  37.2 3.9 %collective-permute-start.2 = (bf16[1024,128]{1,0:T(8,128)(2,1)S(1)}, bf16[1024,128]{1,0:T(8,128)(2,1)S(1)}, u32[]{:S(2)}, u32[]{:S(2)}) collective-permute-start(bf16[1024,128]{1,0:T(8,128)(2,1)S(1)} %get-tuple-element.33), channel_id=1, source_target_pairs={{0,32},{1,33},{2,34},{3,35},{4,36},{5,37},{6,38},{7,39},{8,40},{9,... | collective-permute-start | bytes 786440 | tf_op jit(solution)/shard_map/ppermute | solution.py:299
  37.3 3.9 %collective-permute-start.11 = (bf16[384,128]{1,0:T(8,128)(2,1)S(1)}, bf16[384,128]{1,0:T(8,128)(2,1)S(1)}, u32[]{:S(2)}, u32[]{:S(2)}) collective-permute-start(bf16[384,128]{1,0:T(8,128)(2,1)S(1)} %collective-permute-done.10.more_6_), channel_id=1, source_target_pairs={{0,32},{1,33},{2,34},{3,35},{4,36},{5,37},{6,38},{7,39},{8,40},{9,... | collective-permute-start | bytes 294920 | tf_op jit(solution)/shard_map/ppermute | solution.py:299
  37.8 3.3 %collective-permute-start.7 = (bf16[384,128]{1,0:T(8,128)(2,1)S(1)}, bf16[384,128]{1,0:T(8,128)(2,1)S(1)}, u32[]{:S(2)}, u32[]{:S(2)}) collective-permute-start(bf16[384,128]{1,0:T(8,128)(2,1)S(1)} %collective-permute-done.6.more_2_), channel_id=1, source_target_pairs={{0,32},{1,33},{2,34},{3,35},{4,36},{5,37},{6,38},{7,39},{8,40},{9,... | collective-permute-start | bytes 294920 | tf_op jit(solution)/shard_map/ppermute | solution.py:299
  37.9 3.3 %collective-permute-start.9 = (bf16[384,128]{1,0:T(8,128)(2,1)S(1)}, bf16[384,128]{1,0:T(8,128)(2,1)S(1)}, u32[]{:S(2)}, u32[]{:S(2)}) collective-permute-start(bf16[384,128]{1,0:T(8,128)(2,1)S(1)} %collective-permute-done.8.more_4_), channel_id=1, source_target_pairs={{0,32},{1,33},{2,34},{3,35},{4,36},{5,37},{6,38},{7,39},{8,40},{9,... | collective-permute-start | bytes 294920 | tf_op jit(solution)/shard_map/ppermute | solution.py:299
  38.4 2.8 %copy-start.1 = (bf16[4,96,2,128]{3,2,1,0:T(2,128)(2,1)S(1)}, bf16[4,96,2,128]{3,2,1,0:T(2,128)(2,1)}, u32[]{:S(2)}) copy-start(bf16[4,96,2,128]{3,2,1,0:T(2,128)(2,1)} %param.18) | copy-start | bytes 589828
  38.4 2.8 %copy-start.2 = (bf16[4,96,1024]{2,1,0:T(8,128)(2,1)S(1)}, bf16[4,96,1024]{2,1,0:T(8,128)(2,1)}, u32[]{:S(2)}) copy-start(bf16[4,96,1024]{2,1,0:T(8,128)(2,1)} %param.12) | copy-start | bytes 2359300
  41.2 1.0 copy-start.3
  52.0 5.9 %collective-permute-start.12 = (bf16[384,128]{1,0:T(8,128)(2,1)S(1)}, bf16[384,128]{1,0:T(8,128)(2,1)S(1)}, u32[]{:S(2)}, u32[]{:S(2)}) collective-permute-start(bf16[384,128]{1,0:T(8,128)(2,1)S(1)} %get-tuple-element.19), channel_id=1, source_target_pairs={{32,64},{33,65},{34,66},{35,67},{36,68},{37,69},{38,70},{39,71},{4... | collective-permute-start | bytes 294920 | tf_op jit(solution)/shard_map/ppermute | solution.py:299
  55.6 2.3 %collective-permute-start.13 = (bf16[384,128]{1,0:T(8,128)(2,1)S(1)}, bf16[384,128]{1,0:T(8,128)(2,1)S(1)}, u32[]{:S(2)}, u32[]{:S(2)}) collective-permute-start(bf16[384,128]{1,0:T(8,128)(2,1)S(1)} %get-tuple-element.20), channel_id=1, source_target_pairs={{0,32},{1,33},{2,34},{3,35},{4,36},{5,37},{6,38},{7,39},{8,40},{9,... | collective-permute-start | bytes 294920 | tf_op jit(solution)/shard_map/ppermute | solution.py:299
  58.3 16.5 %collective-permute-start.15 = (bf16[384,512]{1,0:T(8,128)(2,1)S(1)}, bf16[384,512]{1,0:T(8,128)(2,1)S(1)}, u32[]{:S(2)}, u32[]{:S(2)}) collective-permute-start(bf16[384,512]{1,0:T(8,128)(2,1)S(1)} %fusion.1), channel_id=1, source_target_pairs={{0,32},{1,33},{2,34},{3,35},{4,36},{5,37},{6,38},{7,39},{8,40},{9,... | collective-permute-start | bytes 1179656 | tf_op jit(solution)/shard_map/ppermute | solution.py:299
  60.1 26.8 %all-to-all-start.1 = ((bf16[16,64,256]{2,1,0:T(8,128)(2,1)}), bf16[16,64,256]{2,1,0:T(8,128)(2,1)S(1)}, u32[]{:S(2)}, u32[]{:S(2)}) async-start(bf16[16,64,256]{2,1,0:T(8,128)(2,1)} %bitcast.19), calls=%async_computation.1 | async-start | bytes 1048576 | tf_op jit(solution)/shard_map/all_to_all | solution.py:396
  75.1 13.1 %collective-permute-start.16 = (bf16[384,128]{1,0:T(8,128)(2,1)S(1)}, bf16[384,128]{1,0:T(8,128)(2,1)S(1)}, u32[]{:S(2)}, u32[]{:S(2)}) collective-permute-start(bf16[384,128]{1,0:T(8,128)(2,1)S(1)} %get-tuple-element.35), channel_id=1, source_target_pairs={{0,64},{1,65},{2,66},{3,67},{4,68},{5,69},{6,70},{7,71},{8,72},{9,... | collective-permute-start | bytes 294920 | tf_op jit(solution)/shard_map/ppermute | solution.py:299
  77.2 11.0 %collective-permute-start.17 = (bf16[384,128]{1,0:T(8,128)(2,1)S(1)}, bf16[384,128]{1,0:T(8,128)(2,1)S(1)}, u32[]{:S(2)}, u32[]{:S(2)}) collective-permute-start(bf16[384,128]{1,0:T(8,128)(2,1)S(1)} %get-tuple-element.37), channel_id=1, source_target_pairs={{0,128},{1,129},{2,130},{3,131},{4,132},{5,133},{6,134},{7,135},{8... | collective-permute-start | bytes 294920 | tf_op jit(solution)/shard_map/ppermute | solution.py:299
  77.2 11.0 %collective-permute-start.18 = (bf16[384,128]{1,0:T(8,128)(2,1)S(1)}, bf16[384,128]{1,0:T(8,128)(2,1)S(1)}, u32[]{:S(2)}, u32[]{:S(2)}) collective-permute-start(bf16[384,128]{1,0:T(8,128)(2,1)S(1)} %get-tuple-element.36), channel_id=1, source_target_pairs={{0,192},{1,193},{2,194},{3,195},{4,196},{5,197},{6,198},{7,199},{8... | collective-permute-start | bytes 294920 | tf_op jit(solution)/shard_map/ppermute | solution.py:299
  86.9 7.7 %collective-permute-start.14 = (bf16[32,256]{1,0:T(8,128)(2,1)S(1)}, bf16[32,256]{1,0:T(8,128)(2,1)S(1)}, u32[]{:S(2)}, u32[]{:S(2)}) collective-permute-start(bf16[32,256]{1,0:T(8,128)(2,1)S(1)} %fusion.19), channel_id=1, source_target_pairs={{0,1},{1,0},{2,3},{3,2},{4,5},{5,4},{6,7},{7,6},{8,9},{9,8},{10,11... | collective-permute-start | bytes 49160 | tf_op jit(solution)/shard_map/ppermute | solution.py:299
  (3 other events, 2.2 us)

commit v7 on v6

--- a/solution.py
+++ b/solution.py
@@ -22,12 +22,19 @@
 
 def conv_kernel(
     cols,
-    scale, spot_ref, wf_ref, wb_ref, bias_ref, tgt_ref, src_ref, far_ref, near_ref, pair_ref, next_ref, cot_ref,
+    scale, spot_ref, wf_hbm, wb_hbm, bias_hbm, tgt_ref, src_ref, far_ref, near_ref, pair_ref, next_ref, cot_ref,
     *more,
 ):
-    n_more = len(more) - 11
+    n_more = len(more) - 15
     halo_refs = more[:n_more]
-    score_ref, g_ref, far_out, near_out, cs, rows, cotf, cots, gp, sc, gs = more[n_more:]
+    score_ref, g_ref, far_out, near_out, cs, rows, cotf, cots, gp, sc, gs, *filters_at = more[n_more:]
+    wf_ref, wb_ref, bias_ref, arrived = filters_at
+    fetched = [
+        pltpu.make_async_copy(source, target, arrived.at[n])
+        for n, (source, target) in enumerate(((wf_hbm, wf_ref), (wb_hbm, wb_ref), (bias_hbm, bias_ref)))
+    ]
+    for copy in fetched:
+        copy.start()
     hop, core = spot_ref[0], spot_ref[1]
     first = core == 0
     even = spot_ref[2] == 0
@@ -91,6 +98,8 @@
         return 0
 
 
+    for copy in fetched:
+        copy.wait()
     wf = wf_ref[...]
     wb = wb_ref[...]
 
@@ -167,7 +176,7 @@
             jax.ShapeDtypeStruct((n, 128), BF),
             jax.ShapeDtypeStruct((n, 128), BF),
         ),
-        in_specs=[smem] + [pl.BlockSpec()] * 3 + [vmem] * (7 + len(halos)),
+        in_specs=[smem] + [pl.BlockSpec(memory_space=pltpu.HBM)] * 3 + [vmem] * (7 + len(halos)),
         out_specs=(vmem,) * 4,
         scratch_shapes=[
             pltpu.VMEM((4, 8 * cols, 128), F32),
@@ -177,6 +186,8 @@
             pltpu.VMEM(((cols + 2) * 64, 256), BF),
             pltpu.VMEM((2, 8 * cols, 128), F32),
             pltpu.VMEM((4, 4 * cols, 128), F32),
+            *(pltpu.VMEM(w.shape, w.dtype) for w in weights),
+            pltpu.SemaphoreType.DMA((3,)),
         ],
         compiler_params=pltpu.CompilerParams(vmem_limit_bytes=40 * 2**20),
         cost_estimate=pl.CostEstimate(flops=4 * 10**9, transcendentals=10**7, bytes_accessed=4 * 10**6),
@@ -340,18 +351,20 @@
     next_ = moved(next_e, lambda a, b: (a, b + 1 if b % 2 else b - 1))
     upper = lax.broadcasted_iota(jnp.int32, pair.shape, 0) < 2 * cols
     share = jnp.where(upper, pair, next_)
+    weights = filters(w_src, b_src, w_tgt, b_tgt, w_out, t * rows_k, rows_k * n_tgt)
+    share, *weights = lax.optimization_barrier((share, *weights))
     shares = [share]
     for m in range(1, hops):
         shares.append(moved(share, lambda a, b, m=m: (a ^ (2 * m), b)))
-    late = tgt_flat
+    share, late = lax.optimization_barrier((share, tgt_flat))
     tgt_t = lax.optimization_barrier(late.T)
-    weights = filters(w_src, b_src, w_tgt, b_tgt, w_out, t * rows_k, rows_k * n_tgt)
 
     both = jnp.where(even, jnp.concatenate([piece, other], 0), jnp.concatenate([other, piece], 0))
     plane = n_tgt // 2
     src_t = lax.all_to_all(
         jnp.broadcast_to(both[None], (plane, 2 * block, pixels)), ("y", "x"), 0, 0, tiled=True
     ).reshape(chans, pixels)
+    src_t, *shares = lax.optimization_barrier((src_t, *shares))
     halos = []
     for mine in shares:
         halos += [mine, moved(mine, near_row)]

time: 96.6 us -> 91.5 us (0.947)
  starting transfers between devices: 51.9 us -> 43.7 us
  waiting for transfers between devices: 21.2 us -> 28.1 us
  local copies, waits for them, and re-layouts: 7.44 us -> 3.97 us
    all_to_all x1, starting transfers between devices: 14.6 us -> 6.92 us  [body(): lax.all_to_all(part.astype(BF).reshape(plane, 2 * block, pixels), ('y', '...]
    ppermute x19, starting transfers between devices: 30.3 us -> 22.6 us  [moved(): return lax.ppermute(x, SRC + TGT, pairs)]
    all_to_all x1, starting transfers between devices: 7.03 us -> 14.2 us  [body(): lax.all_to_all(jnp.broadcast_to(both[None], (plane, 2 * block, pixels)),...]
    ppermute x19, waiting for transfers between devices: 13.1 us -> 19.8 us  [moved(): return lax.ppermute(x, SRC + TGT, pairs)]
    unnamed x12, local copies, waits for them, and re-layouts: 3.19 us -> 0.73 us
    convert_element_type x1 -> x0, local copies, waits for them, and re-layouts: 0.99 us -> none  [body(): part.astype(BF).reshape(plane, 2 * block, pixels)]
  transfers between devices with their start and end apart: 21 -> 21, of which waited for: 5 -> 10; matrix products, arithmetic and copies ran while one was open for 6% -> 6% of each run, Pallas kernels for 3% -> 3%
where the time goes in v7:
time: 91.5 us; the launch traced here: 90.9 us
  starting transfers between devices  43.7 us (48%)
  waiting for transfers between devices  28.1 us (31%)
  Pallas kernels  10.6 us (12%)
  local copies, waits for them, and re-layouts  3.97 us (4%)
  matrix products  1.86 us (2%)
  other arithmetic  1.81 us (2%)
    ppermute x19, starting transfers between devices, moved(): return lax.ppermute(x, SRC + TGT, pairs)  22.6 us
    ppermute x19, waiting for transfers between devices, moved(): return lax.ppermute(x, SRC + TGT, pairs)  19.8 us
    all_to_all x1, starting transfers between devices, body(): lax.all_to_all(jnp.broadcast_to(both[None], (plane, 2 * block, pixels)),...  14.2 us
    all_to_all x1, waiting for transfers between devices, body(): lax.all_to_all(part.astype(BF).reshape(plane, 2 * block, pixels), ('y', '...  8.25 us
    pallas_call x1, Pallas kernels, conv(): pl.pallas_call(functools.partial(conv_kernel, cols, scale), out_shape=(ja...  7.98 us
    all_to_all x1, starting transfers between devices, body(): lax.all_to_all(part.astype(BF).reshape(plane, 2 * block, pixels), ('y', '...  6.92 us
    pallas_call x1, Pallas kernels, filters(): pl.pallas_call(functools.partial(filters_kernel, total_rows), out_shape=(...  2.66 us
  transfers between devices with their start and end apart: 21, of which 10 were waited for; matrix products, arithmetic and copies ran while one was open for 6% of the time, Pallas kernels for 3%

profile of v7, /device:TPU:32, one launch (start us, length us, event | category | flops | bytes accessed | tf_op | source)
XLA Modules:
  0.0 90.9 jit_solution(1533561943696358290)
XLA Ops:
  1.4 6.3 %collective-permute-start.1 = (bf16[32,256]{1,0:T(8,128)(2,1)S(1)}, bf16[32,256]{1,0:T(8,128)(2,1)S(1)}, u32[]{:S(2)}, u32[]{:S(2)}) collective-permute-start(bf16[32,256]{1,0:T(8,128)(2,1)S(1)} %bitcast_bitcast_fusion), channel_id=1, source_target_pairs={{0,1},{1,0},{2,3},{3,2},{4,5},{5,4},{6,7},{7,6},{8,9},{9,8},{10,11... | collective-permute-start | bytes 49160 | tf_op jit(solution)/shard_map/ppermute | solution.py:310
  10.1 0.8 broadcast_in_dim.22
  11.0 14.2 %all-to-all-start = ((bf16[16,64,256]{2,1,0:T(8,128)(2,1)}), bf16[16,64,256]{2,1,0:T(8,128)(2,1)S(1)}, u32[]{:S(2)}, u32[]{:S(2)}) async-start(bf16[16,64,256]{2,1,0:T(8,128)(2,1)} %broadcast_in_dim.22), calls=%async_computation | async-start | bytes 1048576 | tf_op jit(solution)/shard_map/all_to_all | solution.py:364
  25.2 2.7 %shard_map.130 = (bf16[64,240]{1,0:T(8,128)(2,1)}, bf16[72,256]{1,0:T(8,128)(2,1)}, f32[256,256]{1,0:T(8,128)}) custom-call(s32[1]{0:T(128)} %bitcast.7.row_ref, bf16[9,8,8]{2,1,0:T(8,128)(2,1)} %bitcast.62, bf16[3,3,8]{2,1,0:T(4,128)(2,1)} %bitcast.63, f32[1,8]{1,0:T(1,128)} %bitcast.64, f32[1,8]{1,0:T(1,128)} %bitcast.65, f32[1,8]{1,0:T(1,128)} %bitcast.66, ...), custom_call_target="tpu_custom_call" | custom-call | flops 1000000000 | bytes 1000000 | tf_op jit(solution)/shard_map/pallas_call | solution.py:277
  28.0 1.1 %collective-permute-start.3 = (bf16[384,128]{1,0:T(8,128)(2,1)S(1)}, bf16[384,128]{1,0:T(8,128)(2,1)S(1)}, u32[]{:S(2)}, u32[]{:S(2)}) collective-permute-start(bf16[384,128]{1,0:T(8,128)(2,1)S(1)} %broadcast_select_fusion.2.more_0_), channel_id=1, source_target_pairs={{0,64},{1,65},{2,66},{3,67},{4,68},{5,69},{6,70},{7,71},{8,72},{9,... | collective-permute-start | bytes 294920 | tf_op jit(solution)/shard_map/ppermute | solution.py:310
  29.1 1.5 %collective-permute-start.4 = (bf16[384,128]{1,0:T(8,128)(2,1)S(1)}, bf16[384,128]{1,0:T(8,128)(2,1)S(1)}, u32[]{:S(2)}, u32[]{:S(2)}) collective-permute-start(bf16[384,128]{1,0:T(8,128)(2,1)S(1)} %broadcast_select_fusion.2.more_0_), channel_id=1, source_target_pairs={{0,128},{1,129},{2,130},{3,131},{4,132},{5,133},{6,134},{7,135},{8... | collective-permute-start | bytes 294920 | tf_op jit(solution)/shard_map/ppermute | solution.py:310
  30.6 1.0 %collective-permute-start.5 = (bf16[384,128]{1,0:T(8,128)(2,1)S(1)}, bf16[384,128]{1,0:T(8,128)(2,1)S(1)}, u32[]{:S(2)}, u32[]{:S(2)}) collective-permute-start(bf16[384,128]{1,0:T(8,128)(2,1)S(1)} %broadcast_select_fusion.2.more_0_), channel_id=1, source_target_pairs={{0,192},{1,193},{2,194},{3,195},{4,196},{5,197},{6,198},{7,199},{8... | collective-permute-start | bytes 294920 | tf_op jit(solution)/shard_map/ppermute | solution.py:310
  31.6 1.8 %collective-permute-done.3.more_2_ = bf16[384,128]{1,0:T(8,128)(2,1)S(1)} collective-permute-done((bf16[384,128]{1,0:T(8,128)(2,1)S(1)}, bf16[384,128]{1,0:T(8,128)(2,1)S(1)}, u32[]{:S(2)}, u32[]{:S(2)}) %collective-permute-start.3) | collective-permute-done | bytes 98336 | tf_op jit(solution)/shard_map/ppermute | solution.py:310
  33.3 3.1 %collective-permute-done.4.more_4_ = bf16[384,128]{1,0:T(8,128)(2,1)S(1)} collective-permute-done((bf16[384,128]{1,0:T(8,128)(2,1)S(1)}, bf16[384,128]{1,0:T(8,128)(2,1)S(1)}, u32[]{:S(2)}, u32[]{:S(2)}) %collective-permute-start.4) | collective-permute-done | bytes 98336 | tf_op jit(solution)/shard_map/ppermute | solution.py:310
  36.5 2.5 %collective-permute-done.5.more_6_ = bf16[384,128]{1,0:T(8,128)(2,1)S(1)} collective-permute-done((bf16[384,128]{1,0:T(8,128)(2,1)S(1)}, bf16[384,128]{1,0:T(8,128)(2,1)S(1)}, u32[]{:S(2)}, u32[]{:S(2)}) %collective-permute-start.5) | collective-permute-done | bytes 98336 | tf_op jit(solution)/shard_map/ppermute | solution.py:310
  39.7 1.9 %collective-permute-start.6 = (bf16[1024,128]{1,0:T(8,128)(2,1)}, bf16[1024,128]{1,0:T(8,128)(2,1)S(1)}, u32[]{:S(2)}, u32[]{:S(2)}) collective-permute-start(bf16[1024,128]{1,0:T(8,128)(2,1)} %get-tuple-element.54), channel_id=1, source_target_pairs={{32,64},{33,65},{34,66},{35,67},{36,68},{37,69},{38,70},{39,71},{4... | collective-permute-start | bytes 786440 | tf_op jit(solution)/shard_map/ppermute | solution.py:310
  41.7 1.2 %collective-permute-start.7 = (bf16[1024,128]{1,0:T(8,128)(2,1)S(1)}, bf16[1024,128]{1,0:T(8,128)(2,1)S(1)}, u32[]{:S(2)}, u32[]{:S(2)}) collective-permute-start(bf16[1024,128]{1,0:T(8,128)(2,1)S(1)} %get-tuple-element.53), channel_id=1, source_target_pairs={{0,32},{1,33},{2,34},{3,35},{4,36},{5,37},{6,38},{7,39},{8,40},{9,... | collective-permute-start | bytes 786440 | tf_op jit(solution)/shard_map/ppermute | solution.py:310
  45.5 2.2 %collective-permute-done.6.far_ref = bf16[1024,128]{1,0:T(8,128)(2,1)S(1)} collective-permute-done((bf16[1024,128]{1,0:T(8,128)(2,1)}, bf16[1024,128]{1,0:T(8,128)(2,1)S(1)}, u32[]{:S(2)}, u32[]{:S(2)}) %collective-permute-start.6) | collective-permute-done | bytes 262176 | tf_op jit(solution)/shard_map/ppermute | solution.py:310
  47.7 8.0 %shard_map.131 = (bf16[768,128]{1,0:T(8,128)(2,1)}, f32[384,256]{1,0:T(8,128)S(1)}, bf16[384,128]{1,0:T(8,128)(2,1)S(1)}, bf16[384,128]{1,0:T(8,128)(2,1)S(1)}) custom-call(s32[3]{0:T(128)S(1)} %pad_add_fusion.spot_ref, bf16[64,240]{1,0:T(8,128)(2,1)S(1)} %copy-done.5, bf16[72,256]{1,0:T(8,128)(2,1)S(1)} %copy-done.4, f32[256,256]{1,0:T(8,128)S(1)} %copy-done.3, ...), custom_call_target="tpu_custom_call" | custom-call | flops 4000000000 | bytes 4000000 | tf_op jit(solution)/shard_map/pallas_call | solution.py:171
  55.7 1.9 %collective-permute-start.12 = (bf16[384,128]{1,0:T(8,128)(2,1)S(1)}, bf16[384,128]{1,0:T(8,128)(2,1)S(1)}, u32[]{:S(2)}, u32[]{:S(2)}) collective-permute-start(bf16[384,128]{1,0:T(8,128)(2,1)S(1)} %get-tuple-element.39), channel_id=1, source_target_pairs={{32,64},{33,65},{34,66},{35,67},{36,68},{37,69},{38,70},{39,71},{4... | collective-permute-start | bytes 294920 | tf_op jit(solution)/shard_map/ppermute | solution.py:310
  57.6 1.2 %collective-permute-start.13 = (bf16[384,128]{1,0:T(8,128)(2,1)S(1)}, bf16[384,128]{1,0:T(8,128)(2,1)S(1)}, u32[]{:S(2)}, u32[]{:S(2)}) collective-permute-start(bf16[384,128]{1,0:T(8,128)(2,1)S(1)} %get-tuple-element.40), channel_id=1, source_target_pairs={{0,32},{1,33},{2,34},{3,35},{4,36},{5,37},{6,38},{7,39},{8,40},{9,... | collective-permute-start | bytes 294920 | tf_op jit(solution)/shard_map/ppermute | solution.py:310
  58.8 2.8 %collective-permute-done.12 = bf16[384,128]{1,0:T(8,128)(2,1)S(1)} collective-permute-done((bf16[384,128]{1,0:T(8,128)(2,1)S(1)}, bf16[384,128]{1,0:T(8,128)(2,1)S(1)}, u32[]{:S(2)}, u32[]{:S(2)}) %collective-permute-start.12) | collective-permute-done | bytes 98336 | tf_op jit(solution)/shard_map/ppermute | solution.py:310
  62.1 1.3 %fusion = bf16[1024,256]{1,0:T(8,128)(2,1)} fusion(bf16[1024,384]{0,1:T(8,128)(2,1)S(1)} %bitcast.56, bf16[384,128]{1,0:T(8,128)(2,1)S(1)} %get-tuple-element.44, bf16[384,128]{1,0:T(8,128)(2,1)S(1)} %get-tuple-element.43), kind=kOutput, calls=%fused_computation.1 | convolution fusion | flops 202244096 | bytes 1507328 | tf_op jit(solution)/shard_map/dot_general | solution.py:408
  63.3 6.9 %all-to-all-start.1 = ((bf16[16,64,256]{2,1,0:T(8,128)(2,1)}), bf16[16,64,256]{2,1,0:T(8,128)(2,1)S(1)}, u32[]{:S(2)}, u32[]{:S(2)}) async-start(bf16[16,64,256]{2,1,0:T(8,128)(2,1)} %bitcast.18), calls=%async_computation.1 | async-start | bytes 1048576 | tf_op jit(solution)/shard_map/all_to_all | solution.py:409
  71.1 2.1 %collective-permute-start.17 = (bf16[384,128]{1,0:T(8,128)(2,1)S(1)}, bf16[384,128]{1,0:T(8,128)(2,1)S(1)}, u32[]{:S(2)}, u32[]{:S(2)}) collective-permute-start(bf16[384,128]{1,0:T(8,128)(2,1)S(1)} %get-tuple-element.57), channel_id=1, source_target_pairs={{0,128},{1,129},{2,130},{3,131},{4,132},{5,133},{6,134},{7,135},{8... | collective-permute-start | bytes 294920 | tf_op jit(solution)/shard_map/ppermute | solution.py:310
  73.2 1.0 %collective-permute-start.18 = (bf16[384,128]{1,0:T(8,128)(2,1)S(1)}, bf16[384,128]{1,0:T(8,128)(2,1)S(1)}, u32[]{:S(2)}, u32[]{:S(2)}) collective-permute-start(bf16[384,128]{1,0:T(8,128)(2,1)S(1)} %get-tuple-element.56), channel_id=1, source_target_pairs={{0,192},{1,193},{2,194},{3,195},{4,196},{5,197},{6,198},{7,199},{8... | collective-permute-start | bytes 294920 | tf_op jit(solution)/shard_map/ppermute | solution.py:310
  74.2 8.2 %all-to-all-done.1 = bf16[16,64,256]{2,1,0:T(8,128)(2,1)S(1)} async-done(((bf16[16,64,256]{2,1,0:T(8,128)(2,1)}), bf16[16,64,256]{2,1,0:T(8,128)(2,1)S(1)}, u32[]{:S(2)}, u32[]{:S(2)}) %all-to-all-start.1) | async-done | bytes 524320 | tf_op jit(solution)/shard_map/all_to_all | solution.py:409
  82.6 1.1 %collective-permute-start.14 = (bf16[32,256]{1,0:T(8,128)(2,1)S(1)}, bf16[32,256]{1,0:T(8,128)(2,1)S(1)}, u32[]{:S(2)}, u32[]{:S(2)}) collective-permute-start(bf16[32,256]{1,0:T(8,128)(2,1)S(1)} %fusion.18), channel_id=1, source_target_pairs={{0,1},{1,0},{2,3},{3,2},{4,5},{5,4},{6,7},{7,6},{8,9},{9,8},{10,11... | collective-permute-start | bytes 49160 | tf_op jit(solution)/shard_map/ppermute | solution.py:310
  84.4 5.9 %collective-permute-done.14 = bf16[32,256]{1,0:T(8,128)(2,1)S(1)} collective-permute-done((bf16[32,256]{1,0:T(8,128)(2,1)S(1)}, bf16[32,256]{1,0:T(8,128)(2,1)S(1)}, u32[]{:S(2)}, u32[]{:S(2)}) %collective-permute-start.14) | collective-permute-done | bytes 16416 | tf_op jit(solution)/shard_map/ppermute | solution.py:310
  (54 shorter events, 9.5 us)
Async XLA Ops:
  1.4 8.1 %collective-permute-start.1 = (bf16[32,256]{1,0:T(8,128)(2,1)S(1)}, bf16[32,256]{1,0:T(8,128)(2,1)S(1)}, u32[]{:S(2)}, u32[]{:S(2)}) collective-permute-start(bf16[32,256]{1,0:T(8,128)(2,1)S(1)} %bitcast_bitcast_fusion), channel_id=1, source_target_pairs={{0,1},{1,0},{2,3},{3,2},{4,5},{5,4},{6,7},{7,6},{8,9},{9,8},{10,11... | collective-permute-start | bytes 49160 | tf_op jit(solution)/shard_map/ppermute | solution.py:310
  9.3 18.5 %collective-permute-start = (bf16[384,128]{1,0:T(8,128)(2,1)S(1)}, bf16[384,128]{1,0:T(8,128)(2,1)S(1)}, u32[]{:S(2)}, u32[]{:S(2)}) collective-permute-start(bf16[384,128]{1,0:T(8,128)(2,1)S(1)} %pad_maximum_fusion.1), channel_id=1, source_target_pairs={{0,1},{1,0},{2,3},{3,2},{4,5},{5,4},{6,7},{7,6},{8,9},{9,8},{10,11... | collective-permute-start | bytes 294920 | tf_op jit(solution)/shard_map/ppermute | solution.py:310
  9.4 18.4 %collective-permute-start.2 = (bf16[384,128]{1,0:T(8,128)(2,1)S(1)}, bf16[384,128]{1,0:T(8,128)(2,1)S(1)}, u32[]{:S(2)}, u32[]{:S(2)}) collective-permute-start(bf16[384,128]{1,0:T(8,128)(2,1)S(1)} %pad_maximum_fusion.2), channel_id=1, source_target_pairs={{1,2},{2,1},{3,4},{4,3},{5,6},{6,5},{7,8},{8,7},{9,10},{10,9},{11,... | collective-permute-start | bytes 294920 | tf_op jit(solution)/shard_map/ppermute | solution.py:310
  11.0 28.0 %all-to-all-start = ((bf16[16,64,256]{2,1,0:T(8,128)(2,1)}), bf16[16,64,256]{2,1,0:T(8,128)(2,1)S(1)}, u32[]{:S(2)}, u32[]{:S(2)}) async-start(bf16[16,64,256]{2,1,0:T(8,128)(2,1)} %broadcast_in_dim.22), calls=%async_computation | async-start | bytes 1048576 | tf_op jit(solution)/shard_map/all_to_all | solution.py:364
  27.9 19.8 %copy-start.2 = (bf16[4,96,1024]{2,1,0:T(8,128)(2,1)S(1)}, bf16[4,96,1024]{2,1,0:T(8,128)(2,1)}, u32[]{:S(2)}) copy-start(bf16[4,96,1024]{2,1,0:T(8,128)(2,1)} %param.12) | copy-start | bytes 2359300
  28.0 5.3 %collective-permute-start.3 = (bf16[384,128]{1,0:T(8,128)(2,1)S(1)}, bf16[384,128]{1,0:T(8,128)(2,1)S(1)}, u32[]{:S(2)}, u32[]{:S(2)}) collective-permute-start(bf16[384,128]{1,0:T(8,128)(2,1)S(1)} %broadcast_select_fusion.2.more_0_), channel_id=1, source_target_pairs={{0,64},{1,65},{2,66},{3,67},{4,68},{5,69},{6,70},{7,71},{8,72},{9,... | collective-permute-start | bytes 294920 | tf_op jit(solution)/shard_map/ppermute | solution.py:310
  29.1 7.4 %collective-permute-start.4 = (bf16[384,128]{1,0:T(8,128)(2,1)S(1)}, bf16[384,128]{1,0:T(8,128)(2,1)S(1)}, u32[]{:S(2)}, u32[]{:S(2)}) collective-permute-start(bf16[384,128]{1,0:T(8,128)(2,1)S(1)} %broadcast_select_fusion.2.more_0_), channel_id=1, source_target_pairs={{0,128},{1,129},{2,130},{3,131},{4,132},{5,133},{6,134},{7,135},{8... | collective-permute-start | bytes 294920 | tf_op jit(solution)/shard_map/ppermute | solution.py:310
  30.6 8.4 %collective-permute-start.5 = (bf16[384,128]{1,0:T(8,128)(2,1)S(1)}, bf16[384,128]{1,0:T(8,128)(2,1)S(1)}, u32[]{:S(2)}, u32[]{:S(2)}) collective-permute-start(bf16[384,128]{1,0:T(8,128)(2,1)S(1)} %broadcast_select_fusion.2.more_0_), channel_id=1, source_target_pairs={{0,192},{1,193},{2,194},{3,195},{4,196},{5,197},{6,198},{7,199},{8... | collective-permute-start | bytes 294920 | tf_op jit(solution)/shard_map/ppermute | solution.py:310
  39.0 8.6 %copy-start.1 = (bf16[4,96,2,128]{3,2,1,0:T(2,128)(2,1)S(1)}, bf16[4,96,2,128]{3,2,1,0:T(2,128)(2,1)}, u32[]{:S(2)}) copy-start(bf16[4,96,2,128]{3,2,1,0:T(2,128)(2,1)} %param.18) | copy-start | bytes 589828
  39.0 8.6 %copy-start.3 = (f32[256,256]{1,0:T(8,128)S(1)}, f32[256,256]{1,0:T(8,128)}, u32[]{:S(2)}) copy-start(f32[256,256]{1,0:T(8,128)} %get-tuple-element.28.bias_hbm) | copy-start | bytes 786436
  39.7 7.9 %collective-permute-start.6 = (bf16[1024,128]{1,0:T(8,128)(2,1)}, bf16[1024,128]{1,0:T(8,128)(2,1)S(1)}, u32[]{:S(2)}, u32[]{:S(2)}) collective-permute-start(bf16[1024,128]{1,0:T(8,128)(2,1)} %get-tuple-element.54), channel_id=1, source_target_pairs={{32,64},{33,65},{34,66},{35,67},{36,68},{37,69},{38,70},{39,71},{4... | collective-permute-start | bytes 786440 | tf_op jit(solution)/shard_map/ppermute | solution.py:310
  41.7 6.0 %collective-permute-start.7 = (bf16[1024,128]{1,0:T(8,128)(2,1)S(1)}, bf16[1024,128]{1,0:T(8,128)(2,1)S(1)}, u32[]{:S(2)}, u32[]{:S(2)}) collective-permute-start(bf16[1024,128]{1,0:T(8,128)(2,1)S(1)} %get-tuple-element.53), channel_id=1, source_target_pairs={{0,32},{1,33},{2,34},{3,35},{4,36},{5,37},{6,38},{7,39},{8,40},{9,... | collective-permute-start | bytes 786440 | tf_op jit(solution)/shard_map/ppermute | solution.py:310
  42.9 1.3 %collective-permute-start.10 = (bf16[384,128]{1,0:T(8,128)(2,1)S(1)}, bf16[384,128]{1,0:T(8,128)(2,1)S(1)}, u32[]{:S(2)}, u32[]{:S(2)}) collective-permute-start(bf16[384,128]{1,0:T(8,128)(2,1)S(1)} %collective-permute-done.4.more_4_), channel_id=1, source_target_pairs={{0,32},{1,33},{2,34},{3,35},{4,36},{5,37},{6,38},{7,39},{8,40},{9,... | collective-permute-start | bytes 294920 | tf_op jit(solution)/shard_map/ppermute | solution.py:310
  43.0 1.7 %collective-permute-start.11 = (bf16[384,128]{1,0:T(8,128)(2,1)S(1)}, bf16[384,128]{1,0:T(8,128)(2,1)S(1)}, u32[]{:S(2)}, u32[]{:S(2)}) collective-permute-start(bf16[384,128]{1,0:T(8,128)(2,1)S(1)} %collective-permute-done.5.more_6_), channel_id=1, source_target_pairs={{0,32},{1,33},{2,34},{3,35},{4,36},{5,37},{6,38},{7,39},{8,40},{9,... | collective-permute-start | bytes 294920 | tf_op jit(solution)/shard_map/ppermute | solution.py:310
  43.4 1.3 %collective-permute-start.8 = (bf16[384,128]{1,0:T(8,128)(2,1)S(1)}, bf16[384,128]{1,0:T(8,128)(2,1)S(1)}, u32[]{:S(2)}, u32[]{:S(2)}) collective-permute-start(bf16[384,128]{1,0:T(8,128)(2,1)S(1)} %broadcast_select_fusion.2.more_0_), channel_id=1, source_target_pairs={{0,32},{1,33},{2,34},{3,35},{4,36},{5,37},{6,38},{7,39},{8,40},{9,... | collective-permute-start | bytes 294920 | tf_op jit(solution)/shard_map/ppermute | solution.py:310
  44.2 1.3 %collective-permute-start.9 = (bf16[384,128]{1,0:T(8,128)(2,1)S(1)}, bf16[384,128]{1,0:T(8,128)(2,1)S(1)}, u32[]{:S(2)}, u32[]{:S(2)}) collective-permute-start(bf16[384,128]{1,0:T(8,128)(2,1)S(1)} %collective-permute-done.3.more_2_), channel_id=1, source_target_pairs={{0,32},{1,33},{2,34},{3,35},{4,36},{5,37},{6,38},{7,39},{8,40},{9,... | collective-permute-start | bytes 294920 | tf_op jit(solution)/shard_map/ppermute | solution.py:310
  55.7 5.9 %collective-permute-start.12 = (bf16[384,128]{1,0:T(8,128)(2,1)S(1)}, bf16[384,128]{1,0:T(8,128)(2,1)S(1)}, u32[]{:S(2)}, u32[]{:S(2)}) collective-permute-start(bf16[384,128]{1,0:T(8,128)(2,1)S(1)} %get-tuple-element.39), channel_id=1, source_target_pairs={{32,64},{33,65},{34,66},{35,67},{36,68},{37,69},{38,70},{39,71},{4... | collective-permute-start | bytes 294920 | tf_op jit(solution)/shard_map/ppermute | solution.py:310
  57.6 4.0 %collective-permute-start.13 = (bf16[384,128]{1,0:T(8,128)(2,1)S(1)}, bf16[384,128]{1,0:T(8,128)(2,1)S(1)}, u32[]{:S(2)}, u32[]{:S(2)}) collective-permute-start(bf16[384,128]{1,0:T(8,128)(2,1)S(1)} %get-tuple-element.40), channel_id=1, source_target_pairs={{0,32},{1,33},{2,34},{3,35},{4,36},{5,37},{6,38},{7,39},{8,40},{9,... | collective-permute-start | bytes 294920 | tf_op jit(solution)/shard_map/ppermute | solution.py:310
  62.0 8.3 %collective-permute-start.15 = (bf16[384,512]{1,0:T(8,128)(2,1)S(1)}, bf16[384,512]{1,0:T(8,128)(2,1)S(1)}, u32[]{:S(2)}, u32[]{:S(2)}) collective-permute-start(bf16[384,512]{1,0:T(8,128)(2,1)S(1)} %fusion.1), channel_id=1, source_target_pairs={{0,32},{1,33},{2,34},{3,35},{4,36},{5,37},{6,38},{7,39},{8,40},{9,... | collective-permute-start | bytes 1179656 | tf_op jit(solution)/shard_map/ppermute | solution.py:310
  63.3 19.1 %all-to-all-start.1 = ((bf16[16,64,256]{2,1,0:T(8,128)(2,1)}), bf16[16,64,256]{2,1,0:T(8,128)(2,1)S(1)}, u32[]{:S(2)}, u32[]{:S(2)}) async-start(bf16[16,64,256]{2,1,0:T(8,128)(2,1)} %bitcast.18), calls=%async_computation.1 | async-start | bytes 1048576 | tf_op jit(solution)/shard_map/all_to_all | solution.py:409
  70.6 13.0 %collective-permute-start.16 = (bf16[384,128]{1,0:T(8,128)(2,1)S(1)}, bf16[384,128]{1,0:T(8,128)(2,1)S(1)}, u32[]{:S(2)}, u32[]{:S(2)}) collective-permute-start(bf16[384,128]{1,0:T(8,128)(2,1)S(1)} %get-tuple-element.55), channel_id=1, source_target_pairs={{0,64},{1,65},{2,66},{3,67},{4,68},{5,69},{6,70},{7,71},{8,72},{9,... | collective-permute-start | bytes 294920 | tf_op jit(solution)/shard_map/ppermute | solution.py:310
  71.1 12.6 %collective-permute-start.17 = (bf16[384,128]{1,0:T(8,128)(2,1)S(1)}, bf16[384,128]{1,0:T(8,128)(2,1)S(1)}, u32[]{:S(2)}, u32[]{:S(2)}) collective-permute-start(bf16[384,128]{1,0:T(8,128)(2,1)S(1)} %get-tuple-element.57), channel_id=1, source_target_pairs={{0,128},{1,129},{2,130},{3,131},{4,132},{5,133},{6,134},{7,135},{8... | collective-permute-start | bytes 294920 | tf_op jit(solution)/shard_map/ppermute | solution.py:310
  73.2 10.5 %collective-permute-start.18 = (bf16[384,128]{1,0:T(8,128)(2,1)S(1)}, bf16[384,128]{1,0:T(8,128)(2,1)S(1)}, u32[]{:S(2)}, u32[]{:S(2)}) collective-permute-start(bf16[384,128]{1,0:T(8,128)(2,1)S(1)} %get-tuple-element.56), channel_id=1, source_target_pairs={{0,192},{1,193},{2,194},{3,195},{4,196},{5,197},{6,198},{7,199},{8... | collective-permute-start | bytes 294920 | tf_op jit(solution)/shard_map/ppermute | solution.py:310
  82.6 7.7 %collective-permute-start.14 = (bf16[32,256]{1,0:T(8,128)(2,1)S(1)}, bf16[32,256]{1,0:T(8,128)(2,1)S(1)}, u32[]{:S(2)}, u32[]{:S(2)}) collective-permute-start(bf16[32,256]{1,0:T(8,128)(2,1)S(1)} %fusion.18), channel_id=1, source_target_pairs={{0,1},{1,0},{2,3},{3,2},{4,5},{5,4},{6,7},{7,6},{8,9},{9,8},{10,11... | collective-permute-start | bytes 49160 | tf_op jit(solution)/shard_map/ppermute | solution.py:310
  (3 other events, 10.1 us)

commit v8 on v7

--- a/solution.py
+++ b/solution.py
@@ -284,7 +284,7 @@
         in_specs=[smem] + [vmem] * 8,
         out_specs=(vmem,) * 3,
         scratch_shapes=[pltpu.VMEM((2, 64, 128), F32), pltpu.VMEM((2, 72, 128), F32), pltpu.VMEM((256, 128), F32)],
-        cost_estimate=pl.CostEstimate(flops=10**9, transcendentals=0, bytes_accessed=10**6),
+        cost_estimate=pl.CostEstimate(flops=4 * 10**9, transcendentals=0, bytes_accessed=10**6),
     )(
         first_row.astype(jnp.int32)[None],
         w_tgt.transpose(2, 3, 0, 1).reshape(9, 8, 8),
@@ -351,8 +351,8 @@
     next_ = moved(next_e, lambda a, b: (a, b + 1 if b % 2 else b - 1))
     upper = lax.broadcasted_iota(jnp.int32, pair.shape, 0) < 2 * cols
     share = jnp.where(upper, pair, next_)
+    w_src, b_src, w_tgt, b_tgt, share = lax.optimization_barrier((w_src, b_src, w_tgt, b_tgt, share))
     weights = filters(w_src, b_src, w_tgt, b_tgt, w_out, t * rows_k, rows_k * n_tgt)
-    share, *weights = lax.optimization_barrier((share, *weights))
     shares = [share]
     for m in range(1, hops):
         shares.append(moved(share, lambda a, b, m=m: (a ^ (2 * m), b)))
@@ -364,7 +364,8 @@
     src_t = lax.all_to_all(
         jnp.broadcast_to(both[None], (plane, 2 * block, pixels)), ("y", "x"), 0, 0, tiled=True
     ).reshape(chans, pixels)
-    src_t, *shares = lax.optimization_barrier((src_t, *shares))
+    src_t, w0, w1, w2, *shares = lax.optimization_barrier((src_t, *weights, *shares))
+    weights = (w0, w1, w2)
     halos = []
     for mine in shares:
         halos += [mine, moved(mine, near_row)]

time: 91.5 us -> 89 us (0.973)
  waiting for transfers between devices: 28.1 us -> 22.6 us
  starting transfers between devices: 43.7 us -> 46.4 us
  local copies, waits for them, and re-layouts: 3.97 us -> 4.91 us
    ppermute x19, waiting for transfers between devices: 19.8 us -> 14.4 us  [moved(): return lax.ppermute(x, SRC + TGT, pairs)]
    ppermute x19, starting transfers between devices: 22.6 us -> 25.3 us  [moved(): return lax.ppermute(x, SRC + TGT, pairs)]
    unnamed x12, local copies, waits for them, and re-layouts: 0.73 us -> 1.67 us
  transfers between devices with their start and end apart: 21 -> 21, of which waited for: 10 -> 9; matrix products, arithmetic and copies ran while one was open for 6% -> 6% of each run, Pallas kernels for 3% -> 3%
where the time goes in v8:
time: 89 us; the launch traced here: 88.5 us
  starting transfers between devices  46.4 us (52%)
  waiting for transfers between devices  22.6 us (25%)
  Pallas kernels  10.6 us (12%)
  local copies, waits for them, and re-layouts  4.91 us (6%)
  matrix products  1.86 us (2%)
  other arithmetic  1.12 us (1%)
    ppermute x19, starting transfers between devices, moved(): return lax.ppermute(x, SRC + TGT, pairs)  25.3 us
    ppermute x19, waiting for transfers between devices, moved(): return lax.ppermute(x, SRC + TGT, pairs)  14.4 us
    all_to_all x1, starting transfers between devices, body(): lax.all_to_all(jnp.broadcast_to(both[None], (plane, 2 * block, pixels)),...  14.2 us
    all_to_all x1, waiting for transfers between devices, body(): lax.all_to_all(part.astype(BF).reshape(plane, 2 * block, pixels), ('y', '...  8.25 us
    pallas_call x1, Pallas kernels, conv(): pl.pallas_call(functools.partial(conv_kernel, cols, scale), out_shape=(ja...  7.97 us
    all_to_all x1, starting transfers between devices, body(): lax.all_to_all(part.astype(BF).reshape(plane, 2 * block, pixels), ('y', '...  6.93 us
    pallas_call x1, Pallas kernels, filters(): pl.pallas_call(functools.partial(filters_kernel, total_rows), out_shape=(...  2.66 us
  transfers between devices with their start and end apart: 21, of which 9 were waited for; matrix products, arithmetic and copies ran while one was open for 6% of the time, Pallas kernels for 3%

profile of v8, /device:TPU:32, one launch (start us, length us, event | category | flops | bytes accessed | tf_op | source)
XLA Modules:
  0.0 88.5 jit_solution(4133158059610907441)
XLA Ops:
  1.4 6.3 %collective-permute-start = (bf16[32,256]{1,0:T(8,128)(2,1)S(1)}, bf16[32,256]{1,0:T(8,128)(2,1)S(1)}, u32[]{:S(2)}, u32[]{:S(2)}) collective-permute-start(bf16[32,256]{1,0:T(8,128)(2,1)S(1)} %bitcast_bitcast_fusion), channel_id=1, source_target_pairs={{0,1},{1,0},{2,3},{3,2},{4,5},{5,4},{6,7},{7,6},{8,9},{9,8},{10,11... | collective-permute-start | bytes 49160 | tf_op jit(solution)/shard_map/ppermute | solution.py:310
  10.2 0.8 broadcast_in_dim.18
  11.0 14.2 %all-to-all-start = ((bf16[16,64,256]{2,1,0:T(8,128)(2,1)}), bf16[16,64,256]{2,1,0:T(8,128)(2,1)S(1)}, u32[]{:S(2)}, u32[]{:S(2)}) async-start(bf16[16,64,256]{2,1,0:T(8,128)(2,1)} %broadcast_in_dim.18), calls=%async_computation | async-start | bytes 1048576 | tf_op jit(solution)/shard_map/all_to_all | solution.py:364
  25.3 1.1 %collective-permute-start.3 = (bf16[384,128]{1,0:T(8,128)(2,1)S(1)}, bf16[384,128]{1,0:T(8,128)(2,1)S(1)}, u32[]{:S(2)}, u32[]{:S(2)}) collective-permute-start(bf16[384,128]{1,0:T(8,128)(2,1)S(1)} %broadcast_select_fusion.2.more_0_), channel_id=1, source_target_pairs={{0,64},{1,65},{2,66},{3,67},{4,68},{5,69},{6,70},{7,71},{8,72},{9,... | collective-permute-start | bytes 294920 | tf_op jit(solution)/shard_map/ppermute | solution.py:310
  26.4 1.5 %collective-permute-start.4 = (bf16[384,128]{1,0:T(8,128)(2,1)S(1)}, bf16[384,128]{1,0:T(8,128)(2,1)S(1)}, u32[]{:S(2)}, u32[]{:S(2)}) collective-permute-start(bf16[384,128]{1,0:T(8,128)(2,1)S(1)} %broadcast_select_fusion.2.more_0_), channel_id=1, source_target_pairs={{0,128},{1,129},{2,130},{3,131},{4,132},{5,133},{6,134},{7,135},{8... | collective-permute-start | bytes 294920 | tf_op jit(solution)/shard_map/ppermute | solution.py:310
  27.9 1.0 %collective-permute-start.5 = (bf16[384,128]{1,0:T(8,128)(2,1)S(1)}, bf16[384,128]{1,0:T(8,128)(2,1)S(1)}, u32[]{:S(2)}, u32[]{:S(2)}) collective-permute-start(bf16[384,128]{1,0:T(8,128)(2,1)S(1)} %broadcast_select_fusion.2.more_0_), channel_id=1, source_target_pairs={{0,192},{1,193},{2,194},{3,195},{4,196},{5,197},{6,198},{7,199},{8... | collective-permute-start | bytes 294920 | tf_op jit(solution)/shard_map/ppermute | solution.py:310
  28.9 2.7 %shard_map.130 = (bf16[64,240]{1,0:T(8,128)(2,1)}, bf16[72,256]{1,0:T(8,128)(2,1)}, f32[256,256]{1,0:T(8,128)}) custom-call(s32[1]{0:T(128)} %bitcast.7.row_ref, bf16[9,8,8]{2,1,0:T(8,128)(2,1)} %bitcast.62, bf16[3,3,8]{2,1,0:T(4,128)(2,1)} %bitcast.63, f32[1,8]{1,0:T(1,128)} %bitcast.64, f32[1,8]{1,0:T(1,128)} %bitcast.65, f32[1,8]{1,0:T(1,128)} %bitcast.66, ...), custom_call_target="tpu_custom_call" | custom-call | flops 4000000000 | bytes 1000000 | tf_op jit(solution)/shard_map/pallas_call | solution.py:277
  31.6 2.2 %collective-permute-done.4.more_4_ = bf16[384,128]{1,0:T(8,128)(2,1)S(1)} collective-permute-done((bf16[384,128]{1,0:T(8,128)(2,1)S(1)}, bf16[384,128]{1,0:T(8,128)(2,1)S(1)}, u32[]{:S(2)}, u32[]{:S(2)}) %collective-permute-start.4) | collective-permute-done | bytes 98336 | tf_op jit(solution)/shard_map/ppermute | solution.py:310
  33.8 2.5 %collective-permute-done.5.more_6_ = bf16[384,128]{1,0:T(8,128)(2,1)S(1)} collective-permute-done((bf16[384,128]{1,0:T(8,128)(2,1)S(1)}, bf16[384,128]{1,0:T(8,128)(2,1)S(1)}, u32[]{:S(2)}, u32[]{:S(2)}) %collective-permute-start.5) | collective-permute-done | bytes 98336 | tf_op jit(solution)/shard_map/ppermute | solution.py:310
  36.4 2.1 %collective-permute-start.6 = (bf16[1024,128]{1,0:T(8,128)(2,1)S(1)}, bf16[1024,128]{1,0:T(8,128)(2,1)S(1)}, u32[]{:S(2)}, u32[]{:S(2)}) collective-permute-start(bf16[1024,128]{1,0:T(8,128)(2,1)S(1)} %get-tuple-element.62), channel_id=1, source_target_pairs={{32,64},{33,65},{34,66},{35,67},{36,68},{37,69},{38,70},{39,71},{4... | collective-permute-start | bytes 786440 | tf_op jit(solution)/shard_map/ppermute | solution.py:310
  38.5 1.2 %collective-permute-start.7 = (bf16[1024,128]{1,0:T(8,128)(2,1)S(1)}, bf16[1024,128]{1,0:T(8,128)(2,1)S(1)}, u32[]{:S(2)}, u32[]{:S(2)}) collective-permute-start(bf16[1024,128]{1,0:T(8,128)(2,1)S(1)} %get-tuple-element.61), channel_id=1, source_target_pairs={{0,32},{1,33},{2,34},{3,35},{4,36},{5,37},{6,38},{7,39},{8,40},{9,... | collective-permute-start | bytes 786440 | tf_op jit(solution)/shard_map/ppermute | solution.py:310
  42.3 1.9 %collective-permute-done.6.far_ref = bf16[1024,128]{1,0:T(8,128)(2,1)S(1)} collective-permute-done((bf16[1024,128]{1,0:T(8,128)(2,1)S(1)}, bf16[1024,128]{1,0:T(8,128)(2,1)S(1)}, u32[]{:S(2)}, u32[]{:S(2)}) %collective-permute-start.6) | collective-permute-done | bytes 262176 | tf_op jit(solution)/shard_map/ppermute | solution.py:310
  44.3 0.9 %copy-done.3 = f32[256,256]{1,0:T(8,128)S(1)} copy-done((f32[256,256]{1,0:T(8,128)S(1)}, f32[256,256]{1,0:T(8,128)}, u32[]{:S(2)}) %copy-start.3) | copy-done | bytes 262168
  45.2 8.0 %shard_map.131 = (bf16[768,128]{1,0:T(8,128)(2,1)}, f32[384,256]{1,0:T(8,128)S(1)}, bf16[384,128]{1,0:T(8,128)(2,1)S(1)}, bf16[384,128]{1,0:T(8,128)(2,1)S(1)}) custom-call(s32[3]{0:T(128)S(1)} %pad_add_fusion.spot_ref, bf16[64,240]{1,0:T(8,128)(2,1)S(1)} %copy-done.5, bf16[72,256]{1,0:T(8,128)(2,1)S(1)} %copy-done.4, f32[256,256]{1,0:T(8,128)S(1)} %copy-done.3, ...), custom_call_target="tpu_custom_call" | custom-call | flops 4000000000 | bytes 4000000 | tf_op jit(solution)/shard_map/pallas_call | solution.py:171
  53.2 1.9 %collective-permute-start.12 = (bf16[384,128]{1,0:T(8,128)(2,1)S(1)}, bf16[384,128]{1,0:T(8,128)(2,1)S(1)}, u32[]{:S(2)}, u32[]{:S(2)}) collective-permute-start(bf16[384,128]{1,0:T(8,128)(2,1)S(1)} %get-tuple-element.47), channel_id=1, source_target_pairs={{32,64},{33,65},{34,66},{35,67},{36,68},{37,69},{38,70},{39,71},{4... | collective-permute-start | bytes 294920 | tf_op jit(solution)/shard_map/ppermute | solution.py:310
  55.1 1.2 %collective-permute-start.13 = (bf16[384,128]{1,0:T(8,128)(2,1)S(1)}, bf16[384,128]{1,0:T(8,128)(2,1)S(1)}, u32[]{:S(2)}, u32[]{:S(2)}) collective-permute-start(bf16[384,128]{1,0:T(8,128)(2,1)S(1)} %get-tuple-element.48), channel_id=1, source_target_pairs={{0,32},{1,33},{2,34},{3,35},{4,36},{5,37},{6,38},{7,39},{8,40},{9,... | collective-permute-start | bytes 294920 | tf_op jit(solution)/shard_map/ppermute | solution.py:310
  56.4 2.8 %collective-permute-done.12 = bf16[384,128]{1,0:T(8,128)(2,1)S(1)} collective-permute-done((bf16[384,128]{1,0:T(8,128)(2,1)S(1)}, bf16[384,128]{1,0:T(8,128)(2,1)S(1)}, u32[]{:S(2)}, u32[]{:S(2)}) %collective-permute-start.12) | collective-permute-done | bytes 98336 | tf_op jit(solution)/shard_map/ppermute | solution.py:310
  59.6 1.3 %fusion = bf16[1024,256]{1,0:T(8,128)(2,1)} fusion(bf16[1024,384]{0,1:T(8,128)(2,1)S(1)} %bitcast.56, bf16[384,128]{1,0:T(8,128)(2,1)S(1)} %get-tuple-element.52, bf16[384,128]{1,0:T(8,128)(2,1)S(1)} %get-tuple-element.51), kind=kOutput, calls=%fused_computation.1 | convolution fusion | flops 202244096 | bytes 1507328 | tf_op jit(solution)/shard_map/dot_general | solution.py:409
  60.8 6.9 %all-to-all-start.1 = ((bf16[16,64,256]{2,1,0:T(8,128)(2,1)}), bf16[16,64,256]{2,1,0:T(8,128)(2,1)S(1)}, u32[]{:S(2)}, u32[]{:S(2)}) async-start(bf16[16,64,256]{2,1,0:T(8,128)(2,1)} %bitcast.18), calls=%async_computation.1 | async-start | bytes 1048576 | tf_op jit(solution)/shard_map/all_to_all | solution.py:410
  68.7 2.1 %collective-permute-start.17 = (bf16[384,128]{1,0:T(8,128)(2,1)S(1)}, bf16[384,128]{1,0:T(8,128)(2,1)S(1)}, u32[]{:S(2)}, u32[]{:S(2)}) collective-permute-start(bf16[384,128]{1,0:T(8,128)(2,1)S(1)} %get-tuple-element.65), channel_id=1, source_target_pairs={{0,128},{1,129},{2,130},{3,131},{4,132},{5,133},{6,134},{7,135},{8... | collective-permute-start | bytes 294920 | tf_op jit(solution)/shard_map/ppermute | solution.py:310
  70.7 1.0 %collective-permute-start.18 = (bf16[384,128]{1,0:T(8,128)(2,1)S(1)}, bf16[384,128]{1,0:T(8,128)(2,1)S(1)}, u32[]{:S(2)}, u32[]{:S(2)}) collective-permute-start(bf16[384,128]{1,0:T(8,128)(2,1)S(1)} %get-tuple-element.64), channel_id=1, source_target_pairs={{0,192},{1,193},{2,194},{3,195},{4,196},{5,197},{6,198},{7,199},{8... | collective-permute-start | bytes 294920 | tf_op jit(solution)/shard_map/ppermute | solution.py:310
  71.7 8.2 %all-to-all-done.1 = bf16[16,64,256]{2,1,0:T(8,128)(2,1)S(1)} async-done(((bf16[16,64,256]{2,1,0:T(8,128)(2,1)}), bf16[16,64,256]{2,1,0:T(8,128)(2,1)S(1)}, u32[]{:S(2)}, u32[]{:S(2)}) %all-to-all-start.1) | async-done | bytes 524320 | tf_op jit(solution)/shard_map/all_to_all | solution.py:410
  80.1 3.7 %collective-permute-start.14 = (bf16[32,256]{1,0:T(8,128)(2,1)S(1)}, bf16[32,256]{1,0:T(8,128)(2,1)S(1)}, u32[]{:S(2)}, u32[]{:S(2)}) collective-permute-start(bf16[32,256]{1,0:T(8,128)(2,1)S(1)} %fusion.18), channel_id=1, source_target_pairs={{0,1},{1,0},{2,3},{3,2},{4,5},{5,4},{6,7},{7,6},{8,9},{9,8},{10,11... | collective-permute-start | bytes 49160 | tf_op jit(solution)/shard_map/ppermute | solution.py:310
  84.5 3.3 %collective-permute-done.14 = bf16[32,256]{1,0:T(8,128)(2,1)S(1)} collective-permute-done((bf16[32,256]{1,0:T(8,128)(2,1)S(1)}, bf16[32,256]{1,0:T(8,128)(2,1)S(1)}, u32[]{:S(2)}, u32[]{:S(2)}) %collective-permute-start.14) | collective-permute-done | bytes 16416 | tf_op jit(solution)/shard_map/ppermute | solution.py:310
  (54 shorter events, 8.8 us)
Async XLA Ops:
  1.4 8.1 %collective-permute-start = (bf16[32,256]{1,0:T(8,128)(2,1)S(1)}, bf16[32,256]{1,0:T(8,128)(2,1)S(1)}, u32[]{:S(2)}, u32[]{:S(2)}) collective-permute-start(bf16[32,256]{1,0:T(8,128)(2,1)S(1)} %bitcast_bitcast_fusion), channel_id=1, source_target_pairs={{0,1},{1,0},{2,3},{3,2},{4,5},{5,4},{6,7},{7,6},{8,9},{9,8},{10,11... | collective-permute-start | bytes 49160 | tf_op jit(solution)/shard_map/ppermute | solution.py:310
  9.3 15.9 %collective-permute-start.1 = (bf16[384,128]{1,0:T(8,128)(2,1)S(1)}, bf16[384,128]{1,0:T(8,128)(2,1)S(1)}, u32[]{:S(2)}, u32[]{:S(2)}) collective-permute-start(bf16[384,128]{1,0:T(8,128)(2,1)S(1)} %pad_maximum_fusion.2), channel_id=1, source_target_pairs={{0,1},{1,0},{2,3},{3,2},{4,5},{5,4},{6,7},{7,6},{8,9},{9,8},{10,11... | collective-permute-start | bytes 294920 | tf_op jit(solution)/shard_map/ppermute | solution.py:310
  9.5 15.7 %collective-permute-start.2 = (bf16[384,128]{1,0:T(8,128)(2,1)S(1)}, bf16[384,128]{1,0:T(8,128)(2,1)S(1)}, u32[]{:S(2)}, u32[]{:S(2)}) collective-permute-start(bf16[384,128]{1,0:T(8,128)(2,1)S(1)} %pad_maximum_fusion.1), channel_id=1, source_target_pairs={{1,2},{2,1},{3,4},{4,3},{5,6},{6,5},{7,8},{8,7},{9,10},{10,9},{11,... | collective-permute-start | bytes 294920 | tf_op jit(solution)/shard_map/ppermute | solution.py:310
  11.0 25.3 %all-to-all-start = ((bf16[16,64,256]{2,1,0:T(8,128)(2,1)}), bf16[16,64,256]{2,1,0:T(8,128)(2,1)S(1)}, u32[]{:S(2)}, u32[]{:S(2)}) async-start(bf16[16,64,256]{2,1,0:T(8,128)(2,1)} %broadcast_in_dim.18), calls=%async_computation | async-start | bytes 1048576 | tf_op jit(solution)/shard_map/all_to_all | solution.py:364
  25.3 6.2 %collective-permute-start.3 = (bf16[384,128]{1,0:T(8,128)(2,1)S(1)}, bf16[384,128]{1,0:T(8,128)(2,1)S(1)}, u32[]{:S(2)}, u32[]{:S(2)}) collective-permute-start(bf16[384,128]{1,0:T(8,128)(2,1)S(1)} %broadcast_select_fusion.2.more_0_), channel_id=1, source_target_pairs={{0,64},{1,65},{2,66},{3,67},{4,68},{5,69},{6,70},{7,71},{8,72},{9,... | collective-permute-start | bytes 294920 | tf_op jit(solution)/shard_map/ppermute | solution.py:310
  26.4 7.4 %collective-permute-start.4 = (bf16[384,128]{1,0:T(8,128)(2,1)S(1)}, bf16[384,128]{1,0:T(8,128)(2,1)S(1)}, u32[]{:S(2)}, u32[]{:S(2)}) collective-permute-start(bf16[384,128]{1,0:T(8,128)(2,1)S(1)} %broadcast_select_fusion.2.more_0_), channel_id=1, source_target_pairs={{0,128},{1,129},{2,130},{3,131},{4,132},{5,133},{6,134},{7,135},{8... | collective-permute-start | bytes 294920 | tf_op jit(solution)/shard_map/ppermute | solution.py:310
  27.9 8.4 %collective-permute-start.5 = (bf16[384,128]{1,0:T(8,128)(2,1)S(1)}, bf16[384,128]{1,0:T(8,128)(2,1)S(1)}, u32[]{:S(2)}, u32[]{:S(2)}) collective-permute-start(bf16[384,128]{1,0:T(8,128)(2,1)S(1)} %broadcast_select_fusion.2.more_0_), channel_id=1, source_target_pairs={{0,192},{1,193},{2,194},{3,195},{4,196},{5,197},{6,198},{7,199},{8... | collective-permute-start | bytes 294920 | tf_op jit(solution)/shard_map/ppermute | solution.py:310
  31.6 12.6 %copy-start.2 = (bf16[4,96,1024]{2,1,0:T(8,128)(2,1)S(1)}, bf16[4,96,1024]{2,1,0:T(8,128)(2,1)}, u32[]{:S(2)}) copy-start(bf16[4,96,1024]{2,1,0:T(8,128)(2,1)} %param.12) | copy-start | bytes 2359300
  36.4 7.9 %copy-start.1 = (bf16[4,96,2,128]{3,2,1,0:T(2,128)(2,1)S(1)}, bf16[4,96,2,128]{3,2,1,0:T(2,128)(2,1)}, u32[]{:S(2)}) copy-start(bf16[4,96,2,128]{3,2,1,0:T(2,128)(2,1)} %param.18) | copy-start | bytes 589828
  36.4 7.8 %collective-permute-start.6 = (bf16[1024,128]{1,0:T(8,128)(2,1)S(1)}, bf16[1024,128]{1,0:T(8,128)(2,1)S(1)}, u32[]{:S(2)}, u32[]{:S(2)}) collective-permute-start(bf16[1024,128]{1,0:T(8,128)(2,1)S(1)} %get-tuple-element.62), channel_id=1, source_target_pairs={{32,64},{33,65},{34,66},{35,67},{36,68},{37,69},{38,70},{39,71},{4... | collective-permute-start | bytes 786440 | tf_op jit(solution)/shard_map/ppermute | solution.py:310
  38.5 5.8 %collective-permute-start.7 = (bf16[1024,128]{1,0:T(8,128)(2,1)S(1)}, bf16[1024,128]{1,0:T(8,128)(2,1)S(1)}, u32[]{:S(2)}, u32[]{:S(2)}) collective-permute-start(bf16[1024,128]{1,0:T(8,128)(2,1)S(1)} %get-tuple-element.61), channel_id=1, source_target_pairs={{0,32},{1,33},{2,34},{3,35},{4,36},{5,37},{6,38},{7,39},{8,40},{9,... | collective-permute-start | bytes 786440 | tf_op jit(solution)/shard_map/ppermute | solution.py:310
  39.7 1.3 %collective-permute-start.10 = (bf16[384,128]{1,0:T(8,128)(2,1)S(1)}, bf16[384,128]{1,0:T(8,128)(2,1)S(1)}, u32[]{:S(2)}, u32[]{:S(2)}) collective-permute-start(bf16[384,128]{1,0:T(8,128)(2,1)S(1)} %collective-permute-done.4.more_4_), channel_id=1, source_target_pairs={{0,32},{1,33},{2,34},{3,35},{4,36},{5,37},{6,38},{7,39},{8,40},{9,... | collective-permute-start | bytes 294920 | tf_op jit(solution)/shard_map/ppermute | solution.py:310
  39.8 4.5 %copy-start.5 = (bf16[64,240]{1,0:T(8,128)(2,1)S(1)}, bf16[64,240]{1,0:T(8,128)(2,1)}, u32[]{:S(2)}) copy-start(bf16[64,240]{1,0:T(8,128)(2,1)} %get-tuple-element.36.wf_hbm) | copy-start | bytes 92164
  39.8 1.7 %collective-permute-start.11 = (bf16[384,128]{1,0:T(8,128)(2,1)S(1)}, bf16[384,128]{1,0:T(8,128)(2,1)S(1)}, u32[]{:S(2)}, u32[]{:S(2)}) collective-permute-start(bf16[384,128]{1,0:T(8,128)(2,1)S(1)} %collective-permute-done.5.more_6_), channel_id=1, source_target_pairs={{0,32},{1,33},{2,34},{3,35},{4,36},{5,37},{6,38},{7,39},{8,40},{9,... | collective-permute-start | bytes 294920 | tf_op jit(solution)/shard_map/ppermute | solution.py:310
  40.2 1.3 %collective-permute-start.8 = (bf16[384,128]{1,0:T(8,128)(2,1)S(1)}, bf16[384,128]{1,0:T(8,128)(2,1)S(1)}, u32[]{:S(2)}, u32[]{:S(2)}) collective-permute-start(bf16[384,128]{1,0:T(8,128)(2,1)S(1)} %broadcast_select_fusion.2.more_0_), channel_id=1, source_target_pairs={{0,32},{1,33},{2,34},{3,35},{4,36},{5,37},{6,38},{7,39},{8,40},{9,... | collective-permute-start | bytes 294920 | tf_op jit(solution)/shard_map/ppermute | solution.py:310
  41.0 1.3 %collective-permute-start.9 = (bf16[384,128]{1,0:T(8,128)(2,1)S(1)}, bf16[384,128]{1,0:T(8,128)(2,1)S(1)}, u32[]{:S(2)}, u32[]{:S(2)}) collective-permute-start(bf16[384,128]{1,0:T(8,128)(2,1)S(1)} %collective-permute-done.3.more_2_), channel_id=1, source_target_pairs={{0,32},{1,33},{2,34},{3,35},{4,36},{5,37},{6,38},{7,39},{8,40},{9,... | collective-permute-start | bytes 294920 | tf_op jit(solution)/shard_map/ppermute | solution.py:310
  53.2 5.9 %collective-permute-start.12 = (bf16[384,128]{1,0:T(8,128)(2,1)S(1)}, bf16[384,128]{1,0:T(8,128)(2,1)S(1)}, u32[]{:S(2)}, u32[]{:S(2)}) collective-permute-start(bf16[384,128]{1,0:T(8,128)(2,1)S(1)} %get-tuple-element.47), channel_id=1, source_target_pairs={{32,64},{33,65},{34,66},{35,67},{36,68},{37,69},{38,70},{39,71},{4... | collective-permute-start | bytes 294920 | tf_op jit(solution)/shard_map/ppermute | solution.py:310
  55.1 4.0 %collective-permute-start.13 = (bf16[384,128]{1,0:T(8,128)(2,1)S(1)}, bf16[384,128]{1,0:T(8,128)(2,1)S(1)}, u32[]{:S(2)}, u32[]{:S(2)}) collective-permute-start(bf16[384,128]{1,0:T(8,128)(2,1)S(1)} %get-tuple-element.48), channel_id=1, source_target_pairs={{0,32},{1,33},{2,34},{3,35},{4,36},{5,37},{6,38},{7,39},{8,40},{9,... | collective-permute-start | bytes 294920 | tf_op jit(solution)/shard_map/ppermute | solution.py:310
  59.5 8.3 %collective-permute-start.15 = (bf16[384,512]{1,0:T(8,128)(2,1)S(1)}, bf16[384,512]{1,0:T(8,128)(2,1)S(1)}, u32[]{:S(2)}, u32[]{:S(2)}) collective-permute-start(bf16[384,512]{1,0:T(8,128)(2,1)S(1)} %fusion.1), channel_id=1, source_target_pairs={{0,32},{1,33},{2,34},{3,35},{4,36},{5,37},{6,38},{7,39},{8,40},{9,... | collective-permute-start | bytes 1179656 | tf_op jit(solution)/shard_map/ppermute | solution.py:310
  60.8 19.1 %all-to-all-start.1 = ((bf16[16,64,256]{2,1,0:T(8,128)(2,1)}), bf16[16,64,256]{2,1,0:T(8,128)(2,1)S(1)}, u32[]{:S(2)}, u32[]{:S(2)}) async-start(bf16[16,64,256]{2,1,0:T(8,128)(2,1)} %bitcast.18), calls=%async_computation.1 | async-start | bytes 1048576 | tf_op jit(solution)/shard_map/all_to_all | solution.py:410
  68.2 15.6 %collective-permute-start.16 = (bf16[384,128]{1,0:T(8,128)(2,1)S(1)}, bf16[384,128]{1,0:T(8,128)(2,1)S(1)}, u32[]{:S(2)}, u32[]{:S(2)}) collective-permute-start(bf16[384,128]{1,0:T(8,128)(2,1)S(1)} %get-tuple-element.63), channel_id=1, source_target_pairs={{0,64},{1,65},{2,66},{3,67},{4,68},{5,69},{6,70},{7,71},{8,72},{9,... | collective-permute-start | bytes 294920 | tf_op jit(solution)/shard_map/ppermute | solution.py:310
  68.7 15.1 %collective-permute-start.17 = (bf16[384,128]{1,0:T(8,128)(2,1)S(1)}, bf16[384,128]{1,0:T(8,128)(2,1)S(1)}, u32[]{:S(2)}, u32[]{:S(2)}) collective-permute-start(bf16[384,128]{1,0:T(8,128)(2,1)S(1)} %get-tuple-element.65), channel_id=1, source_target_pairs={{0,128},{1,129},{2,130},{3,131},{4,132},{5,133},{6,134},{7,135},{8... | collective-permute-start | bytes 294920 | tf_op jit(solution)/shard_map/ppermute | solution.py:310
  70.7 13.0 %collective-permute-start.18 = (bf16[384,128]{1,0:T(8,128)(2,1)S(1)}, bf16[384,128]{1,0:T(8,128)(2,1)S(1)}, u32[]{:S(2)}, u32[]{:S(2)}) collective-permute-start(bf16[384,128]{1,0:T(8,128)(2,1)S(1)} %get-tuple-element.64), channel_id=1, source_target_pairs={{0,192},{1,193},{2,194},{3,195},{4,196},{5,197},{6,198},{7,199},{8... | collective-permute-start | bytes 294920 | tf_op jit(solution)/shard_map/ppermute | solution.py:310
  80.1 7.7 %collective-permute-start.14 = (bf16[32,256]{1,0:T(8,128)(2,1)S(1)}, bf16[32,256]{1,0:T(8,128)(2,1)S(1)}, u32[]{:S(2)}, u32[]{:S(2)}) collective-permute-start(bf16[32,256]{1,0:T(8,128)(2,1)S(1)} %fusion.18), channel_id=1, source_target_pairs={{0,1},{1,0},{2,3},{3,2},{4,5},{5,4},{6,7},{7,6},{8,9},{9,8},{10,11... | collective-permute-start | bytes 49160 | tf_op jit(solution)/shard_map/ppermute | solution.py:310
  (3 other events, 6.1 us)

commit v9 on v8

--- a/solution.py
+++ b/solution.py
@@ -107,7 +107,8 @@
         kind = 0 if l == 0 else 2 if l == cols - 1 else 1
         window = rows[pl.ds(l * group, 3 * group), :]
         u = jnp.dot(wf, window, preferred_element_type=F32)
-        u = u + bias_ref[pl.ds(kind * 64, 64), :]
+        b = bias_ref[pl.ds(kind * 64, 64), :]
+        u = u + jnp.concatenate([b, b], 1)
         th = jnp.tanh(u)
         q = u * th
         g = (1.0 + u) + th * (1.0 - q)
@@ -118,6 +119,7 @@
         out = []
         for o in range(8):
             w = bias_ref[pl.ds(192 + o * 8, 8), :]
+            w = jnp.concatenate([w, w], 1)
             total = total + w * s[o * 8:o * 8 + 8]
             out.append(g[o * 8:o * 8 + 8] * (cot * (0.5 * w)))
         gp[pl.ds((l + 1) * 64, 64), :] = jnp.concatenate(out, 0).astype(BF)
@@ -219,7 +221,7 @@
 def filters_kernel(
     total_rows,
     row_ref, wt_ref, ws_ref, b_src_ref, b_tgt_ref, w_out_ref, spread_ref, mask_ref, place_ref,
-    wf_ref, wb_ref, bias_ref, forward, adjoint, bias,
+    wf_ref, wb_ref, bias_ref, forward, adjoint,
 ):
     over_first = (((0,), (0,)), ((), ()))
     source = lanes = None
@@ -265,10 +267,9 @@
                     row = row_ref[0] + (m + d - 3)
                     inside = jnp.logical_and(row >= 0, row < total_rows)
                     total = total + jnp.where(inside, along[d], 0.0)
-            bias[pl.ds(kind * 64 + m, 8, stride=8), :] = jnp.broadcast_to(0.5 * total, (8, 128))
+            bias_ref[pl.ds(kind * 64 + m, 8, stride=8), :] = jnp.broadcast_to(0.5 * total, (8, 128))
     for m in range(8):
-        bias[pl.ds(192 + m, 8, stride=8), :] = jnp.broadcast_to(w_out, (8, 128))
-    bias_ref[...] = jnp.concatenate([bias[...], bias[...]], 1)
+        bias_ref[pl.ds(192 + m, 8, stride=8), :] = jnp.broadcast_to(w_out, (8, 128))
 
 
 def filters(w_src, b_src, w_tgt, b_tgt, w_out, first_row, total_rows):
@@ -279,11 +280,11 @@
         out_shape=(
             jax.ShapeDtypeStruct((64, 3 * TAPS * 8), BF),
             jax.ShapeDtypeStruct((72, 256), BF),
-            jax.ShapeDtypeStruct((256, 256), F32),
+            jax.ShapeDtypeStruct((256, 128), F32),
         ),
         in_specs=[smem] + [vmem] * 8,
         out_specs=(vmem,) * 3,
-        scratch_shapes=[pltpu.VMEM((2, 64, 128), F32), pltpu.VMEM((2, 72, 128), F32), pltpu.VMEM((256, 128), F32)],
+        scratch_shapes=[pltpu.VMEM((2, 64, 128), F32), pltpu.VMEM((2, 72, 128), F32)],
         cost_estimate=pl.CostEstimate(flops=4 * 10**9, transcendentals=0, bytes_accessed=10**6),
     )(
         first_row.astype(jnp.int32)[None],

time: 89 us -> 89.9 us (1.010)
  no operation moved by 1% of the time
where the time goes in v9:
time: 89.9 us; the launch traced here: 89.3 us
  starting transfers between devices  46.4 us (52%)
  waiting for transfers between devices  22.6 us (25%)
  Pallas kernels  10.8 us (12%)
  local copies, waits for them, and re-layouts  5.48 us (6%)
  matrix products  1.87 us (2%)
  other arithmetic  1.12 us (1%)
    ppermute x19, starting transfers between devices, moved(): return lax.ppermute(x, SRC + TGT, pairs)  25.3 us
    ppermute x19, waiting for transfers between devices, moved(): return lax.ppermute(x, SRC + TGT, pairs)  14.4 us
    all_to_all x1, starting transfers between devices, body(): lax.all_to_all(jnp.broadcast_to(both[None], (plane, 2 * block, pixels)),...  14.2 us
    all_to_all x1, waiting for transfers between devices, body(): lax.all_to_all(part.astype(BF).reshape(plane, 2 * block, pixels), ('y', '...  8.24 us
    pallas_call x1, Pallas kernels, conv(): pl.pallas_call(functools.partial(conv_kernel, cols, scale), out_shape=(ja...  8.2 us
    all_to_all x1, starting transfers between devices, body(): lax.all_to_all(part.astype(BF).reshape(plane, 2 * block, pixels), ('y', '...  6.92 us
    pallas_call x1, Pallas kernels, filters(): pl.pallas_call(functools.partial(filters_kernel, total_rows), out_shape=(...  2.61 us
    unnamed x12, local copies, waits for them, and re-layouts  2.25 us
  transfers between devices with their start and end apart: 21, of which 9 were waited for; matrix products, arithmetic and copies ran while one was open for 6% of the time, Pallas kernels for 3%

profile of v9, /device:TPU:32, one launch (start us, length us, event | category | flops | bytes accessed | tf_op | source)
XLA Modules:
  0.0 89.3 jit_solution(7697172564183529012)
XLA Ops:
  1.4 6.3 %collective-permute-start = (bf16[32,256]{1,0:T(8,128)(2,1)S(1)}, bf16[32,256]{1,0:T(8,128)(2,1)S(1)}, u32[]{:S(2)}, u32[]{:S(2)}) collective-permute-start(bf16[32,256]{1,0:T(8,128)(2,1)S(1)} %bitcast_bitcast_fusion), channel_id=1, source_target_pairs={{0,1},{1,0},{2,3},{3,2},{4,5},{5,4},{6,7},{7,6},{8,9},{9,8},{10,11... | collective-permute-start | bytes 49160 | tf_op jit(solution)/shard_map/ppermute | solution.py:311
  8.5 0.8 constant_dynamic-slice_fusion.1
  10.2 0.8 broadcast_in_dim.18
  11.0 14.2 %all-to-all-start = ((bf16[16,64,256]{2,1,0:T(8,128)(2,1)}), bf16[16,64,256]{2,1,0:T(8,128)(2,1)S(1)}, u32[]{:S(2)}, u32[]{:S(2)}) async-start(bf16[16,64,256]{2,1,0:T(8,128)(2,1)} %broadcast_in_dim.18), calls=%async_computation | async-start | bytes 1048576 | tf_op jit(solution)/shard_map/all_to_all | solution.py:365
  25.3 1.1 %collective-permute-start.3 = (bf16[384,128]{1,0:T(8,128)(2,1)S(1)}, bf16[384,128]{1,0:T(8,128)(2,1)S(1)}, u32[]{:S(2)}, u32[]{:S(2)}) collective-permute-start(bf16[384,128]{1,0:T(8,128)(2,1)S(1)} %broadcast_select_fusion.2.more_0_), channel_id=1, source_target_pairs={{0,64},{1,65},{2,66},{3,67},{4,68},{5,69},{6,70},{7,71},{8,72},{9,... | collective-permute-start | bytes 294920 | tf_op jit(solution)/shard_map/ppermute | solution.py:311
  26.4 1.5 %collective-permute-start.4 = (bf16[384,128]{1,0:T(8,128)(2,1)S(1)}, bf16[384,128]{1,0:T(8,128)(2,1)S(1)}, u32[]{:S(2)}, u32[]{:S(2)}) collective-permute-start(bf16[384,128]{1,0:T(8,128)(2,1)S(1)} %broadcast_select_fusion.2.more_0_), channel_id=1, source_target_pairs={{0,128},{1,129},{2,130},{3,131},{4,132},{5,133},{6,134},{7,135},{8... | collective-permute-start | bytes 294920 | tf_op jit(solution)/shard_map/ppermute | solution.py:311
  27.9 1.0 %collective-permute-start.5 = (bf16[384,128]{1,0:T(8,128)(2,1)S(1)}, bf16[384,128]{1,0:T(8,128)(2,1)S(1)}, u32[]{:S(2)}, u32[]{:S(2)}) collective-permute-start(bf16[384,128]{1,0:T(8,128)(2,1)S(1)} %broadcast_select_fusion.2.more_0_), channel_id=1, source_target_pairs={{0,192},{1,193},{2,194},{3,195},{4,196},{5,197},{6,198},{7,199},{8... | collective-permute-start | bytes 294920 | tf_op jit(solution)/shard_map/ppermute | solution.py:311
  28.9 2.6 %shard_map.130 = (bf16[64,240]{1,0:T(8,128)(2,1)}, bf16[72,256]{1,0:T(8,128)(2,1)}, f32[256,128]{1,0:T(8,128)}) custom-call(s32[1]{0:T(128)} %bitcast.7.row_ref, bf16[9,8,8]{2,1,0:T(8,128)(2,1)} %bitcast.62, bf16[3,3,8]{2,1,0:T(4,128)(2,1)} %bitcast.63, f32[1,8]{1,0:T(1,128)} %bitcast.64, f32[1,8]{1,0:T(1,128)} %bitcast.65, f32[1,8]{1,0:T(1,128)} %bitcast.66, ...), custom_call_target="tpu_custom_call" | custom-call | flops 4000000000 | bytes 1000000 | tf_op jit(solution)/shard_map/pallas_call | solution.py:278
  31.5 2.3 %collective-permute-done.4.more_4_ = bf16[384,128]{1,0:T(8,128)(2,1)S(1)} collective-permute-done((bf16[384,128]{1,0:T(8,128)(2,1)S(1)}, bf16[384,128]{1,0:T(8,128)(2,1)S(1)}, u32[]{:S(2)}, u32[]{:S(2)}) %collective-permute-start.4) | collective-permute-done | bytes 98336 | tf_op jit(solution)/shard_map/ppermute | solution.py:311
  33.8 2.5 %collective-permute-done.5.more_6_ = bf16[384,128]{1,0:T(8,128)(2,1)S(1)} collective-permute-done((bf16[384,128]{1,0:T(8,128)(2,1)S(1)}, bf16[384,128]{1,0:T(8,128)(2,1)S(1)}, u32[]{:S(2)}, u32[]{:S(2)}) %collective-permute-start.5) | collective-permute-done | bytes 98336 | tf_op jit(solution)/shard_map/ppermute | solution.py:311
  36.4 2.1 %collective-permute-start.6 = (bf16[1024,128]{1,0:T(8,128)(2,1)S(1)}, bf16[1024,128]{1,0:T(8,128)(2,1)S(1)}, u32[]{:S(2)}, u32[]{:S(2)}) collective-permute-start(bf16[1024,128]{1,0:T(8,128)(2,1)S(1)} %get-tuple-element.62), channel_id=1, source_target_pairs={{32,64},{33,65},{34,66},{35,67},{36,68},{37,69},{38,70},{39,71},{4... | collective-permute-start | bytes 786440 | tf_op jit(solution)/shard_map/ppermute | solution.py:311
  38.5 1.2 %collective-permute-start.7 = (bf16[1024,128]{1,0:T(8,128)(2,1)S(1)}, bf16[1024,128]{1,0:T(8,128)(2,1)S(1)}, u32[]{:S(2)}, u32[]{:S(2)}) collective-permute-start(bf16[1024,128]{1,0:T(8,128)(2,1)S(1)} %get-tuple-element.61), channel_id=1, source_target_pairs={{0,32},{1,33},{2,34},{3,35},{4,36},{5,37},{6,38},{7,39},{8,40},{9,... | collective-permute-start | bytes 786440 | tf_op jit(solution)/shard_map/ppermute | solution.py:311
  42.3 1.9 %collective-permute-done.6.far_ref = bf16[1024,128]{1,0:T(8,128)(2,1)S(1)} collective-permute-done((bf16[1024,128]{1,0:T(8,128)(2,1)S(1)}, bf16[1024,128]{1,0:T(8,128)(2,1)S(1)}, u32[]{:S(2)}, u32[]{:S(2)}) %collective-permute-start.6) | collective-permute-done | bytes 262176 | tf_op jit(solution)/shard_map/ppermute | solution.py:311
  45.8 8.2 %shard_map.131 = (bf16[768,128]{1,0:T(8,128)(2,1)}, f32[384,256]{1,0:T(8,128)S(1)}, bf16[384,128]{1,0:T(8,128)(2,1)S(1)}, bf16[384,128]{1,0:T(8,128)(2,1)S(1)}) custom-call(s32[3]{0:T(128)S(1)} %pad_add_fusion.spot_ref, bf16[64,240]{1,0:T(8,128)(2,1)S(1)} %copy-done.5, bf16[72,256]{1,0:T(8,128)(2,1)S(1)} %copy-done.4, f32[256,128]{1,0:T(8,128)S(1)} %copy-done.3, ...), custom_call_target="tpu_custom_call" | custom-call | flops 4000000000 | bytes 4000000 | tf_op jit(solution)/shard_map/pallas_call | solution.py:173
  54.0 1.9 %collective-permute-start.12 = (bf16[384,128]{1,0:T(8,128)(2,1)S(1)}, bf16[384,128]{1,0:T(8,128)(2,1)S(1)}, u32[]{:S(2)}, u32[]{:S(2)}) collective-permute-start(bf16[384,128]{1,0:T(8,128)(2,1)S(1)} %get-tuple-element.47), channel_id=1, source_target_pairs={{32,64},{33,65},{34,66},{35,67},{36,68},{37,69},{38,70},{39,71},{4... | collective-permute-start | bytes 294920 | tf_op jit(solution)/shard_map/ppermute | solution.py:311
  55.9 1.2 %collective-permute-start.13 = (bf16[384,128]{1,0:T(8,128)(2,1)S(1)}, bf16[384,128]{1,0:T(8,128)(2,1)S(1)}, u32[]{:S(2)}, u32[]{:S(2)}) collective-permute-start(bf16[384,128]{1,0:T(8,128)(2,1)S(1)} %get-tuple-element.48), channel_id=1, source_target_pairs={{0,32},{1,33},{2,34},{3,35},{4,36},{5,37},{6,38},{7,39},{8,40},{9,... | collective-permute-start | bytes 294920 | tf_op jit(solution)/shard_map/ppermute | solution.py:311
  57.2 2.8 %collective-permute-done.12 = bf16[384,128]{1,0:T(8,128)(2,1)S(1)} collective-permute-done((bf16[384,128]{1,0:T(8,128)(2,1)S(1)}, bf16[384,128]{1,0:T(8,128)(2,1)S(1)}, u32[]{:S(2)}, u32[]{:S(2)}) %collective-permute-start.12) | collective-permute-done | bytes 98336 | tf_op jit(solution)/shard_map/ppermute | solution.py:311
  60.4 1.3 %fusion = bf16[1024,256]{1,0:T(8,128)(2,1)} fusion(bf16[1024,384]{0,1:T(8,128)(2,1)S(1)} %bitcast.56, bf16[384,128]{1,0:T(8,128)(2,1)S(1)} %get-tuple-element.52, bf16[384,128]{1,0:T(8,128)(2,1)S(1)} %get-tuple-element.51), kind=kOutput, calls=%fused_computation.1 | convolution fusion | flops 202244096 | bytes 1507328 | tf_op jit(solution)/shard_map/dot_general | solution.py:410
  61.7 6.9 %all-to-all-start.1 = ((bf16[16,64,256]{2,1,0:T(8,128)(2,1)}), bf16[16,64,256]{2,1,0:T(8,128)(2,1)S(1)}, u32[]{:S(2)}, u32[]{:S(2)}) async-start(bf16[16,64,256]{2,1,0:T(8,128)(2,1)} %bitcast.18), calls=%async_computation.1 | async-start | bytes 1048576 | tf_op jit(solution)/shard_map/all_to_all | solution.py:411
  69.5 2.1 %collective-permute-start.17 = (bf16[384,128]{1,0:T(8,128)(2,1)S(1)}, bf16[384,128]{1,0:T(8,128)(2,1)S(1)}, u32[]{:S(2)}, u32[]{:S(2)}) collective-permute-start(bf16[384,128]{1,0:T(8,128)(2,1)S(1)} %get-tuple-element.65), channel_id=1, source_target_pairs={{0,128},{1,129},{2,130},{3,131},{4,132},{5,133},{6,134},{7,135},{8... | collective-permute-start | bytes 294920 | tf_op jit(solution)/shard_map/ppermute | solution.py:311
  71.5 1.0 %collective-permute-start.18 = (bf16[384,128]{1,0:T(8,128)(2,1)S(1)}, bf16[384,128]{1,0:T(8,128)(2,1)S(1)}, u32[]{:S(2)}, u32[]{:S(2)}) collective-permute-start(bf16[384,128]{1,0:T(8,128)(2,1)S(1)} %get-tuple-element.64), channel_id=1, source_target_pairs={{0,192},{1,193},{2,194},{3,195},{4,196},{5,197},{6,198},{7,199},{8... | collective-permute-start | bytes 294920 | tf_op jit(solution)/shard_map/ppermute | solution.py:311
  72.5 8.2 %all-to-all-done.1 = bf16[16,64,256]{2,1,0:T(8,128)(2,1)S(1)} async-done(((bf16[16,64,256]{2,1,0:T(8,128)(2,1)}), bf16[16,64,256]{2,1,0:T(8,128)(2,1)S(1)}, u32[]{:S(2)}, u32[]{:S(2)}) %all-to-all-start.1) | async-done | bytes 524320 | tf_op jit(solution)/shard_map/all_to_all | solution.py:411
  80.9 3.7 %collective-permute-start.14 = (bf16[32,256]{1,0:T(8,128)(2,1)S(1)}, bf16[32,256]{1,0:T(8,128)(2,1)S(1)}, u32[]{:S(2)}, u32[]{:S(2)}) collective-permute-start(bf16[32,256]{1,0:T(8,128)(2,1)S(1)} %fusion.18), channel_id=1, source_target_pairs={{0,1},{1,0},{2,3},{3,2},{4,5},{5,4},{6,7},{7,6},{8,9},{9,8},{10,11... | collective-permute-start | bytes 49160 | tf_op jit(solution)/shard_map/ppermute | solution.py:311
  85.3 3.3 %collective-permute-done.14 = bf16[32,256]{1,0:T(8,128)(2,1)S(1)} collective-permute-done((bf16[32,256]{1,0:T(8,128)(2,1)S(1)}, bf16[32,256]{1,0:T(8,128)(2,1)S(1)}, u32[]{:S(2)}, u32[]{:S(2)}) %collective-permute-start.14) | collective-permute-done | bytes 16416 | tf_op jit(solution)/shard_map/ppermute | solution.py:311
  (54 shorter events, 9.5 us)
Async XLA Ops:
  1.4 8.1 %collective-permute-start = (bf16[32,256]{1,0:T(8,128)(2,1)S(1)}, bf16[32,256]{1,0:T(8,128)(2,1)S(1)}, u32[]{:S(2)}, u32[]{:S(2)}) collective-permute-start(bf16[32,256]{1,0:T(8,128)(2,1)S(1)} %bitcast_bitcast_fusion), channel_id=1, source_target_pairs={{0,1},{1,0},{2,3},{3,2},{4,5},{5,4},{6,7},{7,6},{8,9},{9,8},{10,11... | collective-permute-start | bytes 49160 | tf_op jit(solution)/shard_map/ppermute | solution.py:311
  9.3 15.9 %collective-permute-start.1 = (bf16[384,128]{1,0:T(8,128)(2,1)S(1)}, bf16[384,128]{1,0:T(8,128)(2,1)S(1)}, u32[]{:S(2)}, u32[]{:S(2)}) collective-permute-start(bf16[384,128]{1,0:T(8,128)(2,1)S(1)} %pad_maximum_fusion.2), channel_id=1, source_target_pairs={{0,1},{1,0},{2,3},{3,2},{4,5},{5,4},{6,7},{7,6},{8,9},{9,8},{10,11... | collective-permute-start | bytes 294920 | tf_op jit(solution)/shard_map/ppermute | solution.py:311
  9.5 15.7 %collective-permute-start.2 = (bf16[384,128]{1,0:T(8,128)(2,1)S(1)}, bf16[384,128]{1,0:T(8,128)(2,1)S(1)}, u32[]{:S(2)}, u32[]{:S(2)}) collective-permute-start(bf16[384,128]{1,0:T(8,128)(2,1)S(1)} %pad_maximum_fusion.1), channel_id=1, source_target_pairs={{1,2},{2,1},{3,4},{4,3},{5,6},{6,5},{7,8},{8,7},{9,10},{10,9},{11,... | collective-permute-start | bytes 294920 | tf_op jit(solution)/shard_map/ppermute | solution.py:311
  11.0 25.3 %all-to-all-start = ((bf16[16,64,256]{2,1,0:T(8,128)(2,1)}), bf16[16,64,256]{2,1,0:T(8,128)(2,1)S(1)}, u32[]{:S(2)}, u32[]{:S(2)}) async-start(bf16[16,64,256]{2,1,0:T(8,128)(2,1)} %broadcast_in_dim.18), calls=%async_computation | async-start | bytes 1048576 | tf_op jit(solution)/shard_map/all_to_all | solution.py:365
  25.3 6.2 %collective-permute-start.3 = (bf16[384,128]{1,0:T(8,128)(2,1)S(1)}, bf16[384,128]{1,0:T(8,128)(2,1)S(1)}, u32[]{:S(2)}, u32[]{:S(2)}) collective-permute-start(bf16[384,128]{1,0:T(8,128)(2,1)S(1)} %broadcast_select_fusion.2.more_0_), channel_id=1, source_target_pairs={{0,64},{1,65},{2,66},{3,67},{4,68},{5,69},{6,70},{7,71},{8,72},{9,... | collective-permute-start | bytes 294920 | tf_op jit(solution)/shard_map/ppermute | solution.py:311
  26.4 7.4 %collective-permute-start.4 = (bf16[384,128]{1,0:T(8,128)(2,1)S(1)}, bf16[384,128]{1,0:T(8,128)(2,1)S(1)}, u32[]{:S(2)}, u32[]{:S(2)}) collective-permute-start(bf16[384,128]{1,0:T(8,128)(2,1)S(1)} %broadcast_select_fusion.2.more_0_), channel_id=1, source_target_pairs={{0,128},{1,129},{2,130},{3,131},{4,132},{5,133},{6,134},{7,135},{8... | collective-permute-start | bytes 294920 | tf_op jit(solution)/shard_map/ppermute | solution.py:311
  27.9 8.4 %collective-permute-start.5 = (bf16[384,128]{1,0:T(8,128)(2,1)S(1)}, bf16[384,128]{1,0:T(8,128)(2,1)S(1)}, u32[]{:S(2)}, u32[]{:S(2)}) collective-permute-start(bf16[384,128]{1,0:T(8,128)(2,1)S(1)} %broadcast_select_fusion.2.more_0_), channel_id=1, source_target_pairs={{0,192},{1,193},{2,194},{3,195},{4,196},{5,197},{6,198},{7,199},{8... | collective-permute-start | bytes 294920 | tf_op jit(solution)/shard_map/ppermute | solution.py:311
  31.5 12.7 %copy-start.2 = (bf16[4,96,1024]{2,1,0:T(8,128)(2,1)S(1)}, bf16[4,96,1024]{2,1,0:T(8,128)(2,1)}, u32[]{:S(2)}) copy-start(bf16[4,96,1024]{2,1,0:T(8,128)(2,1)} %param.12) | copy-start | bytes 2359300
  36.4 7.9 %copy-start.1 = (bf16[4,96,2,128]{3,2,1,0:T(2,128)(2,1)S(1)}, bf16[4,96,2,128]{3,2,1,0:T(2,128)(2,1)}, u32[]{:S(2)}) copy-start(bf16[4,96,2,128]{3,2,1,0:T(2,128)(2,1)} %param.18) | copy-start | bytes 589828
  36.4 7.9 %copy-start.3 = (f32[256,128]{1,0:T(8,128)S(1)}, f32[256,128]{1,0:T(8,128)}, u32[]{:S(2)}) copy-start(f32[256,128]{1,0:T(8,128)} %get-tuple-element.38.bias_hbm) | copy-start | bytes 393220
  36.4 7.8 %collective-permute-start.6 = (bf16[1024,128]{1,0:T(8,128)(2,1)S(1)}, bf16[1024,128]{1,0:T(8,128)(2,1)S(1)}, u32[]{:S(2)}, u32[]{:S(2)}) collective-permute-start(bf16[1024,128]{1,0:T(8,128)(2,1)S(1)} %get-tuple-element.62), channel_id=1, source_target_pairs={{32,64},{33,65},{34,66},{35,67},{36,68},{37,69},{38,70},{39,71},{4... | collective-permute-start | bytes 786440 | tf_op jit(solution)/shard_map/ppermute | solution.py:311
  38.5 5.8 %collective-permute-start.7 = (bf16[1024,128]{1,0:T(8,128)(2,1)S(1)}, bf16[1024,128]{1,0:T(8,128)(2,1)S(1)}, u32[]{:S(2)}, u32[]{:S(2)}) collective-permute-start(bf16[1024,128]{1,0:T(8,128)(2,1)S(1)} %get-tuple-element.61), channel_id=1, source_target_pairs={{0,32},{1,33},{2,34},{3,35},{4,36},{5,37},{6,38},{7,39},{8,40},{9,... | collective-permute-start | bytes 786440 | tf_op jit(solution)/shard_map/ppermute | solution.py:311
  39.7 1.3 %collective-permute-start.10 = (bf16[384,128]{1,0:T(8,128)(2,1)S(1)}, bf16[384,128]{1,0:T(8,128)(2,1)S(1)}, u32[]{:S(2)}, u32[]{:S(2)}) collective-permute-start(bf16[384,128]{1,0:T(8,128)(2,1)S(1)} %collective-permute-done.4.more_4_), channel_id=1, source_target_pairs={{0,32},{1,33},{2,34},{3,35},{4,36},{5,37},{6,38},{7,39},{8,40},{9,... | collective-permute-start | bytes 294920 | tf_op jit(solution)/shard_map/ppermute | solution.py:311
  39.8 1.7 %collective-permute-start.11 = (bf16[384,128]{1,0:T(8,128)(2,1)S(1)}, bf16[384,128]{1,0:T(8,128)(2,1)S(1)}, u32[]{:S(2)}, u32[]{:S(2)}) collective-permute-start(bf16[384,128]{1,0:T(8,128)(2,1)S(1)} %collective-permute-done.5.more_6_), channel_id=1, source_target_pairs={{0,32},{1,33},{2,34},{3,35},{4,36},{5,37},{6,38},{7,39},{8,40},{9,... | collective-permute-start | bytes 294920 | tf_op jit(solution)/shard_map/ppermute | solution.py:311
  40.2 1.3 %collective-permute-start.8 = (bf16[384,128]{1,0:T(8,128)(2,1)S(1)}, bf16[384,128]{1,0:T(8,128)(2,1)S(1)}, u32[]{:S(2)}, u32[]{:S(2)}) collective-permute-start(bf16[384,128]{1,0:T(8,128)(2,1)S(1)} %broadcast_select_fusion.2.more_0_), channel_id=1, source_target_pairs={{0,32},{1,33},{2,34},{3,35},{4,36},{5,37},{6,38},{7,39},{8,40},{9,... | collective-permute-start | bytes 294920 | tf_op jit(solution)/shard_map/ppermute | solution.py:311
  41.0 1.3 %collective-permute-start.9 = (bf16[384,128]{1,0:T(8,128)(2,1)S(1)}, bf16[384,128]{1,0:T(8,128)(2,1)S(1)}, u32[]{:S(2)}, u32[]{:S(2)}) collective-permute-start(bf16[384,128]{1,0:T(8,128)(2,1)S(1)} %collective-permute-done.3.more_2_), channel_id=1, source_target_pairs={{0,32},{1,33},{2,34},{3,35},{4,36},{5,37},{6,38},{7,39},{8,40},{9,... | collective-permute-start | bytes 294920 | tf_op jit(solution)/shard_map/ppermute | solution.py:311
  54.0 5.9 %collective-permute-start.12 = (bf16[384,128]{1,0:T(8,128)(2,1)S(1)}, bf16[384,128]{1,0:T(8,128)(2,1)S(1)}, u32[]{:S(2)}, u32[]{:S(2)}) collective-permute-start(bf16[384,128]{1,0:T(8,128)(2,1)S(1)} %get-tuple-element.47), channel_id=1, source_target_pairs={{32,64},{33,65},{34,66},{35,67},{36,68},{37,69},{38,70},{39,71},{4... | collective-permute-start | bytes 294920 | tf_op jit(solution)/shard_map/ppermute | solution.py:311
  55.9 4.0 %collective-permute-start.13 = (bf16[384,128]{1,0:T(8,128)(2,1)S(1)}, bf16[384,128]{1,0:T(8,128)(2,1)S(1)}, u32[]{:S(2)}, u32[]{:S(2)}) collective-permute-start(bf16[384,128]{1,0:T(8,128)(2,1)S(1)} %get-tuple-element.48), channel_id=1, source_target_pairs={{0,32},{1,33},{2,34},{3,35},{4,36},{5,37},{6,38},{7,39},{8,40},{9,... | collective-permute-start | bytes 294920 | tf_op jit(solution)/shard_map/ppermute | solution.py:311
  60.3 8.3 %collective-permute-start.15 = (bf16[384,512]{1,0:T(8,128)(2,1)S(1)}, bf16[384,512]{1,0:T(8,128)(2,1)S(1)}, u32[]{:S(2)}, u32[]{:S(2)}) collective-permute-start(bf16[384,512]{1,0:T(8,128)(2,1)S(1)} %fusion.1), channel_id=1, source_target_pairs={{0,32},{1,33},{2,34},{3,35},{4,36},{5,37},{6,38},{7,39},{8,40},{9,... | collective-permute-start | bytes 1179656 | tf_op jit(solution)/shard_map/ppermute | solution.py:311
  61.7 19.1 %all-to-all-start.1 = ((bf16[16,64,256]{2,1,0:T(8,128)(2,1)}), bf16[16,64,256]{2,1,0:T(8,128)(2,1)S(1)}, u32[]{:S(2)}, u32[]{:S(2)}) async-start(bf16[16,64,256]{2,1,0:T(8,128)(2,1)} %bitcast.18), calls=%async_computation.1 | async-start | bytes 1048576 | tf_op jit(solution)/shard_map/all_to_all | solution.py:411
  69.0 15.6 %collective-permute-start.16 = (bf16[384,128]{1,0:T(8,128)(2,1)S(1)}, bf16[384,128]{1,0:T(8,128)(2,1)S(1)}, u32[]{:S(2)}, u32[]{:S(2)}) collective-permute-start(bf16[384,128]{1,0:T(8,128)(2,1)S(1)} %get-tuple-element.63), channel_id=1, source_target_pairs={{0,64},{1,65},{2,66},{3,67},{4,68},{5,69},{6,70},{7,71},{8,72},{9,... | collective-permute-start | bytes 294920 | tf_op jit(solution)/shard_map/ppermute | solution.py:311
  69.5 15.1 %collective-permute-start.17 = (bf16[384,128]{1,0:T(8,128)(2,1)S(1)}, bf16[384,128]{1,0:T(8,128)(2,1)S(1)}, u32[]{:S(2)}, u32[]{:S(2)}) collective-permute-start(bf16[384,128]{1,0:T(8,128)(2,1)S(1)} %get-tuple-element.65), channel_id=1, source_target_pairs={{0,128},{1,129},{2,130},{3,131},{4,132},{5,133},{6,134},{7,135},{8... | collective-permute-start | bytes 294920 | tf_op jit(solution)/shard_map/ppermute | solution.py:311
  71.5 13.0 %collective-permute-start.18 = (bf16[384,128]{1,0:T(8,128)(2,1)S(1)}, bf16[384,128]{1,0:T(8,128)(2,1)S(1)}, u32[]{:S(2)}, u32[]{:S(2)}) collective-permute-start(bf16[384,128]{1,0:T(8,128)(2,1)S(1)} %get-tuple-element.64), channel_id=1, source_target_pairs={{0,192},{1,193},{2,194},{3,195},{4,196},{5,197},{6,198},{7,199},{8... | collective-permute-start | bytes 294920 | tf_op jit(solution)/shard_map/ppermute | solution.py:311
  80.9 7.7 %collective-permute-start.14 = (bf16[32,256]{1,0:T(8,128)(2,1)S(1)}, bf16[32,256]{1,0:T(8,128)(2,1)S(1)}, u32[]{:S(2)}, u32[]{:S(2)}) collective-permute-start(bf16[32,256]{1,0:T(8,128)(2,1)S(1)} %fusion.18), channel_id=1, source_target_pairs={{0,1},{1,0},{2,3},{3,2},{4,5},{5,4},{6,7},{7,6},{8,9},{9,8},{10,11... | collective-permute-start | bytes 49160 | tf_op jit(solution)/shard_map/ppermute | solution.py:311
  (3 other events, 2.3 us)

commit v10 on v9

--- a/solution.py
+++ b/solution.py
@@ -365,8 +365,7 @@
     src_t = lax.all_to_all(
         jnp.broadcast_to(both[None], (plane, 2 * block, pixels)), ("y", "x"), 0, 0, tiled=True
     ).reshape(chans, pixels)
-    src_t, w0, w1, w2, *shares = lax.optimization_barrier((src_t, *weights, *shares))
-    weights = (w0, w1, w2)
+    src_t, shares[1], shares[2], *weights = lax.optimization_barrier((src_t, shares[1], shares[2], *weights))
     halos = []
     for mine in shares:
         halos += [mine, moved(mine, near_row)]

time: 89.9 us -> 92.2 us (1.026)
  waiting for transfers between devices: 22.6 us -> 28.2 us
  starting transfers between devices: 46.4 us -> 43.2 us
    all_to_all x1, waiting for transfers between devices: 0.01 us -> 3.87 us  [body(): lax.all_to_all(jnp.broadcast_to(both[None], (plane, 2 * block, pixels)),...]
    all_to_all x1, starting transfers between devices: 6.92 us -> 3.57 us  [body(): lax.all_to_all(part.astype(BF).reshape(plane, 2 * block, pixels), ('y', '...]
    ppermute x19, waiting for transfers between devices: 14.4 us -> 16 us  [moved(): return lax.ppermute(x, SRC + TGT, pairs)]
where the time goes in v10:
time: 92.2 us; the launch traced here: 91.5 us
  starting transfers between devices  43.2 us (47%)
  waiting for transfers between devices  28.2 us (31%)
  Pallas kernels  10.8 us (12%)
  local copies, waits for them, and re-layouts  5.48 us (6%)
  matrix products  1.87 us (2%)
  other arithmetic  1.12 us (1%)
    ppermute x19, starting transfers between devices, moved(): return lax.ppermute(x, SRC + TGT, pairs)  25.4 us
    ppermute x19, waiting for transfers between devices, moved(): return lax.ppermute(x, SRC + TGT, pairs)  16 us
    all_to_all x1, starting transfers between devices, body(): lax.all_to_all(jnp.broadcast_to(both[None], (plane, 2 * block, pixels)),...  14.2 us
    all_to_all x1, waiting for transfers between devices, body(): lax.all_to_all(part.astype(BF).reshape(plane, 2 * block, pixels), ('y', '...  8.33 us
    pallas_call x1, Pallas kernels, conv(): pl.pallas_call(functools.partial(conv_kernel, cols, scale), out_shape=(ja...  8.19 us
    all_to_all x1, waiting for transfers between devices, body(): lax.all_to_all(jnp.broadcast_to(both[None], (plane, 2 * block, pixels)),...  3.87 us
    all_to_all x1, starting transfers between devices, body(): lax.all_to_all(part.astype(BF).reshape(plane, 2 * block, pixels), ('y', '...  3.57 us
    pallas_call x1, Pallas kernels, filters(): pl.pallas_call(functools.partial(filters_kernel, total_rows), out_shape=(...  2.6 us
  transfers between devices with their start and end apart: 21, of which 9 were waited for; matrix products, arithmetic and copies ran while one was open for 6% of the time, Pallas kernels for 3%

profile of v10, /device:TPU:32, one launch (start us, length us, event | category | flops | bytes accessed | tf_op | source)
XLA Modules:
  0.0 91.5 jit_solution(8234706651663128167)
XLA Ops:
  1.4 6.3 %collective-permute-start = (bf16[32,256]{1,0:T(8,128)(2,1)S(1)}, bf16[32,256]{1,0:T(8,128)(2,1)S(1)}, u32[]{:S(2)}, u32[]{:S(2)}) collective-permute-start(bf16[32,256]{1,0:T(8,128)(2,1)S(1)} %bitcast_bitcast_fusion), channel_id=1, source_target_pairs={{0,1},{1,0},{2,3},{3,2},{4,5},{5,4},{6,7},{7,6},{8,9},{9,8},{10,11... | collective-permute-start | bytes 49160 | tf_op jit(solution)/shard_map/ppermute | solution.py:311
  7.6 0.8 constant_dynamic-slice_fusion
  8.5 0.8 constant_dynamic-slice_fusion.1
  10.2 0.8 broadcast_in_dim.18
  11.0 14.2 %all-to-all-start = ((bf16[16,64,256]{2,1,0:T(8,128)(2,1)}), bf16[16,64,256]{2,1,0:T(8,128)(2,1)S(1)}, u32[]{:S(2)}, u32[]{:S(2)}) async-start(bf16[16,64,256]{2,1,0:T(8,128)(2,1)} %broadcast_in_dim.18), calls=%async_computation | async-start | bytes 1048576 | tf_op jit(solution)/shard_map/all_to_all | solution.py:365
  25.3 1.1 %collective-permute-start.3 = (bf16[384,128]{1,0:T(8,128)(2,1)S(1)}, bf16[384,128]{1,0:T(8,128)(2,1)S(1)}, u32[]{:S(2)}, u32[]{:S(2)}) collective-permute-start(bf16[384,128]{1,0:T(8,128)(2,1)S(1)} %broadcast_select_fusion.2.more_0_), channel_id=1, source_target_pairs={{0,64},{1,65},{2,66},{3,67},{4,68},{5,69},{6,70},{7,71},{8,72},{9,... | collective-permute-start | bytes 294920 | tf_op jit(solution)/shard_map/ppermute | solution.py:311
  26.4 1.5 %collective-permute-start.4 = (bf16[384,128]{1,0:T(8,128)(2,1)S(1)}, bf16[384,128]{1,0:T(8,128)(2,1)S(1)}, u32[]{:S(2)}, u32[]{:S(2)}) collective-permute-start(bf16[384,128]{1,0:T(8,128)(2,1)S(1)} %broadcast_select_fusion.2.more_0_), channel_id=1, source_target_pairs={{0,128},{1,129},{2,130},{3,131},{4,132},{5,133},{6,134},{7,135},{8... | collective-permute-start | bytes 294920 | tf_op jit(solution)/shard_map/ppermute | solution.py:311
  27.9 2.6 %shard_map.130 = (bf16[64,240]{1,0:T(8,128)(2,1)}, bf16[72,256]{1,0:T(8,128)(2,1)}, f32[256,128]{1,0:T(8,128)}) custom-call(s32[1]{0:T(128)} %bitcast.8.row_ref, bf16[9,8,8]{2,1,0:T(8,128)(2,1)} %bitcast.62, bf16[3,3,8]{2,1,0:T(4,128)(2,1)} %bitcast.63, f32[1,8]{1,0:T(1,128)} %bitcast.64, f32[1,8]{1,0:T(1,128)} %bitcast.65, f32[1,8]{1,0:T(1,128)} %bitcast.66, ...), custom_call_target="tpu_custom_call" | custom-call | flops 4000000000 | bytes 1000000 | tf_op jit(solution)/shard_map/pallas_call | solution.py:278
  30.5 1.5 %collective-permute-done.4.more_4_ = bf16[384,128]{1,0:T(8,128)(2,1)S(1)} collective-permute-done((bf16[384,128]{1,0:T(8,128)(2,1)S(1)}, bf16[384,128]{1,0:T(8,128)(2,1)S(1)}, u32[]{:S(2)}, u32[]{:S(2)}) %collective-permute-start.4) | collective-permute-done | bytes 98336 | tf_op jit(solution)/shard_map/ppermute | solution.py:311
  32.1 3.9 %all-to-all-done = bf16[16,64,256]{2,1,0:T(8,128)(2,1)S(1)} async-done(((bf16[16,64,256]{2,1,0:T(8,128)(2,1)}), bf16[16,64,256]{2,1,0:T(8,128)(2,1)S(1)}, u32[]{:S(2)}, u32[]{:S(2)}) %all-to-all-start) | async-done | bytes 524320 | tf_op jit(solution)/shard_map/all_to_all | solution.py:365
  36.0 2.1 %collective-permute-start.5 = (bf16[1024,128]{1,0:T(8,128)(2,1)S(1)}, bf16[1024,128]{1,0:T(8,128)(2,1)S(1)}, u32[]{:S(2)}, u32[]{:S(2)}) collective-permute-start(bf16[1024,128]{1,0:T(8,128)(2,1)S(1)} %get-tuple-element.58), channel_id=1, source_target_pairs={{32,64},{33,65},{34,66},{35,67},{36,68},{37,69},{38,70},{39,71},{4... | collective-permute-start | bytes 786440 | tf_op jit(solution)/shard_map/ppermute | solution.py:311
  38.0 1.2 %collective-permute-start.6 = (bf16[1024,128]{1,0:T(8,128)(2,1)S(1)}, bf16[1024,128]{1,0:T(8,128)(2,1)S(1)}, u32[]{:S(2)}, u32[]{:S(2)}) collective-permute-start(bf16[1024,128]{1,0:T(8,128)(2,1)S(1)} %get-tuple-element.57), channel_id=1, source_target_pairs={{0,32},{1,33},{2,34},{3,35},{4,36},{5,37},{6,38},{7,39},{8,40},{9,... | collective-permute-start | bytes 786440 | tf_op jit(solution)/shard_map/ppermute | solution.py:311
  39.2 1.0 %collective-permute-start.10 = (bf16[384,128]{1,0:T(8,128)(2,1)S(1)}, bf16[384,128]{1,0:T(8,128)(2,1)S(1)}, u32[]{:S(2)}, u32[]{:S(2)}) collective-permute-start(bf16[384,128]{1,0:T(8,128)(2,1)S(1)} %broadcast_select_fusion.2.more_0_), channel_id=1, source_target_pairs={{0,192},{1,193},{2,194},{3,195},{4,196},{5,197},{6,198},{7,199},{8... | collective-permute-start | bytes 294920 | tf_op jit(solution)/shard_map/ppermute | solution.py:311
  40.3 7.3 %collective-permute-done.10.more_6_ = bf16[384,128]{1,0:T(8,128)(2,1)S(1)} collective-permute-done((bf16[384,128]{1,0:T(8,128)(2,1)S(1)}, bf16[384,128]{1,0:T(8,128)(2,1)S(1)}, u32[]{:S(2)}, u32[]{:S(2)}) %collective-permute-start.10) | collective-permute-done | bytes 98336 | tf_op jit(solution)/shard_map/ppermute | solution.py:311
  51.0 8.2 %shard_map.131 = (bf16[768,128]{1,0:T(8,128)(2,1)}, f32[384,256]{1,0:T(8,128)S(1)}, bf16[384,128]{1,0:T(8,128)(2,1)S(1)}, bf16[384,128]{1,0:T(8,128)(2,1)S(1)}) custom-call(s32[3]{0:T(128)S(1)} %pad_add_fusion.spot_ref, bf16[64,240]{1,0:T(8,128)(2,1)S(1)} %copy-done.5, bf16[72,256]{1,0:T(8,128)(2,1)S(1)} %copy-done.4, f32[256,128]{1,0:T(8,128)S(1)} %copy-done.3, ...), custom_call_target="tpu_custom_call" | custom-call | flops 4000000000 | bytes 4000000 | tf_op jit(solution)/shard_map/pallas_call | solution.py:173
  59.2 1.9 %collective-permute-start.12 = (bf16[384,128]{1,0:T(8,128)(2,1)S(1)}, bf16[384,128]{1,0:T(8,128)(2,1)S(1)}, u32[]{:S(2)}, u32[]{:S(2)}) collective-permute-start(bf16[384,128]{1,0:T(8,128)(2,1)S(1)} %get-tuple-element.43), channel_id=1, source_target_pairs={{32,64},{33,65},{34,66},{35,67},{36,68},{37,69},{38,70},{39,71},{4... | collective-permute-start | bytes 294920 | tf_op jit(solution)/shard_map/ppermute | solution.py:311
  61.1 1.1 %collective-permute-start.13 = (bf16[384,128]{1,0:T(8,128)(2,1)S(1)}, bf16[384,128]{1,0:T(8,128)(2,1)S(1)}, u32[]{:S(2)}, u32[]{:S(2)}) collective-permute-start(bf16[384,128]{1,0:T(8,128)(2,1)S(1)} %get-tuple-element.44), channel_id=1, source_target_pairs={{0,32},{1,33},{2,34},{3,35},{4,36},{5,37},{6,38},{7,39},{8,40},{9,... | collective-permute-start | bytes 294920 | tf_op jit(solution)/shard_map/ppermute | solution.py:311
  62.2 2.9 %collective-permute-done.12 = bf16[384,128]{1,0:T(8,128)(2,1)S(1)} collective-permute-done((bf16[384,128]{1,0:T(8,128)(2,1)S(1)}, bf16[384,128]{1,0:T(8,128)(2,1)S(1)}, u32[]{:S(2)}, u32[]{:S(2)}) %collective-permute-start.12) | collective-permute-done | bytes 98336 | tf_op jit(solution)/shard_map/ppermute | solution.py:311
  65.7 1.3 %fusion = bf16[1024,256]{1,0:T(8,128)(2,1)} fusion(bf16[1024,384]{0,1:T(8,128)(2,1)S(1)} %bitcast.56, bf16[384,128]{1,0:T(8,128)(2,1)S(1)} %get-tuple-element.48, bf16[384,128]{1,0:T(8,128)(2,1)S(1)} %get-tuple-element.47), kind=kOutput, calls=%fused_computation.1 | convolution fusion | flops 202244096 | bytes 1507328 | tf_op jit(solution)/shard_map/dot_general | solution.py:409
  67.0 3.6 %all-to-all-start.1 = ((bf16[16,64,256]{2,1,0:T(8,128)(2,1)}), bf16[16,64,256]{2,1,0:T(8,128)(2,1)S(1)}, u32[]{:S(2)}, u32[]{:S(2)}) async-start(bf16[16,64,256]{2,1,0:T(8,128)(2,1)} %bitcast.18), calls=%async_computation.1 | async-start | bytes 1048576 | tf_op jit(solution)/shard_map/all_to_all | solution.py:410
  71.7 2.1 %collective-permute-start.17 = (bf16[384,128]{1,0:T(8,128)(2,1)S(1)}, bf16[384,128]{1,0:T(8,128)(2,1)S(1)}, u32[]{:S(2)}, u32[]{:S(2)}) collective-permute-start(bf16[384,128]{1,0:T(8,128)(2,1)S(1)} %get-tuple-element.61), channel_id=1, source_target_pairs={{0,128},{1,129},{2,130},{3,131},{4,132},{5,133},{6,134},{7,135},{8... | collective-permute-start | bytes 294920 | tf_op jit(solution)/shard_map/ppermute | solution.py:311
  74.5 8.3 %all-to-all-done.1 = bf16[16,64,256]{2,1,0:T(8,128)(2,1)S(1)} async-done(((bf16[16,64,256]{2,1,0:T(8,128)(2,1)}), bf16[16,64,256]{2,1,0:T(8,128)(2,1)S(1)}, u32[]{:S(2)}, u32[]{:S(2)}) %all-to-all-start.1) | async-done | bytes 524320 | tf_op jit(solution)/shard_map/all_to_all | solution.py:410
  83.0 4.2 %collective-permute-start.14 = (bf16[32,256]{1,0:T(8,128)(2,1)S(1)}, bf16[32,256]{1,0:T(8,128)(2,1)S(1)}, u32[]{:S(2)}, u32[]{:S(2)}) collective-permute-start(bf16[32,256]{1,0:T(8,128)(2,1)S(1)} %fusion.18), channel_id=1, source_target_pairs={{0,1},{1,0},{2,3},{3,2},{4,5},{5,4},{6,7},{7,6},{8,9},{9,8},{10,11... | collective-permute-start | bytes 49160 | tf_op jit(solution)/shard_map/ppermute | solution.py:311
  87.9 3.0 %collective-permute-done.14 = bf16[32,256]{1,0:T(8,128)(2,1)S(1)} collective-permute-done((bf16[32,256]{1,0:T(8,128)(2,1)S(1)}, bf16[32,256]{1,0:T(8,128)(2,1)S(1)}, u32[]{:S(2)}, u32[]{:S(2)}) %collective-permute-start.14) | collective-permute-done | bytes 16416 | tf_op jit(solution)/shard_map/ppermute | solution.py:311
  (54 shorter events, 9.0 us)
Async XLA Ops:
  1.4 8.1 %collective-permute-start = (bf16[32,256]{1,0:T(8,128)(2,1)S(1)}, bf16[32,256]{1,0:T(8,128)(2,1)S(1)}, u32[]{:S(2)}, u32[]{:S(2)}) collective-permute-start(bf16[32,256]{1,0:T(8,128)(2,1)S(1)} %bitcast_bitcast_fusion), channel_id=1, source_target_pairs={{0,1},{1,0},{2,3},{3,2},{4,5},{5,4},{6,7},{7,6},{8,9},{9,8},{10,11... | collective-permute-start | bytes 49160 | tf_op jit(solution)/shard_map/ppermute | solution.py:311
  9.3 15.9 %collective-permute-start.1 = (bf16[384,128]{1,0:T(8,128)(2,1)S(1)}, bf16[384,128]{1,0:T(8,128)(2,1)S(1)}, u32[]{:S(2)}, u32[]{:S(2)}) collective-permute-start(bf16[384,128]{1,0:T(8,128)(2,1)S(1)} %pad_maximum_fusion.2), channel_id=1, source_target_pairs={{0,1},{1,0},{2,3},{3,2},{4,5},{5,4},{6,7},{7,6},{8,9},{9,8},{10,11... | collective-permute-start | bytes 294920 | tf_op jit(solution)/shard_map/ppermute | solution.py:311
  9.5 15.7 %collective-permute-start.2 = (bf16[384,128]{1,0:T(8,128)(2,1)S(1)}, bf16[384,128]{1,0:T(8,128)(2,1)S(1)}, u32[]{:S(2)}, u32[]{:S(2)}) collective-permute-start(bf16[384,128]{1,0:T(8,128)(2,1)S(1)} %pad_maximum_fusion.1), channel_id=1, source_target_pairs={{1,2},{2,1},{3,4},{4,3},{5,6},{6,5},{7,8},{8,7},{9,10},{10,9},{11,... | collective-permute-start | bytes 294920 | tf_op jit(solution)/shard_map/ppermute | solution.py:311
  11.0 24.9 %all-to-all-start = ((bf16[16,64,256]{2,1,0:T(8,128)(2,1)}), bf16[16,64,256]{2,1,0:T(8,128)(2,1)S(1)}, u32[]{:S(2)}, u32[]{:S(2)}) async-start(bf16[16,64,256]{2,1,0:T(8,128)(2,1)} %broadcast_in_dim.18), calls=%async_computation | async-start | bytes 1048576 | tf_op jit(solution)/shard_map/all_to_all | solution.py:365
  25.3 5.2 %collective-permute-start.3 = (bf16[384,128]{1,0:T(8,128)(2,1)S(1)}, bf16[384,128]{1,0:T(8,128)(2,1)S(1)}, u32[]{:S(2)}, u32[]{:S(2)}) collective-permute-start(bf16[384,128]{1,0:T(8,128)(2,1)S(1)} %broadcast_select_fusion.2.more_0_), channel_id=1, source_target_pairs={{0,64},{1,65},{2,66},{3,67},{4,68},{5,69},{6,70},{7,71},{8,72},{9,... | collective-permute-start | bytes 294920 | tf_op jit(solution)/shard_map/ppermute | solution.py:311
  26.4 5.6 %collective-permute-start.4 = (bf16[384,128]{1,0:T(8,128)(2,1)S(1)}, bf16[384,128]{1,0:T(8,128)(2,1)S(1)}, u32[]{:S(2)}, u32[]{:S(2)}) collective-permute-start(bf16[384,128]{1,0:T(8,128)(2,1)S(1)} %broadcast_select_fusion.2.more_0_), channel_id=1, source_target_pairs={{0,128},{1,129},{2,130},{3,131},{4,132},{5,133},{6,134},{7,135},{8... | collective-permute-start | bytes 294920 | tf_op jit(solution)/shard_map/ppermute | solution.py:311
  30.5 18.9 %copy-start.2 = (bf16[4,96,1024]{2,1,0:T(8,128)(2,1)S(1)}, bf16[4,96,1024]{2,1,0:T(8,128)(2,1)}, u32[]{:S(2)}) copy-start(bf16[4,96,1024]{2,1,0:T(8,128)(2,1)} %param.12) | copy-start | bytes 2359300
  35.9 13.5 %copy-start.1 = (bf16[4,96,2,128]{3,2,1,0:T(2,128)(2,1)S(1)}, bf16[4,96,2,128]{3,2,1,0:T(2,128)(2,1)}, u32[]{:S(2)}) copy-start(bf16[4,96,2,128]{3,2,1,0:T(2,128)(2,1)} %param.18) | copy-start | bytes 589828
  35.9 13.5 %copy-start.3 = (f32[256,128]{1,0:T(8,128)S(1)}, f32[256,128]{1,0:T(8,128)}, u32[]{:S(2)}) copy-start(f32[256,128]{1,0:T(8,128)} %get-tuple-element.36.bias_hbm) | copy-start | bytes 393220
  36.0 13.4 %collective-permute-start.5 = (bf16[1024,128]{1,0:T(8,128)(2,1)S(1)}, bf16[1024,128]{1,0:T(8,128)(2,1)S(1)}, u32[]{:S(2)}, u32[]{:S(2)}) collective-permute-start(bf16[1024,128]{1,0:T(8,128)(2,1)S(1)} %get-tuple-element.58), channel_id=1, source_target_pairs={{32,64},{33,65},{34,66},{35,67},{36,68},{37,69},{38,70},{39,71},{4... | collective-permute-start | bytes 786440 | tf_op jit(solution)/shard_map/ppermute | solution.py:311
  38.0 11.4 %collective-permute-start.6 = (bf16[1024,128]{1,0:T(8,128)(2,1)S(1)}, bf16[1024,128]{1,0:T(8,128)(2,1)S(1)}, u32[]{:S(2)}, u32[]{:S(2)}) collective-permute-start(bf16[1024,128]{1,0:T(8,128)(2,1)S(1)} %get-tuple-element.57), channel_id=1, source_target_pairs={{0,32},{1,33},{2,34},{3,35},{4,36},{5,37},{6,38},{7,39},{8,40},{9,... | collective-permute-start | bytes 786440 | tf_op jit(solution)/shard_map/ppermute | solution.py:311
  39.2 8.3 %collective-permute-start.10 = (bf16[384,128]{1,0:T(8,128)(2,1)S(1)}, bf16[384,128]{1,0:T(8,128)(2,1)S(1)}, u32[]{:S(2)}, u32[]{:S(2)}) collective-permute-start(bf16[384,128]{1,0:T(8,128)(2,1)S(1)} %broadcast_select_fusion.2.more_0_), channel_id=1, source_target_pairs={{0,192},{1,193},{2,194},{3,195},{4,196},{5,197},{6,198},{7,199},{8... | collective-permute-start | bytes 294920 | tf_op jit(solution)/shard_map/ppermute | solution.py:311
  40.3 7.8 %collective-permute-start.7 = (bf16[384,128]{1,0:T(8,128)(2,1)S(1)}, bf16[384,128]{1,0:T(8,128)(2,1)S(1)}, u32[]{:S(2)}, u32[]{:S(2)}) collective-permute-start(bf16[384,128]{1,0:T(8,128)(2,1)S(1)} %broadcast_select_fusion.2.more_0_), channel_id=1, source_target_pairs={{0,32},{1,33},{2,34},{3,35},{4,36},{5,37},{6,38},{7,39},{8,40},{9,... | collective-permute-start | bytes 294920 | tf_op jit(solution)/shard_map/ppermute | solution.py:311
  47.6 1.3 %collective-permute-start.11 = (bf16[384,128]{1,0:T(8,128)(2,1)S(1)}, bf16[384,128]{1,0:T(8,128)(2,1)S(1)}, u32[]{:S(2)}, u32[]{:S(2)}) collective-permute-start(bf16[384,128]{1,0:T(8,128)(2,1)S(1)} %collective-permute-done.10.more_6_), channel_id=1, source_target_pairs={{0,32},{1,33},{2,34},{3,35},{4,36},{5,37},{6,38},{7,39},{8,40},{9,... | collective-permute-start | bytes 294920 | tf_op jit(solution)/shard_map/ppermute | solution.py:311
  47.6 1.5 %collective-permute-start.8 = (bf16[384,128]{1,0:T(8,128)(2,1)S(1)}, bf16[384,128]{1,0:T(8,128)(2,1)S(1)}, u32[]{:S(2)}, u32[]{:S(2)}) collective-permute-start(bf16[384,128]{1,0:T(8,128)(2,1)S(1)} %collective-permute-done.3.more_2_), channel_id=1, source_target_pairs={{0,32},{1,33},{2,34},{3,35},{4,36},{5,37},{6,38},{7,39},{8,40},{9,... | collective-permute-start | bytes 294920 | tf_op jit(solution)/shard_map/ppermute | solution.py:311
  48.1 1.3 %collective-permute-start.9 = (bf16[384,128]{1,0:T(8,128)(2,1)S(1)}, bf16[384,128]{1,0:T(8,128)(2,1)S(1)}, u32[]{:S(2)}, u32[]{:S(2)}) collective-permute-start(bf16[384,128]{1,0:T(8,128)(2,1)S(1)} %collective-permute-done.4.more_4_), channel_id=1, source_target_pairs={{0,32},{1,33},{2,34},{3,35},{4,36},{5,37},{6,38},{7,39},{8,40},{9,... | collective-permute-start | bytes 294920 | tf_op jit(solution)/shard_map/ppermute | solution.py:311
  59.2 5.9 %collective-permute-start.12 = (bf16[384,128]{1,0:T(8,128)(2,1)S(1)}, bf16[384,128]{1,0:T(8,128)(2,1)S(1)}, u32[]{:S(2)}, u32[]{:S(2)}) collective-permute-start(bf16[384,128]{1,0:T(8,128)(2,1)S(1)} %get-tuple-element.43), channel_id=1, source_target_pairs={{32,64},{33,65},{34,66},{35,67},{36,68},{37,69},{38,70},{39,71},{4... | collective-permute-start | bytes 294920 | tf_op jit(solution)/shard_map/ppermute | solution.py:311
  61.1 4.0 %collective-permute-start.13 = (bf16[384,128]{1,0:T(8,128)(2,1)S(1)}, bf16[384,128]{1,0:T(8,128)(2,1)S(1)}, u32[]{:S(2)}, u32[]{:S(2)}) collective-permute-start(bf16[384,128]{1,0:T(8,128)(2,1)S(1)} %get-tuple-element.44), channel_id=1, source_target_pairs={{0,32},{1,33},{2,34},{3,35},{4,36},{5,37},{6,38},{7,39},{8,40},{9,... | collective-permute-start | bytes 294920 | tf_op jit(solution)/shard_map/ppermute | solution.py:311
  65.5 5.1 %collective-permute-start.15 = (bf16[384,512]{1,0:T(8,128)(2,1)S(1)}, bf16[384,512]{1,0:T(8,128)(2,1)S(1)}, u32[]{:S(2)}, u32[]{:S(2)}) collective-permute-start(bf16[384,512]{1,0:T(8,128)(2,1)S(1)} %fusion.1), channel_id=1, source_target_pairs={{0,32},{1,33},{2,34},{3,35},{4,36},{5,37},{6,38},{7,39},{8,40},{9,... | collective-permute-start | bytes 1179656 | tf_op jit(solution)/shard_map/ppermute | solution.py:311
  67.0 15.9 %all-to-all-start.1 = ((bf16[16,64,256]{2,1,0:T(8,128)(2,1)}), bf16[16,64,256]{2,1,0:T(8,128)(2,1)S(1)}, u32[]{:S(2)}, u32[]{:S(2)}) async-start(bf16[16,64,256]{2,1,0:T(8,128)(2,1)} %bitcast.18), calls=%async_computation.1 | async-start | bytes 1048576 | tf_op jit(solution)/shard_map/all_to_all | solution.py:410
  70.9 16.2 %collective-permute-start.16 = (bf16[384,128]{1,0:T(8,128)(2,1)S(1)}, bf16[384,128]{1,0:T(8,128)(2,1)S(1)}, u32[]{:S(2)}, u32[]{:S(2)}) collective-permute-start(bf16[384,128]{1,0:T(8,128)(2,1)S(1)} %get-tuple-element.59), channel_id=1, source_target_pairs={{0,64},{1,65},{2,66},{3,67},{4,68},{5,69},{6,70},{7,71},{8,72},{9,... | collective-permute-start | bytes 294920 | tf_op jit(solution)/shard_map/ppermute | solution.py:311
  71.7 15.5 %collective-permute-start.17 = (bf16[384,128]{1,0:T(8,128)(2,1)S(1)}, bf16[384,128]{1,0:T(8,128)(2,1)S(1)}, u32[]{:S(2)}, u32[]{:S(2)}) collective-permute-start(bf16[384,128]{1,0:T(8,128)(2,1)S(1)} %get-tuple-element.61), channel_id=1, source_target_pairs={{0,128},{1,129},{2,130},{3,131},{4,132},{5,133},{6,134},{7,135},{8... | collective-permute-start | bytes 294920 | tf_op jit(solution)/shard_map/ppermute | solution.py:311
  73.7 13.4 %collective-permute-start.18 = (bf16[384,128]{1,0:T(8,128)(2,1)S(1)}, bf16[384,128]{1,0:T(8,128)(2,1)S(1)}, u32[]{:S(2)}, u32[]{:S(2)}) collective-permute-start(bf16[384,128]{1,0:T(8,128)(2,1)S(1)} %get-tuple-element.60), channel_id=1, source_target_pairs={{0,192},{1,193},{2,194},{3,195},{4,196},{5,197},{6,198},{7,199},{8... | collective-permute-start | bytes 294920 | tf_op jit(solution)/shard_map/ppermute | solution.py:311
  83.0 7.9 %collective-permute-start.14 = (bf16[32,256]{1,0:T(8,128)(2,1)S(1)}, bf16[32,256]{1,0:T(8,128)(2,1)S(1)}, u32[]{:S(2)}, u32[]{:S(2)}) collective-permute-start(bf16[32,256]{1,0:T(8,128)(2,1)S(1)} %fusion.18), channel_id=1, source_target_pairs={{0,1},{1,0},{2,3},{3,2},{4,5},{5,4},{6,7},{7,6},{8,9},{9,8},{10,11... | collective-permute-start | bytes 49160 | tf_op jit(solution)/shard_map/ppermute | solution.py:311
  (3 other events, 2.3 us)
